TPU v7x, 32 devices: a whole 2x2x4 slice. The times are simulated.
32 devices in a mesh: dp: 8 (over z, y), fsdp: 4 (over x, core).
Axes of the slice: x: 2, y: 2, z: 4, core: 2. Of those that a mesh axis runs over, the one named last changes fastest.
Arguments:
- inputs: bfloat16 [32, 128, 768], P(('dp', 'fsdp')), may hold values from -6 to 6
- memory: bfloat16 [32, 512, 768], P(('dp', 'fsdp')), may hold values from -6 to 6
- out_cotangent: bfloat16 [32, 128, 768], P(('dp', 'fsdp')), may hold values from -6 to 6
- dec_lengths: int32 [32], P(('dp', 'fsdp')), may hold values from 32 to 128, as said below
- mem_lengths: int32 [32], P(('dp', 'fsdp')), may hold values from 128 to 512, as said below
- self_params: bfloat16 [2359296], P(('dp', 'fsdp'))
- cross_params: bfloat16 [2359296], P(('dp', 'fsdp'))
- ff_params: bfloat16 [4718592], P(('dp', 'fsdp'))
- gains: float32 [3, 768], replicated, may hold values from 0.1 to 1.9
- table: float32 [32, 12], replicated, may hold values from -4 to 4
Outputs:
- block_out: bfloat16 [32, 128, 768], P(('dp', 'fsdp'))
- input_grad: bfloat16 [32, 128, 768], P(('dp', 'fsdp'))
- memory_grad: bfloat16 [32, 512, 768], P(('dp', 'fsdp'))
- self_grad: float32 [2359296], P(('dp', 'fsdp'))
- cross_grad: float32 [2359296], P(('dp', 'fsdp'))
- ff_grad: float32 [4718592], P(('dp', 'fsdp'))
- gains_grad: float32 [3, 768], replicated
- table_grad: float32 [32, 12], replicated
Inputs may be any that keep to these rules, and one draw needn't show every extreme that they name: `dec_lengths`: positions of a decoder slot from its length on are padding; some slot has exactly 128 tokens and some exactly 32. `mem_lengths`: encoder positions of a slot from its length on are padding; some slot has exactly 512 and some exactly 128.
All inputs are finite; a program needn't handle non-finite values.
Results may differ from a plain program's by a relative error of at most 0.03.
The roundings to bfloat16 on the way count: a program that leaves them out, or rounds other values in their place, can miss the bound.
Values may be sent and summed in bfloat16 or wider, within the bound.
A program may use at most 192 MiB of HBM per device.

v0:
```python
import jax
import jax.numpy as jnp
import numpy as np
from jax import lax
from jax.sharding import PartitionSpec as P

D = 768
FF = 2048
H = 12
DH = 64
NB = 32
MAXD = 128


HIGHEST = lax.Precision.HIGHEST
MASKED = -1000000000.0


def product(left, right):
    return jnp.dot(left, right, preferred_element_type=jnp.float32)


def product_t(left, right):
    return lax.dot_general(
        left, right, (((0,), (0,)), ((), ())), preferred_element_type=jnp.float32
    )


def product_nt(left, right):
    return lax.dot_general(
        left, right, (((1,), (1,)), ((), ())), preferred_element_type=jnp.float32
    )


def rms_scale(value, gain):
    return value * lax.rsqrt(jnp.mean(value * value, axis=-1, keepdims=True) + 1e-06) * gain


def gelu_gate(gate_pre, up_pre):
    return jax.nn.gelu(gate_pre, approximate=True) * up_pre


def bucket_rows(start, count, length):
    half_count = NB // 2
    limits = np.ceil(
        half_count * (MAXD / half_count) ** (np.arange(1, half_count) / half_count)
    ).astype(np.int32)
    query_pos = start + jnp.arange(count, dtype=jnp.int32)
    key_pos = jnp.arange(length, dtype=jnp.int32)
    distance = query_pos[:, None] - key_pos[None, :]
    beyond = half_count + jnp.sum(
        (distance[None] >= jnp.asarray(limits)[:, None, None]).astype(jnp.int32), axis=0
    )
    return jnp.where(distance < half_count, jnp.maximum(distance, 0), beyond)


def onehot_block(start, count, length):
    bucket = bucket_rows(start, count, length)
    hot_rows = jnp.arange(NB, dtype=jnp.int32)[:, None, None] == bucket[None]
    return hot_rows.astype(jnp.float32).reshape(NB, count * length)


def position_bias(table, length):
    block_rows = min(length, 128)
    block_count = length // block_rows

    def position_per_block(block):
        bucket_hot = onehot_block(block * block_rows, block_rows, length)
        return lax.dot_general(
            table,
            bucket_hot,
            (((0,), (0,)), ((), ())),
            precision=HIGHEST,
            preferred_element_type=jnp.float32,
        )

    pieces = lax.map(position_per_block, jnp.arange(block_count, dtype=jnp.int32))
    return (
        pieces.reshape(block_count, H, block_rows, length)
        .transpose(1, 0, 2, 3)
        .reshape(H, length, length)
    )


def table_gradient(score_sums, length):
    block_rows = min(length, 128)

    def table_per_block(carry, block):
        ds_piece = score_sums.reshape(H, block_rows * length)
        bucket_hot = onehot_block(block * block_rows, block_rows, length)
        return (
            carry
            + lax.dot_general(
                bucket_hot,
                ds_piece,
                (((1,), (1,)), ((), ())),
                precision=HIGHEST,
                preferred_element_type=jnp.float32,
            ),
            None,
        )

    result, _ = lax.scan(
        table_per_block,
        jnp.zeros((NB, H), jnp.float32),
        jnp.arange(length // block_rows, dtype=jnp.int32),
    )
    return result


def score_block(queries, keys_in, score_bias, keep_mask):
    q_len = queries.shape[0]
    k_len = keys_in.shape[0]
    raw_scores = (
        jnp.einsum(
            "qhe,khe->hqk",
            queries.reshape(q_len, H, DH),
            keys_in.reshape(k_len, H, DH),
            preferred_element_type=jnp.float32,
        )
        + score_bias
    )
    return jnp.where(keep_mask[None], raw_scores, MASKED)


def attend_forward(queries, keys_in, values, score_bias, keep_mask):
    q_len = queries.shape[0]
    k_len = keys_in.shape[0]
    raw_scores = score_block(queries, keys_in, score_bias, keep_mask)
    row_max = jnp.max(raw_scores, axis=2, keepdims=True)
    exponent = jnp.exp(raw_scores - row_max)
    row_sum = jnp.sum(exponent, axis=2, keepdims=True)
    softmax_low = (exponent / row_sum).astype(jnp.bfloat16)
    head_mix = jnp.einsum(
        "hqk,khe->qhe",
        softmax_low,
        values.reshape(k_len, H, DH),
        preferred_element_type=jnp.float32,
    )
    return (head_mix.reshape(q_len, H * DH).astype(jnp.bfloat16), row_max, row_sum)


def attend_backward(queries, keys_in, values, score_bias, keep_mask, row_max, row_sum, d_mix):
    q_len = queries.shape[0]
    k_len = keys_in.shape[0]
    raw_scores = score_block(queries, keys_in, score_bias, keep_mask)
    softmax_out = jnp.exp(raw_scores - row_max) / row_sum
    softmax_low = softmax_out.astype(jnp.bfloat16)
    mix_heads = d_mix.reshape(q_len, H, DH)
    q_heads = queries.reshape(q_len, H, DH)
    k_heads = keys_in.reshape(k_len, H, DH)
    v_heads = values.reshape(k_len, H, DH)
    d_softmax = jnp.einsum("qhe,khe->hqk", mix_heads, v_heads, preferred_element_type=jnp.float32)
    d_scores = (
        softmax_out * (d_softmax - jnp.sum(softmax_out * d_softmax, axis=2, keepdims=True))
    ).astype(jnp.bfloat16)
    d_values = (
        jnp.einsum("hqk,qhe->khe", softmax_low, mix_heads, preferred_element_type=jnp.float32)
        .reshape(k_len, H * DH)
        .astype(jnp.bfloat16)
    )
    d_queries = (
        jnp.einsum("hqk,khe->qhe", d_scores, k_heads, preferred_element_type=jnp.float32)
        .reshape(q_len, H * DH)
        .astype(jnp.bfloat16)
    )
    d_keys = (
        jnp.einsum("hqk,qhe->khe", d_scores, q_heads, preferred_element_type=jnp.float32)
        .reshape(k_len, H * DH)
        .astype(jnp.bfloat16)
    )
    return (d_queries, d_keys, d_values, d_scores)


def attend_slots(queries, keys_in, values, lengths, score_bias, base_mask):
    slot_count = lengths.shape[0]
    q_len = queries.shape[0] // slot_count
    k_len = keys_in.shape[0] // slot_count
    key_pos = jnp.arange(k_len, dtype=jnp.int32)

    def per_slot(slot_item):
        q_slot, k_slot, v_slot, slot_len = slot_item
        keep_mask = base_mask & (key_pos[None, :] < slot_len)
        return attend_forward(q_slot, k_slot, v_slot, score_bias, keep_mask)

    head_mix, row_max, row_sum = lax.map(
        per_slot,
        (
            queries.reshape(slot_count, q_len, -1),
            keys_in.reshape(slot_count, k_len, -1),
            values.reshape(slot_count, k_len, -1),
            lengths,
        ),
    )
    return (head_mix.reshape(slot_count * q_len, -1), row_max, row_sum)


def attend_back_slots(
    queries, keys_in, values, lengths, score_bias, base_mask, row_max, row_sum, d_mix, with_table
):
    slot_count = lengths.shape[0]
    q_len = queries.shape[0] // slot_count
    k_len = keys_in.shape[0] // slot_count
    key_pos = jnp.arange(k_len, dtype=jnp.int32)
    if with_table:
        start = jnp.zeros((H, q_len, k_len), jnp.float32)
    else:
        start = jnp.zeros((), jnp.float32)

    def per_slot(carry, slot_item):
        q_slot, k_slot, v_slot, slot_len, max_slot, sum_slot, dmix_slot = slot_item
        keep_mask = base_mask & (key_pos[None, :] < slot_len)
        d_queries, d_keys, d_values, d_scores = attend_backward(
            q_slot, k_slot, v_slot, score_bias, keep_mask, max_slot, sum_slot, dmix_slot
        )
        if with_table:
            carry = carry + d_scores.astype(jnp.float32)
        return (carry, (d_queries, d_keys, d_values))

    score_sums, grad_parts = lax.scan(
        per_slot,
        start,
        (
            queries.reshape(slot_count, q_len, -1),
            keys_in.reshape(slot_count, k_len, -1),
            values.reshape(slot_count, k_len, -1),
            lengths,
            row_max,
            row_sum,
            d_mix.reshape(slot_count, q_len, -1),
        ),
    )
    return (
        grad_parts[0].reshape(slot_count * q_len, -1),
        grad_parts[1].reshape(slot_count * k_len, -1),
        grad_parts[2].reshape(slot_count * k_len, -1),
        score_sums,
    )


def gather_weights(self_params, cross_params, ff_params):
    return (
        lax.all_gather(self_params, ("dp", "fsdp"), axis=0, tiled=True),
        lax.all_gather(cross_params, ("dp", "fsdp"), axis=0, tiled=True),
        lax.all_gather(ff_params, ("dp", "fsdp"), axis=0, tiled=True),
    )


def scatter_grads(self_full, cross_full, ff_full):
    wide_count = lax.axis_size("dp")
    spread = (
        lax.all_to_all(
            self_full.reshape(wide_count, -1).astype(jnp.bfloat16),
            "dp",
            split_axis=0,
            concat_axis=0,
            tiled=True,
        ).astype(jnp.float32),
        lax.all_to_all(
            cross_full.reshape(wide_count, -1).astype(jnp.bfloat16),
            "dp",
            split_axis=0,
            concat_axis=0,
            tiled=True,
        ).astype(jnp.float32),
        lax.all_to_all(
            ff_full.reshape(wide_count, -1).astype(jnp.bfloat16),
            "dp",
            split_axis=0,
            concat_axis=0,
            tiled=True,
        ).astype(jnp.float32),
    )
    self_block = jnp.sum(spread[0], axis=0)
    cross_block = jnp.sum(spread[1], axis=0)
    ff_block = jnp.sum(spread[2], axis=0)
    return (
        lax.psum_scatter(
            self_block.astype(jnp.bfloat16), "fsdp", scatter_dimension=0, tiled=True
        ).astype(jnp.float32),
        lax.psum_scatter(
            cross_block.astype(jnp.bfloat16), "fsdp", scatter_dimension=0, tiled=True
        ).astype(jnp.float32),
        lax.psum_scatter(
            ff_block.astype(jnp.bfloat16), "fsdp", scatter_dimension=0, tiled=True
        ).astype(jnp.float32),
    )


def unpack(weights):
    self_flat, cross_flat, ff_flat = weights
    self_mats = self_flat.reshape(4, D, D)
    cross_mats = cross_flat.reshape(4, D, D)
    block_size = D * FF
    return (
        self_mats[0],
        self_mats[1],
        self_mats[2],
        self_mats[3],
        cross_mats[0],
        cross_mats[1],
        cross_mats[2],
        cross_mats[3],
        ff_flat[:block_size].reshape(D, FF),
        ff_flat[block_size : 2 * block_size].reshape(D, FF),
        ff_flat[2 * block_size :].reshape(FF, D),
    )


def run_forward(
    weights, flat_in, flat_mem, gains, pos_bias, causal, open_mask, dec_lengths, mem_lengths
):
    w_sq, w_sk, w_sv, w_so, w_cq, w_ck, w_cv, w_co, w_gate, w_up, w_down = unpack(weights)
    norm_one = rms_scale(flat_in, gains[0]).astype(jnp.bfloat16)
    self_q = product(norm_one, w_sq).astype(jnp.bfloat16)
    self_k = product(norm_one, w_sk).astype(jnp.bfloat16)
    self_v = product(norm_one, w_sv).astype(jnp.bfloat16)
    self_mix, self_max, self_sum = attend_slots(
        self_q, self_k, self_v, dec_lengths, pos_bias, causal
    )
    resid_one = flat_in + product(self_mix, w_so)
    norm_two = rms_scale(resid_one, gains[1]).astype(jnp.bfloat16)
    cross_q = product(norm_two, w_cq).astype(jnp.bfloat16)
    cross_k = product(flat_mem, w_ck).astype(jnp.bfloat16)
    cross_v = product(flat_mem, w_cv).astype(jnp.bfloat16)
    cross_mix, cross_max, cross_sum = attend_slots(
        cross_q, cross_k, cross_v, mem_lengths, 0.0, open_mask
    )
    resid_two = resid_one + product(cross_mix, w_co)
    norm_three = rms_scale(resid_two, gains[2]).astype(jnp.bfloat16)
    gate_pre = product(norm_three, w_gate)
    up_pre = product(norm_three, w_up)
    hidden = gelu_gate(gate_pre, up_pre).astype(jnp.bfloat16)
    block = resid_two + product(hidden, w_down)
    return (
        norm_one,
        self_q,
        self_k,
        self_v,
        self_mix,
        self_max,
        self_sum,
        resid_one,
        norm_two,
        cross_q,
        cross_k,
        cross_v,
        cross_mix,
        cross_max,
        cross_sum,
        resid_two,
        norm_three,
        gate_pre,
        up_pre,
        hidden,
        block,
    )


def local(
    inputs,
    memory,
    out_cotangent,
    dec_lengths,
    mem_lengths,
    self_params,
    cross_params,
    ff_params,
    gains,
    table,
):
    slot_count, length, model_width = inputs.shape
    mem_len = memory.shape[1]
    row_count = slot_count * length
    pos_bias = position_bias(table, length)
    positions = jnp.arange(length, dtype=jnp.int32)
    causal = positions[None, :] <= positions[:, None]
    open_mask = jnp.ones((length, mem_len), dtype=bool)
    flat_in = inputs.reshape(row_count, model_width).astype(jnp.float32)
    flat_mem = memory.reshape(slot_count * mem_len, model_width)
    weights = gather_weights(self_params, cross_params, ff_params)
    first_pass = run_forward(
        weights, flat_in, flat_mem, gains, pos_bias, causal, open_mask, dec_lengths, mem_lengths
    )
    block_out = first_pass[20].astype(jnp.bfloat16).reshape(slot_count, length, model_width)
    again = gather_weights(self_params, cross_params, ff_params)
    w_sq, w_sk, w_sv, w_so, w_cq, w_ck, w_cv, w_co, w_gate, w_up, w_down = unpack(again)
    (
        norm_one,
        self_q,
        self_k,
        self_v,
        self_mix,
        self_max,
        self_sum,
        resid_one,
        norm_two,
        cross_q,
        cross_k,
        cross_v,
        cross_mix,
        cross_max,
        cross_sum,
        resid_two,
        norm_three,
        gate_pre,
        up_pre,
        hidden,
        _,
    ) = run_forward(
        again, flat_in, flat_mem, gains, pos_bias, causal, open_mask, dec_lengths, mem_lengths
    )
    d_out = out_cotangent.reshape(row_count, model_width)
    grad_down = product_t(hidden, d_out)
    d_hidden = product_nt(d_out, w_down).astype(jnp.bfloat16)
    _, pull_gate = jax.vjp(gelu_gate, gate_pre, up_pre)
    d_gate, d_up = pull_gate(d_hidden.astype(jnp.float32))
    d_gate = d_gate.astype(jnp.bfloat16)
    d_up = d_up.astype(jnp.bfloat16)
    grad_gate = product_t(norm_three, d_gate)
    grad_up = product_t(norm_three, d_up)
    d_norm_three = product_nt(d_gate, w_gate) + product_nt(d_up, w_up)
    _, pull_three = jax.vjp(rms_scale, resid_two, gains[2])
    d_from_three, grad_gain_three = pull_three(d_norm_three)
    d_resid_two = d_out.astype(jnp.float32) + d_from_three
    d_cross = d_resid_two.astype(jnp.bfloat16)
    grad_co = product_t(cross_mix, d_cross)
    d_cross_mix = product_nt(d_cross, w_co).astype(jnp.bfloat16)
    dq_cross, dk_cross, dv_cross, _ = attend_back_slots(
        cross_q,
        cross_k,
        cross_v,
        mem_lengths,
        0.0,
        open_mask,
        cross_max,
        cross_sum,
        d_cross_mix,
        False,
    )
    grad_cq = product_t(norm_two, dq_cross)
    grad_ck = product_t(flat_mem, dk_cross)
    grad_cv = product_t(flat_mem, dv_cross)
    memory_grad = (product_nt(dk_cross, w_ck) + product_nt(dv_cross, w_cv)).astype(jnp.bfloat16)
    _, pull_two = jax.vjp(rms_scale, resid_one, gains[1])
    d_from_two, grad_gain_two = pull_two(product_nt(dq_cross, w_cq))
    d_resid_one = d_resid_two + d_from_two
    d_self = d_resid_one.astype(jnp.bfloat16)
    grad_so = product_t(self_mix, d_self)
    d_self_mix = product_nt(d_self, w_so).astype(jnp.bfloat16)
    dq_self, dk_self, dv_self, score_sums = attend_back_slots(
        self_q, self_k, self_v, dec_lengths, pos_bias, causal, self_max, self_sum, d_self_mix, True
    )
    grad_sq = product_t(norm_one, dq_self)
    grad_sk = product_t(norm_one, dk_self)
    grad_sv = product_t(norm_one, dv_self)
    d_norm_one = product_nt(dq_self, w_sq) + product_nt(dk_self, w_sk) + product_nt(dv_self, w_sv)
    _, pull_one = jax.vjp(rms_scale, flat_in, gains[0])
    d_from_one, grad_gain_one = pull_one(d_norm_one)
    input_grad = (d_resid_one + d_from_one).astype(jnp.bfloat16)
    table_local = table_gradient(score_sums, length)
    self_full = jnp.stack([grad_sq, grad_sk, grad_sv, grad_so]).reshape(-1)
    cross_full = jnp.stack([grad_cq, grad_ck, grad_cv, grad_co]).reshape(-1)
    ff_full = jnp.concatenate([grad_gate.reshape(-1), grad_up.reshape(-1), grad_down.reshape(-1)])
    self_shard, cross_shard, ff_shard = scatter_grads(self_full, cross_full, ff_full)
    gain_local = jnp.stack([grad_gain_one, grad_gain_two, grad_gain_three])
    gain_total, table_total = lax.psum((gain_local, table_local), ("dp", "fsdp"))
    return (
        block_out,
        input_grad.reshape(slot_count, length, model_width),
        memory_grad.reshape(slot_count, mem_len, model_width),
        self_shard,
        cross_shard,
        ff_shard,
        gain_total,
        table_total,
    )


def solution(mesh):
    placed = (
        P(("dp", "fsdp"), None, None),
        P(("dp", "fsdp"), None, None),
        P(("dp", "fsdp"), None, None),
        P(("dp", "fsdp")),
        P(("dp", "fsdp")),
        P(("dp", "fsdp")),
        P(("dp", "fsdp")),
        P(("dp", "fsdp")),
        P(),
        P(),
    )
    return jax.shard_map(
        local,
        mesh=mesh,
        in_specs=placed,
        out_specs=(
            P(("dp", "fsdp"), None, None),
            P(("dp", "fsdp"), None, None),
            P(("dp", "fsdp"), None, None),
            P(("dp", "fsdp")),
            P(("dp", "fsdp")),
            P(("dp", "fsdp")),
            P(),
            P(),
        ),
        check_vma=False,
    )
```

profile of v0, /device:TPU:0, one launch (start us, length us, event | category | flops | bytes accessed | tf_op | source)
XLA Modules:
  0.0 944.5 jit_solution(2415599310014176707)
XLA Ops:
  18.2 59.1 %all-gather.4.cloned.1.call-done = bf16[2359296]{0:T(1024)(128)(2,1)} async-done(((bf16[73728]{0:T(1024)(128)(2,1)}), bf16[2359296]{0:T(1024)(128)(2,1)}) %all-gather.4.cloned.1.call-update) | async-done | bytes 4718608 | tf_op jit(solution)/shard_map/all_gather | solution.py:243
  77.3 4.1 fusion.84
  83.4 59.2 %all-gather.6.cloned.1.call-done = bf16[2359296]{0:T(1024)(128)(2,1)} async-done(((bf16[73728]{0:T(1024)(128)(2,1)}), bf16[2359296]{0:T(1024)(128)(2,1)}) %all-gather.6.cloned.1.call-update) | async-done | bytes 4718608 | tf_op jit(solution)/shard_map/all_gather | solution.py:244
  142.7 4.2 fusion.83
  146.9 3.3 slice.204
  150.2 3.4 slice.202
  153.6 3.0 convolution_convert_fusion.12
  158.8 3.3 slice.200
  168.9 2.6 slice.191
  174.3 2.6 slice.189
  185.2 4.0 fusion.86
  189.2 3.0 convolution_convert_fusion.22
  193.0 33.5 %all-gather.8.cloned.1.call-done = bf16[4718592]{0:T(1024)(128)(2,1)} async-done(((bf16[147456]{0:T(1024)(128)(2,1)}), bf16[4718592]{0:T(1024)(128)(2,1)}) %all-gather.8.cloned.1.call-update) | async-done | bytes 9437200 | tf_op jit(solution)/shard_map/all_gather | solution.py:245
  226.5 6.8 fusion.82
  233.2 6.6 slice.211
  239.9 5.8 slice.209
  245.6 5.8 slice.207
  251.4 2.6 fusion.88
  264.3 3.0 multiply_reduce_fusion
  274.8 2.5 convolution_convert_fusion.16
  282.2 2.5 pad_maximum_fusion.1
  284.7 8.6 convert_element_type.341
  293.8 30.1 %reduce.12 = bf16[8,294912]{1,0:T(8,128)(2,1)} reduce(bf16[8,1,294912]{2,1,0:T(2,128)(2,1)} %convert_element_type.341, bf16[]{:T(256)} %broadcast.308), dimensions={1}, to_apply=%convert_element_type.341.reduce_sub_computation | reduce | bytes 9437186 | tf_op jit(solution)/shard_map/convert_element_type | solution.py:253
  323.9 9.0 reshape.619
  332.9 4.9 all-to-all-start
  337.8 3.7 convolution_convert_fusion
  341.5 6.4 reshape.607
  350.0 2.7 copy.105
  353.7 2.7 copy.104
  364.5 8.2 convert_element_type.342
  372.6 30.4 %reduce.13 = bf16[8,294912]{1,0:T(8,128)(2,1)} reduce(bf16[8,1,294912]{2,1,0:T(2,128)(2,1)} %convert_element_type.342, bf16[]{:T(256)} %broadcast.308), dimensions={1}, to_apply=%convert_element_type.342.reduce_sub_computation | reduce | bytes 9437186 | tf_op jit(solution)/shard_map/convert_element_type | solution.py:260
  403.0 8.9 reshape.621
  411.9 31.0 %all-to-all-done = bf16[8,2,147456]{2,1,0:T(2,128)(2,1)} async-done(((bf16[8,2,147456]{2,1,0:T(2,128)(2,1)}), bf16[8,2,147456]{2,1,0:T(2,128)(2,1)}, u32[]{:S(2)}, u32[]{:S(2)}) %all-to-all-start) | async-done | bytes 4718624 | tf_op jit(solution)/shard_map/all_to_all | solution.py:252
  442.9 4.6 all-to-all-start.1
  447.5 13.0 %pad_maximum_fusion = bf16[4718592]{0:T(1024)(128)(2,1)} fusion(bf16[1572864]{0:T(1024)(128)(2,1)} %reshape.607, bf16[1572864]{0:T(1024)(128)(2,1)} %bitcast.209, bf16[1572864]{0:T(1024)(128)(2,1)} %bitcast.210), kind=kLoop, calls=%fused_computation.2 | loop fusion | flops 28311552 | bytes 18874368 | tf_op jit(solution)/shard_map/concatenate | solution.py:464
  460.6 12.1 %convert_element_type.343 = bf16[8,1,589824]{2,1,0:T(2,128)(2,1)} reshape(bf16[4718592]{0:T(1024)(128)(2,1)} %pad_maximum_fusion) | data formatting | bytes 18874368 | tf_op jit(solution)/shard_map/convert_element_type | solution.py:267
  472.7 59.4 %reduce.14 = bf16[8,589824]{1,0:T(8,128)(2,1)} reduce(bf16[8,1,589824]{2,1,0:T(2,128)(2,1)} %convert_element_type.343, bf16[]{:T(256)} %broadcast.308), dimensions={1}, to_apply=%convert_element_type.343.reduce_sub_computation | reduce | bytes 18874370 | tf_op jit(solution)/shard_map/convert_element_type | solution.py:267
  532.1 25.2 %reshape.623 = bf16[8,2,294912]{2,1,0:T(2,128)(2,1)} reshape(bf16[8,589824]{1,0:T(8,128)(2,1)} %reduce.14) | data formatting | bytes 18874368
  557.3 6.0 all-to-all-start.2
  570.1 218.6 %all-reduce.3 = (f32[3,768]{1,0:T(4,128)}, f32[32,12]{0,1:T(8,128)}) all-reduce(f32[3,768]{1,0:T(4,128)S(1)} %pad_maximum_fusion.3, f32[32,12]{0,1:T(8,128)S(1)} %fusion.26), channel_id=1, replica_groups=mesh['dp'=8,'fsdp'=4] {'dp','fsdp'}, use_global_device_ids=true, to_apply=%region_22.23 | all-reduce | flops 2688 | bytes 21504 | tf_op jit(solution)/shard_map/psum | solution.py:467
  788.7 9.3 reshape.620
  798.0 14.4 %reduce_sum.213 = bf16[294912]{0:T(1024)(128)(2,1)} reduce(bf16[8,1,294912]{2,1,0:T(2,128)(2,1)} %reshape.620, bf16[]{:T(256)} %constant.170.clone.1), dimensions={0,1}, to_apply=%region_13.14 | reduce | flops 2064384 | bytes 5308418 | tf_op jit(solution)/shard_map/reduce_sum | solution.py:274
  812.4 9.3 reshape.622
  821.6 14.4 %reduce_sum.217 = bf16[294912]{0:T(1024)(128)(2,1)} reduce(bf16[8,1,294912]{2,1,0:T(2,128)(2,1)} %reshape.622, bf16[]{:T(256)} %constant.170.clone.1), dimensions={0,1}, to_apply=%region_15.16 | reduce | flops 2064384 | bytes 5308418 | tf_op jit(solution)/shard_map/reduce_sum | solution.py:275
  836.0 14.5 %reshape.624 = bf16[8,1,589824]{2,1,0:T(2,128)(2,1)} reshape(bf16[8,2,294912]{2,1,0:T(2,128)(2,1)} %all-to-all-done.2) | data formatting | bytes 18874368
  850.5 27.1 %reduce_sum.218 = bf16[589824]{0:T(1024)(128)(2,1)} reduce(bf16[8,1,589824]{2,1,0:T(2,128)(2,1)} %reshape.624, bf16[]{:T(256)} %constant.170.clone.1), dimensions={0,1}, to_apply=%region_17.18 | reduce | flops 4128768 | bytes 10616834 | tf_op jit(solution)/shard_map/reduce_sum | solution.py:276
  879.5 3.3 fusion.25
  886.2 47.9 %all-reduce.7.cloned.1.call-done = (bf16[294912]{0:T(1024)(128)(2,1)}, bf16[294912]{0:T(1024)(128)(2,1)}, bf16[589824]{0:T(1024)(128)(2,1)}) async-done(((bf16[294912]{0:T(1024)(128)(2,1)}, bf16[294912]{0:T(1024)(128)(2,1)}, bf16[589824]{0:T(1024)(128)(2,1)}), (bf16[294912]{0:T(1024)(128)(2,1)}, bf16[294912]{0:T(1024)(128)(2,1)}, bf16[589824]{0:T(1024)(128)(2,1)})) %all-reduce.7.cloned.1.call-update) | async-done | bytes 2359312
  (264 shorter events, 80.4 us)
Async XLA Ops:
  7.2 146.4 %copy-start = (bf16[1,512,768]{2,1,0:T(8,128)(2,1)S(1)}, bf16[1,512,768]{2,1,0:T(8,128)(2,1)}, u32[]{:S(2)}) copy-start(bf16[1,512,768]{2,1,0:T(8,128)(2,1)} %param.13) | copy-start | bytes 2359300
  7.2 70.1 %all-gather.4.cloned.1.call-start = ((), (), s32[]{:S(2)}) async-start(), calls=%async_computation.3 | async-start | bytes 4866048 | tf_op jit(solution)/shard_map/all_gather | solution.py:243
  7.9 134.8 %all-gather.6.cloned.1.call-start = ((), (), s32[]{:S(2)}) async-start(), calls=%async_computation.4 | async-start | bytes 4866048 | tf_op jit(solution)/shard_map/all_gather | solution.py:244
  8.7 217.8 %all-gather.8.cloned.1.call-start = ((), (), s32[]{:S(2)}) async-start(), calls=%async_computation.5 | async-start | bytes 9732096 | tf_op jit(solution)/shard_map/all_gather | solution.py:245
  12.3 164.6 %copy-start.63 = (f32[128]{0:T(128)}, f32[128]{0:T(128)S(1)}, u32[]{:S(2)}) copy-start(f32[128]{0:T(128)S(1)} %fusion.71) | copy-start | bytes 1540
  168.3 4.3 copy-start.6
  168.9 10.9 %copy-start.37 = (bf16[128,768]{0,1:T(8,128)(2,1)}, bf16[128,768]{0,1:T(8,128)(2,1)S(1)}, u32[]{:S(2)}) copy-start(bf16[128,768]{0,1:T(8,128)(2,1)S(1)} %copy.80) | copy-start | bytes 589828
  171.5 6.5 copy-start.10
  176.9 5.5 copy-start.8
  182.7 6.5 copy-start.46
  184.6 4.6 copy-start.77
  184.6 84.6 %copy-start.71 = (f32[128]{0:T(128)}, f32[128]{0:T(128)S(1)}, u32[]{:S(2)}) copy-start(f32[128]{0:T(128)S(1)} %fusion.72) | copy-start | bytes 1540
  185.2 4.0 copy-start.48
  189.2 3.0 copy-start.68
  189.2 3.0 copy-start.12
  192.7 40.5 %copy-start.79 = (f32[128]{0:T(128)}, f32[128]{0:T(128)S(1)}, u32[]{:S(2)}) copy-start(f32[128]{0:T(128)S(1)} %get-tuple-element.219) | copy-start | bytes 1540
  192.7 69.9 %copy-start.15 = (f32[128,768]{1,0:T(8,128)}, f32[128,768]{1,0:T(8,128)S(1)}, u32[]{:S(2)}) copy-start(f32[128,768]{1,0:T(8,128)S(1)} %get-tuple-element.220) | copy-start | bytes 1179652
  192.7 40.5 %copy-start.73 = (f32[128]{0:T(128)}, f32[128]{0:T(128)S(1)}, u32[]{:S(2)}) copy-start(f32[128]{0:T(128)S(1)} %fusion.73) | copy-start | bytes 1540
  251.4 2.8 copy-start.3
  258.5 4.1 copy-start.30
  258.5 4.1 copy-start.32
  264.2 3.0 copy-start.58
  264.2 3.2 copy-start.27
  264.2 3.2 copy-start.69
  271.0 3.8 copy-start.62
  271.8 8.1 copy-start.17
  332.9 4.9 copy-start.55
  332.9 110.0 %all-to-all-start = ((bf16[8,2,147456]{2,1,0:T(2,128)(2,1)}), bf16[8,2,147456]{2,1,0:T(2,128)(2,1)}, u32[]{:S(2)}, u32[]{:S(2)}) async-start(bf16[8,2,147456]{2,1,0:T(2,128)(2,1)} %reshape.619), calls=%async_computation | async-start | bytes 9437184 | tf_op jit(solution)/shard_map/all_to_all | solution.py:252
  353.6 2.8 copy-start.21
  353.6 3.2 copy-start.41
  353.7 3.2 copy-start.72
  442.9 114.4 %all-to-all-start.1 = ((bf16[8,2,147456]{2,1,0:T(2,128)(2,1)}), bf16[8,2,147456]{2,1,0:T(2,128)(2,1)}, u32[]{:S(2)}, u32[]{:S(2)}) async-start(bf16[8,2,147456]{2,1,0:T(2,128)(2,1)} %reshape.621), calls=%async_computation.1 | async-start | bytes 9437184 | tf_op jit(solution)/shard_map/all_to_all | solution.py:259
  557.3 6.1 copy-start.83
  557.3 8.0 copy-start.23
  557.3 9.3 copy-start.67
  557.3 9.3 copy-start.66
  557.3 9.3 copy-start.36
  557.3 278.7 %all-to-all-start.2 = ((bf16[8,2,294912]{2,1,0:T(2,128)(2,1)}), bf16[8,2,294912]{2,1,0:T(2,128)(2,1)}, u32[]{:S(2)}, u32[]{:S(2)}) async-start(bf16[8,2,294912]{2,1,0:T(2,128)(2,1)} %reshape.623), calls=%async_computation.2 | async-start | bytes 18874368 | tf_op jit(solution)/shard_map/all_to_all | solution.py:266
  563.4 5.0 copy-start.7
  563.4 5.0 copy-start.34
  563.4 370.7 %all-reduce.7.cloned.1.call-start = ((), (), s32[]{:S(2)}) async-start(), calls=%async_computation.6 | async-start | bytes 4718592
  565.3 3.6 copy-start.9
  565.4 3.6 copy-start.53
  565.4 3.6 copy-start.65
  568.4 220.3 %copy-start.76 = (f32[128]{0:T(128)S(1)}, f32[128]{0:T(128)}, u32[]{:S(2)}) copy-start(f32[128]{0:T(128)} %copy-done.75) | copy-start | bytes 1540
  879.5 3.3 copy-start.42
  879.5 3.3 copy-start.51
  882.8 54.9 %copy-start.1 = (bf16[1,512,768]{2,1,0:T(8,128)(2,1)S(1)}, bf16[1,512,768]{2,1,0:T(8,128)(2,1)}, u32[]{:S(2)}) copy-start(bf16[1,512,768]{2,1,0:T(8,128)(2,1)} %param.13) | copy-start | bytes 2359300
  (44 other events, 77.6 us)
Sparse Core Ops, SparseCore 0:
  10.9 66.3 all-gather.3
  80.2 62.4 all-gather.5
  145.6 80.8 all-gather.7
  877.8 56.2 all-reduce.6
where the time goes:
time: 950 us; the launch traced here: 944 us
  waiting for transfers between devices  233 us (25%)
  blocking collectives  219 us (23%)
  other arithmetic  205 us (22%)
  local copies, waits for them, and re-layouts  193 us (20%)
  matrix products  61.9 us (7%)
  between operations  17.7 us (2%)
  starting transfers between devices  15.7 us (2%)
    psum x1, blocking collectives, local(): lax.psum((gain_local, table_local), ('dp', 'fsdp'))  219 us
    unnamed x180, local copies, waits for them, and re-layouts  91.2 us
    convert_element_type x1, other arithmetic, scatter_grads(): ff_full.reshape(wide_count, -1).astype(jnp.bfloat16)  59.4 us
    all_gather x1, waiting for transfers between devices, gather_weights(): lax.all_gather(cross_params, ('dp', 'fsdp'), axis=0, tiled=True)  59.2 us
    all_gather x1, waiting for transfers between devices, gather_weights(): lax.all_gather(self_params, ('dp', 'fsdp'), axis=0, tiled=True)  59.1 us
    unnamed x5, waiting for transfers between devices  49.9 us
    all_gather x1, waiting for transfers between devices, gather_weights(): lax.all_gather(ff_params, ('dp', 'fsdp'), axis=0, tiled=True)  33.5 us
    all_to_all x1, waiting for transfers between devices, scatter_grads(): lax.all_to_all(self_full.reshape(wide_count, -1).astype(jnp.bfloat16), 'd...  31 us
  transfers between devices with their start and end apart: 7, of which 5 were waited for; matrix products, arithmetic and copies ran while one was open for 32% of the time, Pallas kernels for 0%

commit v1 on v0

--- a/solution.py
+++ b/solution.py
@@ -1,7 +1,11 @@
+import functools
+
 import jax
 import jax.numpy as jnp
 import numpy as np
 from jax import lax
+from jax.experimental import pallas as pl
+from jax.experimental.pallas import tpu as pltpu
 from jax.sharding import PartitionSpec as P
 
 D = 768
@@ -10,10 +14,1019 @@
 DH = 64
 NB = 32
 MAXD = 128
+PAIRS = H // 2
+MASKED = -1000000000.0
+BF = jnp.bfloat16
+F32 = jnp.float32
+MESH = pl.DeviceIdType.MESH
+
+AR = 96
+AU = 288
+FU = 576
+GROUPS = (
+    (2, 3), (2, 2), (2, 0), (2, 1),
+    (1, 3), (1, 2), (1, 1), (1, 0),
+    (0, 3), (0, 2), (0, 1), (0, 0),
+)
+UNIT = tuple(FU if t == 2 else AU for t, _ in GROUPS)
+OWN = tuple(4 * sum(UNIT[:g]) for g in range(12))
+OWN_ROWS = 4 * sum(UNIT)
+LAND = tuple(3 * sum(UNIT[:g]) for g in range(12))
+LAND_ROWS = 3 * sum(UNIT)
+ZBASE = (0, 3 * AU, 6 * AU)
+Z_ROWS = 6 * AU + 3 * FU
+STAGE = 4 * FU
+
+
+def limits():
+    half = NB // 2
+    return [
+        int(v)
+        for v in np.ceil(half * (MAXD / half) ** (np.arange(1, half) / half)).astype(np.int32)
+    ]
+
+
+def bucket_of(distance):
+    half = NB // 2
+    beyond = jnp.full(distance.shape, half, jnp.int32)
+    for limit in limits():
+        beyond = beyond + jnp.where(distance >= limit, 1, 0)
+    return jnp.where(distance < half, jnp.maximum(distance, 0), beyond)
+
+
+def nn(left, right):
+    return jnp.dot(left, right, preferred_element_type=F32)
+
+
+def nt(left, right):
+    return lax.dot_general(left, right, (((1,), (1,)), ((), ())), preferred_element_type=F32)
+
+
+def tn(left, right):
+    return lax.dot_general(left, right, (((0,), (0,)), ((), ())), preferred_element_type=F32)
+
+
+def al(value, step):
+    return pl.multiple_of(value, step)
+
+
+def rms(value, gain):
+    r = lax.rsqrt(jnp.mean(value * value, axis=-1, keepdims=True) + 1e-06)
+    return value * r * gain
+
+
+def rms_back(value, gain, dz):
+    r = lax.rsqrt(jnp.mean(value * value, axis=-1, keepdims=True) + 1e-06)
+    inner = jnp.mean(value * gain * dz, axis=-1, keepdims=True)
+    dv = r * gain * dz - value * (r * r * r) * inner
+    dg = jnp.sum(value * r * dz, axis=0, keepdims=True)
+    return dv, dg
+
+
+class Layer:
+    def __init__(self, refs):
+        self.__dict__.update(refs)
+        self.flat, self.dm = self.ps, self.n3
+        dp = lax.axis_index("dp")
+        fs = lax.axis_index("fsdp")
+        self.z, self.y = dp // 2, dp % 2
+        self.x, self.c = fs // 2, fs % 2
+        self.shard = dp * 4 + fs
+
+    def dev(self, z=None, fx=0, fy=0, fc=0):
+        z = self.z if z is None else z
+        y = (self.y + fy) % 2
+        x = (self.x + fx) % 2
+        c = (self.c + fc) % 2
+        return (z * 2 + y, x * 2 + c)
+
+    def chip(self, fx=0, fy=0):
+        return ((self.y + fy) % 2) * 2 + (self.x + fx) % 2
+
+    def shard_at(self, z, fx=0, fy=0, fc=0):
+        return z * 8 + self.chip(fx, fy) * 2 + (self.c + fc) % 2
+
+    def copy(self, src, dst, send, recv, device):
+        return pltpu.make_async_remote_copy(
+            src_ref=src, dst_ref=dst, send_sem=send, recv_sem=recv,
+            device_id=device, device_id_type=MESH,
+        )
+
+    def piece(self, tensor, shard, half=None):
+        rows = FU if tensor == 2 else AR
+        ref = (self.ws, self.wc, self.wf)[tensor]
+        start = shard * rows
+        if half is not None:
+            rows = rows // 2
+            start = start + half * rows
+        return ref.at[pl.ds(al(start, 16), rows), :]
+
+    def gcopy(self, tensor, zs, kind):
+        if kind == 0:
+            part, dev = self.piece(tensor, self.shard_at(zs)), self.dev(fx=1)
+        elif kind == 1:
+            part, dev = self.piece(tensor, self.shard_at(zs)), self.dev(fy=1)
+        elif kind == 2:
+            part, dev = self.piece(tensor, self.shard_at(zs, fx=1), 0), self.dev(fy=1)
+        elif kind == 3:
+            part, dev = self.piece(tensor, self.shard_at(zs, fy=1), 1), self.dev(fx=1)
+        else:
+            fx, fy = ((0, 0), (1, 0), (0, 1), (1, 1))[kind - 4]
+            part, dev = self.piece(tensor, self.shard_at(zs, fx, fy)), self.dev(fc=1)
+        row = (tensor * 4 + zs) * 8 + kind
+        return self.copy(part, part, self.gsend.at[row], self.grecv.at[row], dev)
+
+    def start(self, tensor, zs, kind):
+        self.gcopy(tensor, zs, kind).start()
+
+    def arrive(self, tensor, zs, kind):
+        if kind < 2:
+            part = self.piece(tensor, self.shard_at(zs, fx=1 - kind, fy=kind))
+        elif kind < 4:
+            part = self.piece(tensor, self.shard_at(zs, 1, 1), kind - 2)
+        else:
+            fx, fy = ((0, 0), (1, 0), (0, 1), (1, 1))[kind - 4]
+            part = self.piece(tensor, self.shard_at(zs, fx, fy, 1))
+        row = (tensor * 4 + zs) * 8 + kind
+        self.copy(
+            part, part, self.gsend.at[row], self.grecv.at[row], self.dev(fc=1)).wait_recv()
+
+    def z_arrive(self, tensor, k):
+        part = self.piece(tensor, self.shard_at((self.z + 4 - k) % 4))
+        row = tensor * 3 + k - 1
+        self.copy(
+            part, part, self.zsend.at[row], self.zrecv.at[row], self.dev(fc=1)).wait_recv()
+
+    def zcopy(self, tensor, k):
+        part = self.piece(tensor, self.shard)
+        row = tensor * 3 + k - 1
+        return self.copy(
+            part, part, self.zsend.at[row], self.zrecv.at[row], self.dev(z=(self.z + k) % 4)
+        )
+
+    def z_sends(self, tensor):
+        for k in (1, 3, 2):
+            self.zcopy(tensor, k).start()
+
+    def p1(self, tensor, zs, k=None):
+        if k is None:
+            for kk in (1, 2, 3):
+                @pl.when((self.z + 4 - kk) % 4 == zs)
+                def _(kk=kk):
+                    self.z_arrive(tensor, kk)
+        elif k:
+            self.z_arrive(tensor, k)
+        for kind in (0, 1, 4):
+            self.start(tensor, zs, kind)
+
+    def p2(self, tensor, zs):
+        self.arrive(tensor, zs, 0)
+        self.start(tensor, zs, 2)
+        self.start(tensor, zs, 5)
+        self.arrive(tensor, zs, 1)
+        self.start(tensor, zs, 3)
+        self.start(tensor, zs, 6)
+
+    def p3(self, tensor, zs):
+        self.arrive(tensor, zs, 2)
+        self.arrive(tensor, zs, 3)
+        self.start(tensor, zs, 7)
+
+    def p4(self, tensor, zs):
+        for kind in (4, 5, 6, 7):
+            self.arrive(tensor, zs, kind)
+
+    def sends_done(self, tensor):
+        for zs in range(4):
+            self.plane_sent(tensor, zs)
+        for k in (1, 2, 3):
+            self.zcopy(tensor, k).wait_send()
+
+    def plane_sent(self, tensor, zs):
+        for kind in range(8):
+            self.gcopy(tensor, zs, kind).wait_send()
+
+    def own_rows(self):
+        for src, dst in ((self.sh_s, self.ws), (self.sh_c, self.wc)):
+            self.flat[0:576, :] = src[...].astype(F32)
+            row = al(self.shard * AR, 16)
+            for t in range(6):
+                dst[pl.ds(row, AR), 128 * t:128 * t + 128] = self.flat[
+                    pl.ds(t, AR, stride=6), :].astype(BF)
+        self.own_ff()
+
+    def own_ff(self):
+        self.flat[0:1152, :] = self.sh_f[...].astype(F32)
+        base = self.shard * FU
+        flat, wf = self.flat, self.wf
+
+        def wide(rows):
+            for u in range(4):
+                for w in range(2):
+                    top = flat[pl.ds(4 * u + w, rows, stride=16), :]
+                    low = flat[pl.ds(4 * u + w + 2, rows, stride=16), :]
+                    wf[pl.ds(al(base + 2 * rows * u, 16), 2 * rows), 128 * w:128 * w + 128] = (
+                        jnp.concatenate([top, low], axis=0).astype(BF))
+
+        def tall(first, rows, offset):
+            for t in range(6):
+                wf[pl.ds(al(base + offset + rows * (t // 2), 16), rows),
+                   128 * (t % 2):128 * (t % 2) + 128] = flat[
+                       pl.ds(first + t, rows, stride=6), :].astype(BF)
+
+        @pl.when(self.shard < 21)
+        def _():
+            wide(72)
+
+        @pl.when(self.shard == 21)
+        def _():
+            wide(24)
+            tall(384, 128, 192)
+
+        @pl.when(self.shard > 21)
+        def _():
+            tall(0, 192, 0)
+
+    def build_wide(self, ch):
+        rows1 = 24 if ch == 10 else 72
+
+        def step(u, _):
+            low = self.wf[pl.ds(al(1152 * ch + 144 * u, 16), 144), :].astype(F32)
+            high = self.wf[
+                pl.ds(al(1152 * ch + FU + 2 * rows1 * u, 16), 2 * rows1), :].astype(F32)
+            for w in range(2):
+                value = jnp.concatenate(
+                    [low[72 * w:72 * w + 72], high[rows1 * w:rows1 * w + rows1]], axis=0)
+                self.wgu[144 * ch:144 * ch + 72 + rows1,
+                         pl.ds(al(512 * u + 256 * w, 256), 256)] = value.astype(BF)
+            return 0
+
+        lax.fori_loop(0, 4, step, 0)
+
+    def build_tall(self, s):
+        first, rows, offset = (0, 128, 192) if s == 21 else (192 * s - 4096, 192, 0)
+        for p in range(3):
+            self.wd[first:first + rows, 256 * p:256 * p + 256] = self.wf[
+                FU * s + offset + rows * p:FU * s + offset + rows * p + rows, :]
+
+    def build_plane(self, zs):
+        if zs < 2:
+            for ch in range(4 * zs, 4 * zs + 4):
+                self.build_wide(ch)
+        elif zs == 2:
+            for ch in (8, 9, 10):
+                self.build_wide(ch)
+            for s in (21, 22, 23):
+                self.build_tall(s)
+        else:
+            for s in range(24, 32):
+                self.build_tall(s)
+
+    def masks(self):
+        lane = lax.broadcasted_iota(jnp.int32, (128, 128), 1)
+        self.left = lane < DH
+
+    def stack(self, pair):
+        zero = jnp.zeros_like(pair)
+        return jnp.concatenate(
+            [jnp.where(self.left, pair, zero), jnp.where(self.left, zero, pair)], axis=0)
+
+    def unstack(self, both):
+        rows = both.shape[0] // 2
+        return jnp.where(self.left, both[0:rows], both[rows:])
+
+    def bias(self):
+        lane = lax.broadcasted_iota(jnp.int32, (1, 128), 1)
+        bucket = bucket_of((128 - lane) % 128)
+        for h in range(H):
+            row = jnp.zeros((1, 128), F32)
+            for b in range(NB):
+                row = jnp.where(bucket == b, self.table[b, h], row)
+            full = jnp.broadcast_to(row, (128, 128))
+            self.ps[128 * h:128 * h + 128, :] = pltpu.roll(
+                full, 0, 1, stride=1, stride_axis=0)
+
+    def project(self, left, ref, row, out):
+        for p in range(3):
+            out[:, 256 * p:256 * p + 256] = nn(
+                left, ref[row:row + D, 256 * p:256 * p + 256]).astype(BF)
+
+    def add_product(self, left, ref, row, base, out):
+        for p in range(3):
+            cols = slice(256 * p, 256 * p + 256)
+            out[:, cols] = base[:, cols].astype(F32) + nn(left, ref[row:row + D, cols])
+
+    def heads(self, p):
+        return pl.ds(al(p * 256, 256), 256)
+
+    def self_forward(self):
+        x = self.x_in[...].astype(F32)
+        self.n1[...] = rms(x, self.gains[0:1, :]).astype(BF)
+        n1 = self.n1[...]
+        for m, out in enumerate((self.q, self.k, self.v)):
+            self.project(n1, self.ws, D * m, out)
+        length = self.dl[0]
+        row = lax.broadcasted_iota(jnp.int32, (256, 128), 0) % 128
+        col = lax.broadcasted_iota(jnp.int32, (256, 128), 1)
+        keep = (col <= row) & (col < length)
+
+        def pair(p, _):
+            cols = pl.ds(al(p * 128, 128), 128)
+            s = nt(self.stack(self.q[:, cols]), self.k[:, cols]) + self.ps[self.heads(p), :]
+            s = jnp.where(keep, s, MASKED)
+            e = jnp.exp(s - jnp.max(s, axis=-1, keepdims=True))
+            prob = e / jnp.sum(e, axis=-1, keepdims=True)
+            self.ps[self.heads(p), :] = prob
+            self.mix[:, cols] = self.unstack(nn(prob.astype(BF), self.v[:, cols])).astype(BF)
+            return 0
+
+        lax.fori_loop(0, PAIRS, pair, 0)
+        self.add_product(self.mix[...], self.ws, 3 * D, self.x_in, self.r1)
+        self.n2[...] = rms(self.r1[...], self.gains[1:2, :]).astype(BF)
+
+    def cross_kv(self, m, out):
+        for i in range(4):
+            for p in range(3):
+                out[128 * i:128 * i + 128, 256 * p:256 * p + 256] = nn(
+                    self.mem[128 * i:128 * i + 128, :],
+                    self.wc[D * m:D * m + D, 256 * p:256 * p + 256]).astype(BF)
+
+    def cross_probs(self, p):
+        cols = pl.ds(al(p * 128, 128), 128)
+        col = lax.broadcasted_iota(jnp.int32, (256, self.mem.shape[0]), 1)
+        s = nt(self.stack(self.cq[:, cols]), self.ck[:, cols])
+        s = jnp.where(col < self.ml[0], s, MASKED)
+        e = jnp.exp(s - jnp.max(s, axis=-1, keepdims=True))
+        return e / jnp.sum(e, axis=-1, keepdims=True)
+
+    def cross_forward(self):
+        self.project(self.n2[...], self.wc, 0, self.cq)
+
+        def pair(p, _):
+            cols = pl.ds(al(p * 128, 128), 128)
+            prob = self.cross_probs(p)
+            self.cmix[:, cols] = self.unstack(nn(prob.astype(BF), self.cv[:, cols])).astype(BF)
+            return 0
+
+        lax.fori_loop(0, PAIRS, pair, 0)
+        self.add_product(self.cmix[...], self.wc, 3 * D, self.r1, self.r2)
+        self.n3[...] = rms(self.r2[...], self.gains[2:3, :]).astype(BF)
+
+    def ff_forward(self):
+        n3 = self.n3[...]
+        c0 = float(np.sqrt(2.0 / np.pi))
+
+        def chunk(i, _):
+            cols = pl.ds(al(i * 256, 256), 256)
+            a = nn(n3, self.wgu[0:D, cols])
+            up = nn(n3, self.wgu[D:2 * D, cols])
+            sq = a * a
+            t = jnp.tanh(c0 * (a + 0.044715 * a * sq))
+            gelu = 0.5 * a * (1.0 + t)
+            slope = 0.5 * (1.0 + t) + 0.5 * a * (1.0 - t * t) * (c0 * (1.0 + 0.134145 * sq))
+            self.ga[:, cols] = gelu
+            self.ub[:, cols] = up * slope
+            self.hid[:, cols] = (gelu * up).astype(BF)
+            return 0
+
+        lax.fori_loop(0, FF // 256, chunk, 0)
+
+    def out_rows(self):
+        hid = self.hid[...]
+        for p in range(3):
+            cols = slice(256 * p, 256 * p + 256)
+            self.block[:, cols] = (self.r2[:, cols] + nn(hid, self.wd[:, cols])).astype(BF)
+
+    def d_hidden(self):
+        g = self.g[...]
+
+        def chunk(i, _):
+            at = al(i * 256, 256)
+            cols = pl.ds(at, 256)
+            dh = nt(g, self.wd[pl.ds(at, 256), :]).astype(BF).astype(F32)
+            self.dg[:, cols] = (dh * self.ub[:, cols]).astype(BF)
+            self.du[:, cols] = (dh * self.ga[:, cols]).astype(BF)
+            return 0
+
+        lax.fori_loop(0, FF // 256, chunk, 0)
+
+    def place(self, g):
+        own = OWN[g]
+        out = OWN_ROWS + (g % 2) * STAGE
+        return own + self.c * (out - own), out + self.c * (own - out)
+
+    def grad_tall(self, g, ch, i):
+        b0, b1 = self.place(g)
+        gout = self.g[...]
+        first = 384 * ch - 4096
+
+        for p in range(3):
+            both = nn(self.hidt[pl.ds(al(first, 16), 384), :], gout[:, 256 * p:256 * p + 256])
+            self.gb[pl.ds(al(b0 + FU * i + 192 * p, 16), 192), :] = both[0:192].astype(BF)
+            self.gb[pl.ds(al(b1 + FU * i + 192 * p, 16), 192), :] = both[192:].astype(BF)
+
+    def grad_tall_part(self, base, i, first, rows, offset):
+        for p in range(3):
+            value = nn(self.hidt[first:first + rows, :], self.g[:, 256 * p:256 * p + 256])
+            self.gb[pl.ds(al(base + FU * i + offset + rows * p, 16), rows), :] = value.astype(BF)
+
+    def grad_wide(self, g, ch, i):
+        b0, b1 = self.place(g)
+        rows1 = 24 if ch == 10 else 72
+        first, end = 144 * ch, 144 * ch + 72 + rows1
+
+        def step(u, _):
+            cols = pl.ds(al(512 * u, 512), 512)
+            parts = []
+            if first < D:
+                parts.append(nn(self.n3t[first:min(end, D), :], self.dg[:, cols]))
+            if end > D:
+                parts.append(nn(self.n3t[max(first, D) - D:end - D, :], self.du[:, cols]))
+            both = parts[0] if len(parts) == 1 else jnp.concatenate(parts, axis=0)
+            for base, at, rows in ((b0, 0, 72), (b1, 72, rows1)):
+                value = jnp.concatenate(
+                    [both[at:at + rows, 0:256], both[at:at + rows, 256:512]], axis=0)
+                self.gb[pl.ds(al(base + FU * i + 2 * rows * u, 16), 2 * rows), :] = (
+                    value.astype(BF))
+            return 0
+
+        lax.fori_loop(0, 4, step, 0)
+
+    def grad_ff(self, g):
+        zb = GROUPS[g][1]
+        if zb == 3:
+            def step(i, _):
+                self.grad_tall(g, 12 + i, i)
+                return 0
+            lax.fori_loop(0, 4, step, 0)
+        elif zb == 2:
+            b0, b1 = self.place(g)
+            for i in range(3):
+                self.grad_wide(g, 8 + i, i)
+            self.grad_tall_part(b1, 2, 0, 128, 192)
+            self.grad_tall_part(b0, 3, 128, 192, 0)
+            self.grad_tall_part(b1, 3, 320, 192, 0)
+        else:
+            for i in range(4):
+                self.grad_wide(g, 4 * zb + i, i)
+
+    def grad_square(self, g, leftt, right):
+        b0, b1 = self.place(g)
+
+        def step(i, _):
+            rows = leftt[pl.ds(al(192 * i, 16), 192), :]
+            for p in range(3):
+                both = nn(rows, right[:, 256 * p:256 * p + 256])
+                self.gb[pl.ds(al(b0 + AU * i + 96 * p, 16), 96), :] = both[0:96].astype(BF)
+                self.gb[pl.ds(al(b1 + AU * i + 96 * p, 16), 96), :] = both[96:].astype(BF)
+            return 0
+
+        lax.fori_loop(0, 4, step, 0)
+
+    def back_product(self, terms, out):
+        for p in range(3):
+            total = None
+            for d_ref, w_ref, row, width in terms:
+                value = nt(d_ref[...], w_ref[row + 256 * p:row + 256 * p + 256, 0:width])
+                total = value if total is None else total + value
+            out[:, 256 * p:256 * p + 256] = total
+
+    def norm_three_back(self):
+        self.back_product(((self.dg, self.wgu, 0, FF), (self.du, self.wgu, D, FF)), self.dz)
+        dv, dg = rms_back(self.r2[...], self.gains[2:3, :], self.dz[...])
+        self.redg[2:3, :] = dg
+        self.dr[...] = self.g[...].astype(F32) + dv
+        self.drb[...] = self.dr[...].astype(BF)
+
+    def cross_back(self):
+        for p in range(3):
+            self.dm[:, 256 * p:256 * p + 256] = nt(
+                self.drb[...], self.wc[3 * D + 256 * p:3 * D + 256 * p + 256, :]).astype(BF)
+
+        def pair(p, _):
+            cols = pl.ds(al(p * 128, 128), 128)
+            dms = self.stack(self.dm[:, cols])
+            kp = self.ck[:, cols]
+            qs = self.stack(self.cq[:, cols])
+            prob = self.cross_probs(p)
+            dp = nt(dms, self.cv[:, cols])
+            ds = (prob * (dp - jnp.sum(prob * dp, axis=-1, keepdims=True))).astype(BF)
+            self.cv[:, cols] = tn(prob.astype(BF), dms).astype(BF)
+            self.cq[:, cols] = self.unstack(nn(ds, kp)).astype(BF)
+            self.ck[:, cols] = tn(ds, qs).astype(BF)
+            return 0
+
+        lax.fori_loop(0, PAIRS, pair, 0)
+
+    def memory_rows(self):
+        for i in range(4):
+            rows = slice(128 * i, 128 * i + 128)
+            for p in range(3):
+                wrow = 256 * p
+                self.mgrad[rows, 256 * p:256 * p + 256] = (
+                    nt(self.ck[rows, :], self.wc[D + wrow:D + wrow + 256, :])
+                    + nt(self.cv[rows, :], self.wc[2 * D + wrow:2 * D + wrow + 256, :])
+                ).astype(BF)
+
+    def norm_two_back(self):
+        self.back_product(((self.cq, self.wc, 0, D),), self.dz)
+        dv, dg = rms_back(self.r1[...], self.gains[1:2, :], self.dz[...])
+        self.redg[1:2, :] = dg
+        self.dr[...] = self.dr[...] + dv
+        self.drb[...] = self.dr[...].astype(BF)
+
+    def self_back(self):
+        for p in range(3):
+            self.dm[:, 256 * p:256 * p + 256] = nt(
+                self.drb[...], self.ws[3 * D + 256 * p:3 * D + 256 * p + 256, :]).astype(BF)
+
+        def pair(p, _):
+            cols = pl.ds(al(p * 128, 128), 128)
+            dms = self.stack(self.dm[:, cols])
+            kp = self.k[:, cols]
+            qs = self.stack(self.q[:, cols])
+            prob = self.ps[self.heads(p), :]
+            dp = nt(dms, self.v[:, cols])
+            ds = (prob * (dp - jnp.sum(prob * dp, axis=-1, keepdims=True))).astype(BF)
+            self.ps[self.heads(p), :] = ds.astype(F32)
+            self.v[:, cols] = tn(prob.astype(BF), dms).astype(BF)
+            self.q[:, cols] = self.unstack(nn(ds, kp)).astype(BF)
+            self.k[:, cols] = tn(ds, qs).astype(BF)
+            return 0
+
+        lax.fori_loop(0, PAIRS, pair, 0)
+
+    def norm_one_back(self):
+        self.back_product(
+            ((self.q, self.ws, 0, D), (self.k, self.ws, D, D), (self.v, self.ws, 2 * D, D)),
+            self.dz)
+        dv, dg = rms_back(self.x_in[...].astype(F32), self.gains[0:1, :], self.dz[...])
+        self.redg[0:1, :] = dg
+        self.xgrad[...] = (self.dr[...] + dv).astype(BF)
+
+    def table_back(self):
+        row = lax.broadcasted_iota(jnp.int32, (128, 128), 0)
+        col = lax.broadcasted_iota(jnp.int32, (128, 128), 1)
+        flip = jnp.where(row + col == 127, 1.0, 0.0).astype(BF)
+        self.diag[...] = jnp.zeros_like(self.diag)
+        for p in range(PAIRS):
+            back = nn(self.ps[256 * p:256 * p + 256, :].astype(BF), flip)
+            for hh in range(2):
+                turned = pltpu.roll(
+                    back[128 * hh:128 * hh + 128], 0, 1, stride=1, stride_axis=0)
+                self.diag[2 * p + hh:2 * p + hh + 1, :] = jnp.sum(turned, axis=0, keepdims=True)
+        lane = lax.broadcasted_iota(jnp.int32, (NB, 128), 1)
+        hot = jnp.where(
+            bucket_of((lane + 1) % 128) == lax.broadcasted_iota(jnp.int32, (NB, 128), 0), 1.0, 0.0)
+        self.redt[:, 0:16] = lax.dot_general(
+            hot, self.diag[...], (((1,), (1,)), ((), ())),
+            precision=lax.Precision.HIGHEST, preferred_element_type=F32)
+
+    def ropy(self, src, dst, g, kind, device):
+        row = g * 8 + kind
+        return self.copy(src, dst, self.rsend.at[row], self.rrecv.at[row], device)
+
+    def own(self, g, chip, half=None):
+        unit = UNIT[g]
+        start = OWN[g] + chip * unit
+        if half is not None:
+            unit = unit // 2
+            start = start + half * unit
+        return pl.ds(al(start, 16), unit)
+
+    def land(self, g, which, half=None):
+        unit = UNIT[g]
+        start = LAND[g] + (0, unit // 2, unit, 2 * unit)[which]
+        rows = unit // 2 if which < 2 else unit
+        if half is not None:
+            rows = unit // 2
+            start = start + half * rows
+        return pl.ds(start, rows)
+
+    def scopy(self, g, kind):
+        gb, lb = self.gb, self.lb
+        if kind == 0:
+            rows = 4 * UNIT[g]
+            return self.ropy(
+                gb.at[pl.ds(OWN_ROWS + (g % 2) * STAGE, rows), :],
+                self.wf.at[pl.ds(OWN[g], rows), :], g, 0, self.dev(fc=1))
+        src, dst, dev = {
+            1: (self.own(g, self.chip(1, 1), 0), self.land(g, 0), self.dev(fx=1)),
+            2: (self.own(g, self.chip(1, 1), 1), self.land(g, 1), self.dev(fy=1)),
+            3: (self.own(g, self.chip(1, 0), 0), self.land(g, 2, 0), self.dev(fx=1)),
+            4: (self.own(g, self.chip(1, 0), 1), self.land(g, 2, 1), self.dev(fx=1)),
+            5: (self.own(g, self.chip(0, 1), 1), self.land(g, 3, 1), self.dev(fy=1)),
+            6: (self.own(g, self.chip(0, 1), 0), self.land(g, 3, 0), self.dev(fy=1)),
+        }[kind]
+        return self.ropy(gb.at[src, :], lb.at[dst, :], g, kind, dev)
+
+    def to_owner(self, g):
+        t, zb = GROUPS[g]
+        unit = UNIT[g]
+        slot = (self.z + 3 - zb) % 4
+        return self.copy(
+            self.gb.at[self.own(g, self.chip()), :],
+            self.zb.at[pl.ds(al(ZBASE[t] + slot * unit, 16), unit), :],
+            self.rsend.at[g * 8 + 7], self.orecv.at[t * 3 + slot], self.dev(z=zb))
+
+    def from_plane(self, g, slot):
+        t, zb = GROUPS[g]
+        unit = UNIT[g]
+        return self.copy(
+            self.gb.at[self.own(g, self.chip()), :],
+            self.zb.at[pl.ds(ZBASE[t] + slot * unit, unit), :],
+            self.rsend.at[g * 8 + 7], self.orecv.at[t * 3 + slot], self.dev(z=zb))
+
+    def rs0(self, g):
+        self.scopy(g, 0).start()
+
+    def stage_free(self, g):
+        if g >= 2:
+            self.scopy(g - 2, 0).wait_send()
+
+    def accumulate(self, dst, src_ref, src):
+        self.gb[dst, :] = (
+            self.gb[dst, :].astype(F32) + src_ref[src, :].astype(F32)).astype(BF)
+
+    def rs1(self, g):
+        self.scopy(g, 0).wait_recv()
+        for fx, fy, kinds in ((1, 1, (1, 2)), (1, 0, (3,)), (0, 1, (5,)), (0, 0, ())):
+            rows = self.own(g, self.chip(fx, fy))
+            self.accumulate(rows, self.wf, rows)
+            for kind in kinds:
+                self.scopy(g, kind).start()
+
+    def rs2(self, g):
+        self.scopy(g, 1).wait_recv()
+        self.accumulate(self.own(g, self.chip(0, 1), 0), self.lb, self.land(g, 0))
+        self.scopy(g, 6).start()
+        self.scopy(g, 2).wait_recv()
+        self.accumulate(self.own(g, self.chip(1, 0), 1), self.lb, self.land(g, 1))
+        self.scopy(g, 4).start()
+
+    def rs3(self, g):
+        for kind in (3, 5, 4, 6):
+            self.scopy(g, kind).wait_recv()
+        rows = self.own(g, self.chip())
+        self.gb[rows, :] = (
+            self.gb[rows, :].astype(F32) + self.lb[self.land(g, 2), :].astype(F32)
+            + self.lb[self.land(g, 3), :].astype(F32)).astype(BF)
+
+        @pl.when(self.z != GROUPS[g][1])
+        def _():
+            self.to_owner(g).start()
+
+    def rs4(self, g):
+        t, zb = GROUPS[g]
+        unit = UNIT[g]
+
+        @pl.when(self.z == zb)
+        def _():
+            for slot in range(3):
+                self.from_plane(g, slot).wait_recv()
+            rows = self.own(g, self.chip())
+
+            def total(start, size, lanes):
+                at = pl.ds(al(OWN[g] + self.chip() * unit + start, 16), size)
+                value = self.gb[at, lanes].astype(F32)
+                for slot in range(3):
+                    value = value + self.zb[
+                        pl.ds(ZBASE[t] + slot * unit + start, size), lanes].astype(F32)
+                return value
+
+            del rows
+            if t < 2:
+                out = (self.gs, self.gc)[t]
+                for k in range(6):
+                    out[pl.ds(k, AR, stride=6), :] = total(
+                        96 * (k // 2), 96, slice(128 * (k % 2), 128 * (k % 2) + 128))
+                return
+            out = self.gf
+
+            def wide(rows):
+                for u in range(4):
+                    for w in range(2):
+                        v = total(2 * rows * u, 2 * rows, slice(128 * w, 128 * w + 128))
+                        out[pl.ds(4 * u + w, rows, stride=16), :] = v[0:rows]
+                        out[pl.ds(4 * u + w + 2, rows, stride=16), :] = v[rows:]
+
+            def tall(first, rows, offset):
+                for k in range(6):
+                    out[pl.ds(first + k, rows, stride=6), :] = total(
+                        offset + rows * (k // 2), rows, slice(128 * (k % 2), 128 * (k % 2) + 128))
+
+            if zb < 2:
+                wide(72)
+            elif zb == 3:
+                tall(0, 192, 0)
+            else:
+                @pl.when(self.shard < 21)
+                def _():
+                    wide(72)
+
+                @pl.when(self.shard == 21)
+                def _():
+                    wide(24)
+                    tall(384, 128, 192)
+
+                @pl.when(self.shard > 21)
+                def _():
+                    tall(0, 192, 0)
+
+    def group_sent(self, g):
+        for kind in range(1, 7):
+            self.scopy(g, kind).wait_send()
+
+        @pl.when(self.z != GROUPS[g][1])
+        def _():
+            self.to_owner(g).wait_send()
+
+    def small(self, step, which):
+        dev = (
+            self.dev(fc=1), self.dev(fx=1), self.dev(fy=1),
+            self.dev(z=self.z + 1 - 2 * (self.z % 2)), self.dev(z=(self.z + 2) % 4),
+        )[step]
+        src, dst = ((self.redg, self.landg), (self.redt, self.landt))[which]
+        row = step * 2 + which
+        return self.copy(
+            src.at[step], dst.at[step], self.ssend.at[row], self.srecv.at[row], dev)
+
+    def small_start(self, step):
+        for which in range(2):
+            self.small(step, which).start()
+
+    def small_add(self, step):
+        for which in range(2):
+            self.small(step, which).wait_recv()
+        self.redg[step + 1] = self.redg[step] + self.landg[step]
+        self.redt[step + 1] = self.redt[step] + self.landt[step]
+
+
+NAMES = (
+    "x_in", "mem", "g", "dl", "ml", "sh_s", "sh_c", "sh_f", "gains", "table",
+    "block", "xgrad", "mgrad", "gs", "gc", "gf", "ggain", "gtable",
+    "ws", "wc", "wf", "wgu", "wd", "gb", "lb", "zb",
+    "n1", "q", "k", "v", "mix", "r1", "n2", "cq", "ck", "cv", "cmix", "r2", "n3",
+    "ga", "ub", "hid", "hidt", "n3t", "dg", "du", "dz", "dr", "drb", "tt", "memt",
+    "ps", "diag", "redga", "redta", "landg", "landt",
+    "gsend", "grecv", "zsend", "zrecv", "rsend", "rrecv", "orecv", "ssend", "srecv", "free",
+)
+
+
+def kernel(*args):
+    refs = dict(zip(NAMES, args))
+    st = Layer(refs)
+    st.redg, st.redt = st.redga.at[0], st.redta.at[0]
+
+    barrier = pltpu.get_barrier_semaphore()
+    others = [st.dev(fc=1), st.dev(fx=1), st.dev(fy=1)] + [
+        st.dev(z=(st.z + k) % 4) for k in (1, 2, 3)]
+    for other in others:
+        pl.semaphore_signal(barrier, inc=1, device_id=other, device_id_type=MESH)
+    st.own_rows()
+    st.masks()
+    pl.semaphore_wait(barrier, 6)
+
+    st.z_sends(0)
+    plane = [(st.z + 4 - k) % 4 for k in range(4)]
+    st.p1(0, plane[0], 0)
+    st.bias()
+    st.p1(0, plane[1], 1)
+    st.p2(0, plane[0])
+    st.p1(0, plane[3], 3)
+    st.p2(0, plane[1])
+    st.p3(0, plane[0])
+    st.p1(0, plane[2], 2)
+    st.z_sends(1)
+    st.p2(0, plane[3])
+    st.p3(0, plane[1])
+    st.p1(1, plane[0], 0)
+    st.p2(0, plane[2])
+    st.p3(0, plane[3])
+    st.p1(1, plane[1], 1)
+    st.p2(1, plane[0])
+    st.p3(0, plane[2])
+    for zs in range(4):
+        st.p4(0, plane[zs])
+    st.self_forward()
+    st.p1(1, plane[3], 3)
+    st.p2(1, plane[1])
+    st.p3(1, plane[0])
+    st.p1(1, plane[2], 2)
+    st.z_sends(2)
+    st.p2(1, plane[3])
+    st.p3(1, plane[1])
+    st.p1(2, 0)
+    st.p2(1, plane[2])
+    st.p3(1, plane[3])
+    st.p1(2, 1)
+    st.p2(2, 0)
+    st.p3(1, plane[2])
+    for zs in range(4):
+        st.p4(1, plane[zs])
+    st.cross_kv(1, st.ck)
+    st.cross_kv(2, st.cv)
+    st.p1(2, 2)
+    st.p2(2, 1)
+    st.p3(2, 0)
+    st.cross_forward()
+    st.p1(2, 3)
+    st.p2(2, 2)
+    st.p3(2, 1)
+    st.p4(2, 0)
+    st.build_plane(0)
+    st.p4(2, 1)
+    st.build_plane(1)
+    st.p2(2, 3)
+    st.p3(2, 2)
+    st.p4(2, 2)
+    st.build_plane(2)
+    st.ff_forward()
+    st.hidt[...] = st.hid[...].T
+    st.p3(2, 3)
+    st.p4(2, 3)
+    st.build_plane(3)
+    for t in range(3):
+        st.sends_done(t)
+    pl.semaphore_signal(st.free, inc=1, device_id=st.dev(fc=1), device_id_type=MESH)
+    st.grad_ff(0)
+    pl.semaphore_wait(st.free, 1)
+    st.rs0(0)
+    st.d_hidden()
+    st.n3t[...] = st.n3[...].T
+    st.grad_ff(1)
+    st.rs0(1)
+    st.rs1(0)
+    st.out_rows()
+    st.stage_free(2)
+    st.grad_ff(2)
+    st.rs0(2)
+    st.rs1(1)
+    st.rs2(0)
+    st.stage_free(3)
+    st.grad_ff(3)
+    st.rs0(3)
+    st.rs1(2)
+    st.rs2(1)
+    st.rs3(0)
+    st.norm_three_back()
+    st.tt[...] = st.cmix[...].T
+    st.stage_free(4)
+    st.grad_square(4, st.tt, st.drb)
+    st.rs0(4)
+    st.rs1(3)
+    st.rs2(2)
+    st.rs3(1)
+    st.rs4(0)
+    st.cross_back()
+    st.memt[...] = st.mem[...].T
+    st.stage_free(5)
+    st.grad_square(5, st.memt, st.cv)
+    st.rs0(5)
+    st.rs1(4)
+    st.rs2(3)
+    st.rs3(2)
+    st.rs4(1)
+    st.stage_free(6)
+    st.grad_square(6, st.memt, st.ck)
+    st.rs0(6)
+    st.rs1(5)
+    st.rs2(4)
+    st.rs3(3)
+    st.rs4(2)
+    st.tt[...] = st.n2[...].T
+    st.stage_free(7)
+    st.grad_square(7, st.tt, st.cq)
+    st.rs0(7)
+    st.norm_two_back()
+    st.rs1(6)
+    st.rs2(5)
+    st.rs3(4)
+    st.rs4(3)
+    st.tt[...] = st.mix[...].T
+    st.stage_free(8)
+    st.grad_square(8, st.tt, st.drb)
+    st.rs0(8)
+    st.self_back()
+    st.rs1(7)
+    st.rs2(6)
+    st.rs3(5)
+    st.rs4(4)
+    st.tt[...] = st.n1[...].T
+    st.stage_free(9)
+    st.grad_square(9, st.tt, st.v)
+    st.rs0(9)
+    st.rs1(8)
+    st.rs2(7)
+    st.rs3(6)
+    st.rs4(5)
+    st.stage_free(10)
+    st.grad_square(10, st.tt, st.k)
+    st.rs0(10)
+    st.norm_one_back()
+    st.table_back()
+    st.redg, st.redt = st.redga, st.redta
+    st.small_start(0)
+    st.rs1(9)
+    st.rs2(8)
+    st.rs3(7)
+    st.rs4(6)
+    st.small_add(0)
+    st.small_start(1)
+    st.stage_free(11)
+    st.grad_square(11, st.tt, st.q)
+    st.rs0(11)
+    st.rs1(10)
+    st.rs2(9)
+    st.rs3(8)
+    st.rs4(7)
+    st.small_add(1)
+    st.small_start(2)
+    st.rs1(11)
+    st.rs2(10)
+    st.rs3(9)
+    st.rs4(8)
+    st.memory_rows()
+    st.small_add(2)
+    st.small_start(3)
+    st.rs2(11)
+    st.rs3(10)
+    st.rs4(9)
+    st.small_add(3)
+    st.small_start(4)
+    st.rs3(11)
+    st.rs4(10)
+    st.small_add(4)
+    st.ggain[...] = st.redga[5, 0:3, :]
+    st.gtable[...] = st.redta[5, :, 0:H]
+    st.rs4(11)
+    for g in range(12):
+        st.group_sent(g)
+    st.scopy(10, 0).wait_send()
+    st.scopy(11, 0).wait_send()
+    for step in range(5):
+        for which in range(2):
+            st.small(step, which).wait_send()
+
+
+def fused(inputs, memory, out_cotangent, dec_lengths, mem_lengths, self_params, cross_params,
+          ff_params, gains, table):
+    slots, length, width = inputs.shape
+    mem_len = memory.shape[1]
+    vm = pl.BlockSpec(memory_space=pltpu.VMEM)
+    sm = pl.BlockSpec(memory_space=pltpu.SMEM)
+    s = jax.ShapeDtypeStruct
+    rows_s, rows_f = self_params.shape[0] // 128, ff_params.shape[0] // 128
+    row = pltpu.VMEM((length, D), BF)
+    rowf = pltpu.VMEM((length, D), F32)
+    memory_row = pltpu.VMEM((mem_len, D), BF)
+    dma = pltpu.SemaphoreType.DMA
+    outs = pl.pallas_call(
+        kernel,
+        out_shape=(
+            s((length, D), BF), s((length, D), BF), s((mem_len, D), BF),
+            s((rows_s, 128), F32), s((rows_s, 128), F32), s((rows_f, 128), F32),
+            s((3, D), F32), s((NB, H), F32),
+        ),
+        in_specs=[vm, vm, vm, sm, sm, vm, vm, vm, vm, sm],
+        out_specs=[vm] * 8,
+        scratch_shapes=[
+            pltpu.VMEM((4 * D, D), BF), pltpu.VMEM((4 * D, D), BF),
+            pltpu.VMEM((32 * FU, 256), BF),
+            pltpu.VMEM((2 * D, FF), BF), pltpu.VMEM((FF, D), BF),
+            pltpu.VMEM((OWN_ROWS + 2 * STAGE, 256), BF),
+            pltpu.VMEM((LAND_ROWS, 256), BF), pltpu.VMEM((Z_ROWS, 256), BF),
+            row, row, row, row, row, rowf, row, row, memory_row, memory_row, row, rowf, row,
+            pltpu.VMEM((length, FF), F32), pltpu.VMEM((length, FF), F32),
+            pltpu.VMEM((length, FF), BF), pltpu.VMEM((FF, length), BF),
+            pltpu.VMEM((D, length), BF),
+            pltpu.VMEM((length, FF), BF), pltpu.VMEM((length, FF), BF),
+            rowf, rowf, row, pltpu.VMEM((D, length), BF), pltpu.VMEM((D, mem_len), BF),
+            pltpu.VMEM((H * length, length), F32),
+            pltpu.VMEM((16, 128), F32),
+            pltpu.VMEM((6, 8, D), F32), pltpu.VMEM((6, NB, 128), F32),
+            pltpu.VMEM((5, 8, D), F32), pltpu.VMEM((5, NB, 128), F32),
+            dma((96,)), dma((96,)), dma((9,)), dma((9,)), dma((96,)), dma((96,)), dma((9,)),
+            dma((10,)), dma((10,)), pltpu.SemaphoreType.REGULAR,
+        ],
+        compiler_params=pltpu.CompilerParams(
+            collective_id=0, has_side_effects=True, vmem_limit_bytes=67000000),
+        cost_estimate=pl.CostEstimate(
+            flops=10_000_000_000, bytes_accessed=8_000_000, transcendentals=2_000_000),
+    )(
+        inputs.reshape(length, width), memory.reshape(mem_len, width),
+        out_cotangent.reshape(length, width), dec_lengths, mem_lengths,
+        self_params.reshape(rows_s, 128), cross_params.reshape(rows_s, 128),
+        ff_params.reshape(rows_f, 128), gains, table,
+    )
+    return (
+        outs[0].reshape(inputs.shape), outs[1].reshape(inputs.shape),
+        outs[2].reshape(memory.shape), outs[3].reshape(-1), outs[4].reshape(-1),
+        outs[5].reshape(-1), outs[6], outs[7],
+    )
 
 
 HIGHEST = lax.Precision.HIGHEST
-MASKED = -1000000000.0
 
 
 def product(left, right):
@@ -357,7 +1370,7 @@
     )
 
 
-def local(
+def by_collectives(
     inputs,
     memory,
     out_cotangent,
@@ -478,31 +1491,14 @@
 
 
 def solution(mesh):
-    placed = (
-        P(("dp", "fsdp"), None, None),
-        P(("dp", "fsdp"), None, None),
-        P(("dp", "fsdp"), None, None),
-        P(("dp", "fsdp")),
-        P(("dp", "fsdp")),
-        P(("dp", "fsdp")),
-        P(("dp", "fsdp")),
-        P(("dp", "fsdp")),
-        P(),
-        P(),
-    )
+    whole = ("dp", "fsdp")
+    rows = P(whole, None, None)
+    flat = P(whole)
+    small = mesh.shape["dp"] == 8 and mesh.shape["fsdp"] == 4
     return jax.shard_map(
-        local,
+        fused if small else by_collectives,
         mesh=mesh,
-        in_specs=placed,
-        out_specs=(
-            P(("dp", "fsdp"), None, None),
-            P(("dp", "fsdp"), None, None),
-            P(("dp", "fsdp"), None, None),
-            P(("dp", "fsdp")),
-            P(("dp", "fsdp")),
-            P(("dp", "fsdp")),
-            P(),
-            P(),
-        ),
+        in_specs=(rows, rows, rows, flat, flat, flat, flat, flat, P(), P()),
+        out_specs=(rows, rows, rows, flat, flat, flat, P(), P()),
         check_vma=False,
     )

time: 950 us -> 234 us (0.25)
  waiting for transfers between devices: 233 us -> 0 us
  Pallas kernels: 0 us -> 223 us
  blocking collectives: 219 us -> 0 us
  other arithmetic: 205 us -> 0 us
  local copies, waits for them, and re-layouts: 193 us -> 9.45 us
  matrix products: 61.9 us -> 0 us
  between operations: 17.7 us -> 1.98 us
  starting transfers between devices: 15.7 us -> 0 us
    pallas_call x0 -> x1, Pallas kernels: none -> 223 us  [fused(): pl.pallas_call(kernel, out_shape=(s((length, D), BF), s((length, D), BF),...]
    psum x1 -> x0, blocking collectives: 219 us -> none  [local(): lax.psum((gain_local, table_local), ('dp', 'fsdp'))]
    all_gather x3 -> x0, waiting for transfers between devices: 152 us -> none  [the longest x1 59.2 us: gather_weights(): lax.all_gather(cross_params, ('dp', 'fsdp'), axis=0, tiled=True)]
    convert_element_type x8 -> x0, other arithmetic: 124 us -> none  [the longest x1 59.4 us: scatter_grads(): ff_full.reshape(wide_count, -1).astype(jnp.bfloat16)]
    unnamed x180 -> x21, local copies, waits for them, and re-layouts: 91.2 us -> 9.45 us
    dot_general x46 -> x0, matrix products: 57.9 us -> none  [the longest x11 16.7 us: product(): return jnp.dot(left, right, preferred_element_type=jnp.float32)]
    reduce_sum x5 -> x0, other arithmetic: 57.8 us -> none  [the longest x1 27.1 us: scatter_grads(): ff_block = jnp.sum(spread[2], axis=0)]
    slice x15 -> x0, local copies, waits for them, and re-layouts: 54.2 us -> none  [the longest x2 13.4 us: unpack(): ff_flat[2 * block_size:].reshape(FF, D)]
  transfers between devices with their start and end apart: 7 -> 0, of which waited for: 5 -> 0; matrix products, arithmetic and copies ran while one was open for 32% -> 0% of each run, Pallas kernels for 0% -> 0%
where the time goes in v1:
time: 234 us
  Pallas kernels  223 us (95%)
  local copies, waits for them, and re-layouts  9.45 us (4%)
    pallas_call x1, Pallas kernels, fused(): pl.pallas_call(kernel, out_shape=(s((length, D), BF), s((length, D), BF),...  223 us
    unnamed x21, local copies, waits for them, and re-layouts  9.45 us

profile of v1, /device:TPU:0, one launch (start us, length us, event | category | flops | bytes accessed | tf_op | source)
XLA Modules:
  0.0 234.2 jit_solution(15983558909108989463)
XLA Ops:
  0.6 0.0 copy-start.5
  1.9 0.0 copy-done.5
  2.0 0.7 copy.18.args_9_
  2.6 222.7 %shard_map.161 = (bf16[128,768]{1,0:T(8,128)(2,1)}, bf16[128,768]{1,0:T(8,128)(2,1)}, bf16[512,768]{1,0:T(8,128)(2,1)}, f32[576,128]{1,0:T(8,128)}, f32[576,128]...) custom-call(bf16[128,768]{1,0:T(8,128)(2,1)} %bitcast.20, bf16[512,768]{1,0:T(8,128)(2,1)} %bitcast.18, ...), custom_call_target="tpu_custom_call" | custom-call | flops 10000000000 | bytes 8000000 | tf_op jit(solution)/shard_map/pallas_call | solution.py:984
  225.4 0.0 copy-start
  225.4 1.5 copy.19
  226.9 1.6 copy.29
  228.5 1.6 copy.30
  230.1 0.0 copy-done
  230.1 0.0 copy-start.3
  230.1 0.0 copy-start.2
  230.1 0.9 copy.31
  231.0 0.2 copy-done.3
  231.2 0.0 copy-start.1
  231.2 0.7 copy.32
  232.0 0.0 copy-done.2
  232.0 0.7 copy.33
  232.7 0.0 copy-done.1
  232.7 0.0 copy-start.4
  232.7 0.9 copy.34
  233.6 0.0 copy-done.4
  233.6 0.6 copy.35
Async XLA Ops:
  0.6 1.3 copy-start.5
  225.4 4.7 %copy-start = (bf16[512,768]{1,0:T(8,128)(2,1)S(1)}, bf16[512,768]{1,0:T(8,128)(2,1)}, u32[]{:S(2)}) copy-start(bf16[512,768]{1,0:T(8,128)(2,1)} %get-tuple-element.18) | copy-start | bytes 2359300
  230.1 1.1 copy-start.3
  230.1 1.9 copy-start.2
  231.2 1.5 copy-start.1
  232.7 0.9 copy-start.4

commit v2 on v1

--- a/solution.py
+++ b/solution.py
@@ -26,8 +26,10 @@
 GROUPS = (
     (2, 3), (2, 2), (2, 0), (2, 1),
     (1, 3), (1, 2), (1, 1), (1, 0),
-    (0, 3), (0, 2), (0, 1), (0, 0),
+    (0, 3), (0, 0), (0, 2), (0, 1),
 )
+PAIR = (True,) * 2 + (False,) * 10
+SHARED = (False, False, True)
 UNIT = tuple(FU if t == 2 else AU for t, _ in GROUPS)
 OWN = tuple(4 * sum(UNIT[:g]) for g in range(12))
 OWN_ROWS = 4 * sum(UNIT)
@@ -36,6 +38,8 @@
 ZBASE = (0, 3 * AU, 6 * AU)
 Z_ROWS = 6 * AU + 3 * FU
 STAGE = 4 * FU
+ROLES = ((1, 1), (1, 0), (0, 1), (0, 0))
+SIB = (0, 12, 13, 14)
 
 
 def limits():
@@ -112,44 +116,59 @@
             device_id=device, device_id_type=MESH,
         )
 
-    def piece(self, tensor, shard, half=None):
+    def piece(self, tensor, shard, half=None, par=None):
         rows = FU if tensor == 2 else AR
         ref = (self.ws, self.wc, self.wf)[tensor]
         start = shard * rows
-        if half is not None:
-            rows = rows // 2
-            start = start + half * rows
-        return ref.at[pl.ds(al(start, 16), rows), :]
-
-    def gcopy(self, tensor, zs, kind):
-        if kind == 0:
-            part, dev = self.piece(tensor, self.shard_at(zs)), self.dev(fx=1)
-        elif kind == 1:
-            part, dev = self.piece(tensor, self.shard_at(zs)), self.dev(fy=1)
-        elif kind == 2:
-            part, dev = self.piece(tensor, self.shard_at(zs, fx=1), 0), self.dev(fy=1)
-        elif kind == 3:
-            part, dev = self.piece(tensor, self.shard_at(zs, fy=1), 1), self.dev(fx=1)
+        if half is None:
+            return ref.at[pl.ds(al(start, 16), rows), :]
+        rows = rows // 2
+        start = pl.ds(al(start + half * rows, 16), rows)
+        if not SHARED[tensor]:
+            return ref.at[start, :]
+        width = ref.shape[1] // 2
+        return ref.at[start, pl.ds(al(par * width, 128), width)]
+
+    def plane(self, tensor, k):
+        return k if tensor == 2 else (self.z + 4 - k) % 4
+
+    def gcopy(self, tensor, zs, kind, there=False):
+        par = self.z % 2
+        if kind < 2:
+            spot, dev = (0, 0), ((1, 0), (0, 1))[kind]
+            if there:
+                spot = dev
+            part, dev = self.piece(tensor, self.shard_at(zs, *spot)), self.dev(None, *dev)
+        elif kind < 4:
+            spot, dev = ((1, 0), (0, 1)) if kind == 2 else ((0, 1), (1, 0))
+            if there:
+                spot = (1, 1)
+            part = self.piece(tensor, self.shard_at(zs, *spot), kind - 2, par)
+            dev = self.dev(None, *dev)
+        elif kind < 8:
+            spot = ((0, 0), (1, 0), (0, 1), (1, 1))[kind - 4]
+            part = self.piece(tensor, self.shard_at(zs, *spot, 1 if there else 0))
+            dev = self.dev(fc=1)
         else:
-            fx, fy = ((0, 0), (1, 0), (0, 1), (1, 1))[kind - 4]
-            part, dev = self.piece(tensor, self.shard_at(zs, fx, fy)), self.dev(fc=1)
-        row = (tensor * 4 + zs) * 8 + kind
+            part = self.piece(
+                tensor, self.shard_at(zs, 1, 1), kind - 8, 1 - par if there else par)
+            dev = self.dev(z=self.z + 1 - 2 * par)
+        row = (tensor * 4 + zs) * 10 + kind
         return self.copy(part, part, self.gsend.at[row], self.grecv.at[row], dev)
 
-    def start(self, tensor, zs, kind):
-        self.gcopy(tensor, zs, kind).start()
-
-    def arrive(self, tensor, zs, kind):
-        if kind < 2:
-            part = self.piece(tensor, self.shard_at(zs, fx=1 - kind, fy=kind))
-        elif kind < 4:
-            part = self.piece(tensor, self.shard_at(zs, 1, 1), kind - 2)
-        else:
-            fx, fy = ((0, 0), (1, 0), (0, 1), (1, 1))[kind - 4]
-            part = self.piece(tensor, self.shard_at(zs, fx, fy, 1))
-        row = (tensor * 4 + zs) * 8 + kind
-        self.copy(
-            part, part, self.gsend.at[row], self.grecv.at[row], self.dev(fc=1)).wait_recv()
+    def start(self, tensor, zs, *kinds):
+        for kind in kinds:
+            self.gcopy(tensor, zs, kind).start()
+
+    def arrive(self, tensor, zs, *kinds):
+        for kind in kinds:
+            self.gcopy(tensor, zs, kind, True).wait_recv()
+
+    def zcopy(self, tensor, k):
+        part = self.piece(tensor, self.shard)
+        row = tensor * 3 + k - 1
+        return self.copy(
+            part, part, self.zsend.at[row], self.zrecv.at[row], self.dev(z=(self.z + k) % 4))
 
     def z_arrive(self, tensor, k):
         part = self.piece(tensor, self.shard_at((self.z + 4 - k) % 4))
@@ -157,63 +176,77 @@
         self.copy(
             part, part, self.zsend.at[row], self.zrecv.at[row], self.dev(fc=1)).wait_recv()
 
-    def zcopy(self, tensor, k):
-        part = self.piece(tensor, self.shard)
-        row = tensor * 3 + k - 1
-        return self.copy(
-            part, part, self.zsend.at[row], self.zrecv.at[row], self.dev(z=(self.z + k) % 4)
-        )
-
-    def z_sends(self, tensor):
-        for k in (1, 3, 2):
-            self.zcopy(tensor, k).start()
-
-    def p1(self, tensor, zs, k=None):
-        if k is None:
-            for kk in (1, 2, 3):
-                @pl.when((self.z + 4 - kk) % 4 == zs)
-                def _(kk=kk):
-                    self.z_arrive(tensor, kk)
-        elif k:
+    def own_z(self, tensor, k):
+        self.zcopy(tensor, k).start()
+
+    def own_xy(self, tensor):
+        self.start(tensor, self.z, 0, 1, 4)
+
+    def p1(self, tensor, k):
+        if tensor < 2:
             self.z_arrive(tensor, k)
-        for kind in (0, 1, 4):
-            self.start(tensor, zs, kind)
-
-    def p2(self, tensor, zs):
+            self.start(tensor, self.plane(tensor, k), 0, 1, 4)
+            return
+        for up in (1, 2, 3):
+            @pl.when((self.z + 4 - up) % 4 == k)
+            def _(up=up):
+                self.z_arrive(tensor, up)
+                self.start(tensor, k, 0, 1, 4)
+
+        @pl.when(self.z == k)
+        def _():
+            self.start(tensor, k, 0, 1, 4)
+
+    def p2x(self, tensor, k):
+        zs = self.plane(tensor, k)
         self.arrive(tensor, zs, 0)
-        self.start(tensor, zs, 2)
-        self.start(tensor, zs, 5)
+        self.start(tensor, zs, 2, 5)
+
+    def p2y(self, tensor, k):
+        zs = self.plane(tensor, k)
         self.arrive(tensor, zs, 1)
-        self.start(tensor, zs, 3)
-        self.start(tensor, zs, 6)
-
-    def p3(self, tensor, zs):
-        self.arrive(tensor, zs, 2)
-        self.arrive(tensor, zs, 3)
-        self.start(tensor, zs, 7)
-
-    def p4(self, tensor, zs):
-        for kind in (4, 5, 6, 7):
-            self.arrive(tensor, zs, kind)
-
-    def sends_done(self, tensor):
-        for zs in range(4):
-            self.plane_sent(tensor, zs)
+        self.start(tensor, zs, 3, 6)
+
+    def p3(self, tensor, k, half):
+        zs = self.plane(tensor, k)
+        self.arrive(tensor, zs, 2 + half)
+        if SHARED[tensor]:
+            self.start(tensor, zs, 8 + half)
+        elif half:
+            self.start(tensor, zs, 7)
+
+    def p4(self, tensor, k):
+        if SHARED[tensor]:
+            zs = self.plane(tensor, k)
+            self.arrive(tensor, zs, 8, 9)
+            self.start(tensor, zs, 7)
+
+    def p5(self, tensor, k):
+        self.arrive(tensor, self.plane(tensor, k), 4, 5, 6, 7)
+
+    def plane_sent(self, tensor, k):
+        for kind in range(10 if SHARED[tensor] else 8):
+            self.gcopy(tensor, self.plane(tensor, k), kind).wait_send()
+
+    def z_sent(self, tensor):
         for k in (1, 2, 3):
             self.zcopy(tensor, k).wait_send()
 
-    def plane_sent(self, tensor, zs):
-        for kind in range(8):
-            self.gcopy(tensor, zs, kind).wait_send()
-
-    def own_rows(self):
-        for src, dst in ((self.sh_s, self.ws), (self.sh_c, self.wc)):
-            self.flat[0:576, :] = src[...].astype(F32)
-            row = al(self.shard * AR, 16)
-            for t in range(6):
-                dst[pl.ds(row, AR), 128 * t:128 * t + 128] = self.flat[
-                    pl.ds(t, AR, stride=6), :].astype(BF)
-        self.own_ff()
+    def credit(self, which):
+        if which == 0:
+            self.z_sent(2)
+        for k in ((0,), (1, 2, 3))[which]:
+            self.plane_sent(2, k)
+        pl.semaphore_signal(
+            self.free.at[which], inc=1, device_id=self.dev(fc=1), device_id_type=MESH)
+
+    def own_square(self, tensor):
+        src, dst = ((self.sh_s, self.ws), (self.sh_c, self.wc))[tensor]
+        self.flat[0:576, :] = src[...].astype(F32)
+        row = al(self.shard * AR, 16)
+        for t in range(6):
+            dst[pl.ds(row, AR), 128 * t:128 * t + 128] = self.flat[
+                pl.ds(t, AR, stride=6), :].astype(BF)
 
     def own_ff(self):
         self.flat[0:1152, :] = self.sh_f[...].astype(F32)
@@ -301,7 +334,7 @@
         for h in range(H):
             row = jnp.zeros((1, 128), F32)
             for b in range(NB):
-                row = jnp.where(bucket == b, self.table[b, h], row)
+                row = jnp.where(bucket == b, self.table[h, b], row)
             full = jnp.broadcast_to(row, (128, 128))
             self.ps[128 * h:128 * h + 128, :] = pltpu.roll(
                 full, 0, 1, stride=1, stride_axis=0)
@@ -344,7 +377,8 @@
         self.add_product(self.mix[...], self.ws, 3 * D, self.x_in, self.r1)
         self.n2[...] = rms(self.r1[...], self.gains[1:2, :]).astype(BF)
 
-    def cross_kv(self, m, out):
+    def cross_kv(self, m):
+        out = (self.ck, self.cv)[m - 1]
         for i in range(4):
             for p in range(3):
                 out[128 * i:128 * i + 128, 256 * p:256 * p + 256] = nn(
@@ -359,8 +393,9 @@
         e = jnp.exp(s - jnp.max(s, axis=-1, keepdims=True))
         return e / jnp.sum(e, axis=-1, keepdims=True)
 
-    def cross_forward(self):
-        self.project(self.n2[...], self.wc, 0, self.cq)
+    def cross_forward(self, part):
+        if part == 0:
+            self.project(self.n2[...], self.wc, 0, self.cq)
 
         def pair(p, _):
             cols = pl.ds(al(p * 128, 128), 128)
@@ -368,28 +403,39 @@
             self.cmix[:, cols] = self.unstack(nn(prob.astype(BF), self.cv[:, cols])).astype(BF)
             return 0
 
-        lax.fori_loop(0, PAIRS, pair, 0)
-        self.add_product(self.cmix[...], self.wc, 3 * D, self.r1, self.r2)
-        self.n3[...] = rms(self.r2[...], self.gains[2:3, :]).astype(BF)
-
-    def ff_forward(self):
+        lax.fori_loop(2 * part, 2 * part + 2, pair, 0)
+        if part == 2:
+            self.add_product(self.cmix[...], self.wc, 3 * D, self.r1, self.r2)
+            self.n3[...] = rms(self.r2[...], self.gains[2:3, :]).astype(BF)
+
+    def ff_gate(self):
         n3 = self.n3[...]
         c0 = float(np.sqrt(2.0 / np.pi))
 
         def chunk(i, _):
             cols = pl.ds(al(i * 256, 256), 256)
             a = nn(n3, self.wgu[0:D, cols])
-            up = nn(n3, self.wgu[D:2 * D, cols])
             sq = a * a
             t = jnp.tanh(c0 * (a + 0.044715 * a * sq))
-            gelu = 0.5 * a * (1.0 + t)
-            slope = 0.5 * (1.0 + t) + 0.5 * a * (1.0 - t * t) * (c0 * (1.0 + 0.134145 * sq))
-            self.ga[:, cols] = gelu
-            self.ub[:, cols] = up * slope
-            self.hid[:, cols] = (gelu * up).astype(BF)
+            self.ga[:, cols] = 0.5 * a * (1.0 + t)
+            self.ub[:, cols] = 0.5 * (1.0 + t) + 0.5 * a * (1.0 - t * t) * (
+                c0 * (1.0 + 0.134145 * sq))
             return 0
 
         lax.fori_loop(0, FF // 256, chunk, 0)
+
+    def ff_up(self):
+        n3 = self.n3[...]
+
+        def chunk(i, _):
+            cols = pl.ds(al(i * 256, 256), 256)
+            up = nn(n3, self.wgu[D:2 * D, cols])
+            self.ub[:, cols] = up * self.ub[:, cols]
+            self.hid[:, cols] = (self.ga[:, cols] * up).astype(BF)
+            return 0
+
+        lax.fori_loop(0, FF // 256, chunk, 0)
+        self.hidt[...] = self.hid[...].T
 
     def out_rows(self):
         hid = self.hid[...]
@@ -397,7 +443,7 @@
             cols = slice(256 * p, 256 * p + 256)
             self.block[:, cols] = (self.r2[:, cols] + nn(hid, self.wd[:, cols])).astype(BF)
 
-    def d_hidden(self):
+    def d_hidden(self, part):
         g = self.g[...]
 
         def chunk(i, _):
@@ -408,20 +454,19 @@
             self.du[:, cols] = (dh * self.ga[:, cols]).astype(BF)
             return 0
 
-        lax.fori_loop(0, FF // 256, chunk, 0)
+        lax.fori_loop(4 * part, 4 * part + 4, chunk, 0)
 
     def place(self, g):
         own = OWN[g]
         out = OWN_ROWS + (g % 2) * STAGE
         return own + self.c * (out - own), out + self.c * (own - out)
 
-    def grad_tall(self, g, ch, i):
+    def grad_tall(self, g, i):
         b0, b1 = self.place(g)
-        gout = self.g[...]
-        first = 384 * ch - 4096
-
         for p in range(3):
-            both = nn(self.hidt[pl.ds(al(first, 16), 384), :], gout[:, 256 * p:256 * p + 256])
+            both = nn(
+                self.hidt[pl.ds(al(512 + 384 * i, 16), 384), :],
+                self.g[:, 256 * p:256 * p + 256])
             self.gb[pl.ds(al(b0 + FU * i + 192 * p, 16), 192), :] = both[0:192].astype(BF)
             self.gb[pl.ds(al(b1 + FU * i + 192 * p, 16), 192), :] = both[192:].astype(BF)
 
@@ -454,12 +499,7 @@
 
     def grad_ff(self, g):
         zb = GROUPS[g][1]
-        if zb == 3:
-            def step(i, _):
-                self.grad_tall(g, 12 + i, i)
-                return 0
-            lax.fori_loop(0, 4, step, 0)
-        elif zb == 2:
+        if zb == 2:
             b0, b1 = self.place(g)
             for i in range(3):
                 self.grad_wide(g, 8 + i, i)
@@ -470,18 +510,25 @@
             for i in range(4):
                 self.grad_wide(g, 4 * zb + i, i)
 
-    def grad_square(self, g, leftt, right):
+    def grad_square(self, g, i):
+        t, zb = GROUPS[g]
+        left = self.memt if t == 1 and zb in (1, 2) else self.tt
+        right = ((self.q, self.k, self.v, self.drb), (self.cq, self.ck, self.cv, self.drb))[t][zb]
         b0, b1 = self.place(g)
-
-        def step(i, _):
-            rows = leftt[pl.ds(al(192 * i, 16), 192), :]
-            for p in range(3):
-                both = nn(rows, right[:, 256 * p:256 * p + 256])
-                self.gb[pl.ds(al(b0 + AU * i + 96 * p, 16), 96), :] = both[0:96].astype(BF)
-                self.gb[pl.ds(al(b1 + AU * i + 96 * p, 16), 96), :] = both[96:].astype(BF)
-            return 0
-
-        lax.fori_loop(0, 4, step, 0)
+        rows = left[pl.ds(al(192 * i, 16), 192), :]
+        for p in range(3):
+            both = nn(rows, right[:, 256 * p:256 * p + 256])
+            self.gb[pl.ds(al(b0 + AU * i + 96 * p, 16), 96), :] = both[0:96].astype(BF)
+            self.gb[pl.ds(al(b1 + AU * i + 96 * p, 16), 96), :] = both[96:].astype(BF)
+
+    def turn(self, g):
+        if g == 1:
+            self.n3t[...] = self.n3[...].T
+        elif g == 5:
+            self.memt[...] = self.mem[...].T
+        elif g in (4, 7, 8, 9):
+            left = {4: self.cmix, 7: self.n2, 8: self.mix, 9: self.n1}[g]
+            self.tt[...] = left[...].T
 
     def back_product(self, terms, out):
         for p in range(3):
@@ -494,12 +541,12 @@
     def norm_three_back(self):
         self.back_product(((self.dg, self.wgu, 0, FF), (self.du, self.wgu, D, FF)), self.dz)
         dv, dg = rms_back(self.r2[...], self.gains[2:3, :], self.dz[...])
-        self.redg[2:3, :] = dg
+        self.redg[0, 2:3, :] = dg
         self.dr[...] = self.g[...].astype(F32) + dv
         self.drb[...] = self.dr[...].astype(BF)
 
-    def cross_back(self):
-        for p in range(3):
+    def cross_back(self, part):
+        for p in range(3) if part == 0 else ():
             self.dm[:, 256 * p:256 * p + 256] = nt(
                 self.drb[...], self.wc[3 * D + 256 * p:3 * D + 256 * p + 256, :]).astype(BF)
 
@@ -516,27 +563,26 @@
             self.ck[:, cols] = tn(ds, qs).astype(BF)
             return 0
 
-        lax.fori_loop(0, PAIRS, pair, 0)
-
-    def memory_rows(self):
-        for i in range(4):
-            rows = slice(128 * i, 128 * i + 128)
-            for p in range(3):
-                wrow = 256 * p
-                self.mgrad[rows, 256 * p:256 * p + 256] = (
-                    nt(self.ck[rows, :], self.wc[D + wrow:D + wrow + 256, :])
-                    + nt(self.cv[rows, :], self.wc[2 * D + wrow:2 * D + wrow + 256, :])
-                ).astype(BF)
+        lax.fori_loop(2 * part, 2 * part + 2, pair, 0)
+
+    def memory_rows(self, i):
+        rows = slice(128 * i, 128 * i + 128)
+        for p in range(3):
+            wrow = 256 * p
+            self.mgrad[rows, 256 * p:256 * p + 256] = (
+                nt(self.ck[rows, :], self.wc[D + wrow:D + wrow + 256, :])
+                + nt(self.cv[rows, :], self.wc[2 * D + wrow:2 * D + wrow + 256, :])
+            ).astype(BF)
 
     def norm_two_back(self):
         self.back_product(((self.cq, self.wc, 0, D),), self.dz)
         dv, dg = rms_back(self.r1[...], self.gains[1:2, :], self.dz[...])
-        self.redg[1:2, :] = dg
+        self.redg[0, 1:2, :] = dg
         self.dr[...] = self.dr[...] + dv
         self.drb[...] = self.dr[...].astype(BF)
 
-    def self_back(self):
-        for p in range(3):
+    def self_back(self, part):
+        for p in range(3) if part == 0 else ():
             self.dm[:, 256 * p:256 * p + 256] = nt(
                 self.drb[...], self.ws[3 * D + 256 * p:3 * D + 256 * p + 256, :]).astype(BF)
 
@@ -554,14 +600,14 @@
             self.k[:, cols] = tn(ds, qs).astype(BF)
             return 0
 
-        lax.fori_loop(0, PAIRS, pair, 0)
+        lax.fori_loop(3 * part, 3 * part + 3, pair, 0)
 
     def norm_one_back(self):
         self.back_product(
             ((self.q, self.ws, 0, D), (self.k, self.ws, D, D), (self.v, self.ws, 2 * D, D)),
             self.dz)
         dv, dg = rms_back(self.x_in[...].astype(F32), self.gains[0:1, :], self.dz[...])
-        self.redg[0:1, :] = dg
+        self.redg[0, 0:1, :] = dg
         self.xgrad[...] = (self.dr[...] + dv).astype(BF)
 
     def table_back(self):
@@ -578,13 +624,9 @@
         lane = lax.broadcasted_iota(jnp.int32, (NB, 128), 1)
         hot = jnp.where(
             bucket_of((lane + 1) % 128) == lax.broadcasted_iota(jnp.int32, (NB, 128), 0), 1.0, 0.0)
-        self.redt[:, 0:16] = lax.dot_general(
-            hot, self.diag[...], (((1,), (1,)), ((), ())),
+        self.redt[0, :, 0:NB] = lax.dot_general(
+            self.diag[...], hot, (((1,), (1,)), ((), ())),
             precision=lax.Precision.HIGHEST, preferred_element_type=F32)
-
-    def ropy(self, src, dst, g, kind, device):
-        row = g * 8 + kind
-        return self.copy(src, dst, self.rsend.at[row], self.rrecv.at[row], device)
 
     def own(self, g, chip, half=None):
         unit = UNIT[g]
@@ -603,70 +645,127 @@
             start = start + half * rows
         return pl.ds(start, rows)
 
+    def lanes(self, g, mine):
+        if not PAIR[g]:
+            return slice(None)
+        par = self.z % 2
+        return pl.ds(al((par if mine else 1 - par) * 128, 128), 128)
+
     def scopy(self, g, kind):
         gb, lb = self.gb, self.lb
-        if kind == 0:
-            rows = 4 * UNIT[g]
-            return self.ropy(
-                gb.at[pl.ds(OWN_ROWS + (g % 2) * STAGE, rows), :],
-                self.wf.at[pl.ds(OWN[g], rows), :], g, 0, self.dev(fc=1))
-        src, dst, dev = {
-            1: (self.own(g, self.chip(1, 1), 0), self.land(g, 0), self.dev(fx=1)),
-            2: (self.own(g, self.chip(1, 1), 1), self.land(g, 1), self.dev(fy=1)),
-            3: (self.own(g, self.chip(1, 0), 0), self.land(g, 2, 0), self.dev(fx=1)),
-            4: (self.own(g, self.chip(1, 0), 1), self.land(g, 2, 1), self.dev(fx=1)),
-            5: (self.own(g, self.chip(0, 1), 1), self.land(g, 3, 1), self.dev(fy=1)),
-            6: (self.own(g, self.chip(0, 1), 0), self.land(g, 3, 0), self.dev(fy=1)),
+        row = g * 15 + kind
+        sems = self.rsend.at[row], self.rrecv.at[row]
+        if kind in SIB:
+            unit = UNIT[g]
+            at = self.chip(*ROLES[SIB.index(kind)]) * unit
+            return self.copy(
+                gb.at[pl.ds(al(OWN_ROWS + (g % 2) * STAGE + at, 16), unit), :],
+                self.wf.at[pl.ds(al(OWN[g] + at, 16), unit), :], *sems, self.dev(fc=1))
+        spot, half, lanes, where, dev = {
+            1: ((1, 1), 0, True, 0, (1, 0)),
+            2: ((1, 1), 1, True, 1, (0, 1)),
+            3: ((1, 0), 0, None, 2, (1, 0)),
+            4: ((1, 0), 1, True, 2, (1, 0)),
+            5: ((1, 0), 1, False, 2, (1, 0)),
+            6: ((0, 1), 1, None, 3, (0, 1)),
+            7: ((0, 1), 0, True, 3, (0, 1)),
+            8: ((0, 1), 0, False, 3, (0, 1)),
+            9: ((1, 1), 0, False, 0, None),
+            10: ((1, 1), 1, False, 1, None),
         }[kind]
-        return self.ropy(gb.at[src, :], lb.at[dst, :], g, kind, dev)
-
-    def to_owner(self, g):
+        src = self.own(g, self.chip(*spot), half)
+        dst = self.land(g, where, half if where > 1 else None)
+        lanes = slice(None) if lanes is None else self.lanes(g, lanes)
+        put = self.lanes(g, True) if dev is None else lanes
+        dev = self.dev(z=self.z + 1 - 2 * (self.z % 2)) if dev is None else self.dev(None, *dev)
+        return self.copy(gb.at[src, lanes], lb.at[dst, put], *sems, dev)
+
+    def came(self, g, *kinds):
+        for kind in kinds:
+            if kind in (9, 10):
+                part = self.lb.at[self.land(g, kind - 9), self.lanes(g, False)]
+                row = g * 15 + kind
+                self.copy(
+                    part, part, self.rsend.at[row], self.rrecv.at[row],
+                    self.dev(fc=1)).wait_recv()
+            else:
+                self.scopy(g, kind).wait_recv()
+
+    def go(self, g, *kinds):
+        for kind in kinds:
+            self.scopy(g, kind).start()
+
+    def to_owner(self, g, slot=None):
         t, zb = GROUPS[g]
         unit = UNIT[g]
-        slot = (self.z + 3 - zb) % 4
+        if slot is None:
+            slot = (self.z + 3 - zb) % 4
         return self.copy(
             self.gb.at[self.own(g, self.chip()), :],
             self.zb.at[pl.ds(al(ZBASE[t] + slot * unit, 16), unit), :],
-            self.rsend.at[g * 8 + 7], self.orecv.at[t * 3 + slot], self.dev(z=zb))
-
-    def from_plane(self, g, slot):
-        t, zb = GROUPS[g]
-        unit = UNIT[g]
-        return self.copy(
-            self.gb.at[self.own(g, self.chip()), :],
-            self.zb.at[pl.ds(ZBASE[t] + slot * unit, unit), :],
-            self.rsend.at[g * 8 + 7], self.orecv.at[t * 3 + slot], self.dev(z=zb))
-
-    def rs0(self, g):
-        self.scopy(g, 0).start()
-
-    def stage_free(self, g):
+            self.rsend.at[g * 15 + 11], self.orecv.at[t * 3 + slot], self.dev(z=zb))
+
+    def ready(self, g):
+        self.turn(g)
         if g >= 2:
-            self.scopy(g - 2, 0).wait_send()
-
-    def accumulate(self, dst, src_ref, src):
-        self.gb[dst, :] = (
-            self.gb[dst, :].astype(F32) + src_ref[src, :].astype(F32)).astype(BF)
-
-    def rs1(self, g):
-        self.scopy(g, 0).wait_recv()
-        for fx, fy, kinds in ((1, 1, (1, 2)), (1, 0, (3,)), (0, 1, (5,)), (0, 0, ())):
-            rows = self.own(g, self.chip(fx, fy))
-            self.accumulate(rows, self.wf, rows)
-            for kind in kinds:
-                self.scopy(g, kind).start()
-
-    def rs2(self, g):
-        self.scopy(g, 1).wait_recv()
-        self.accumulate(self.own(g, self.chip(0, 1), 0), self.lb, self.land(g, 0))
-        self.scopy(g, 6).start()
-        self.scopy(g, 2).wait_recv()
-        self.accumulate(self.own(g, self.chip(1, 0), 1), self.lb, self.land(g, 1))
-        self.scopy(g, 4).start()
-
-    def rs3(self, g):
-        for kind in (3, 5, 4, 6):
-            self.scopy(g, kind).wait_recv()
+            for role in range(4):
+                self.scopy(g - 2, SIB[role]).wait_send()
+
+    def allowed(self, g):
+        if g in (0, 2):
+            pl.semaphore_wait(self.free.at[g // 2], 1)
+
+    def part(self, g, i):
+        (self.grad_tall if g == 0 else self.grad_square)(g, i)
+
+    def grad(self, g):
+        self.ready(g)
+        if 0 < g < 4:
+            self.grad_ff(g)
+        else:
+            def step(i, _):
+                self.part(g, i)
+                return 0
+            lax.fori_loop(0, 4, step, 0)
+        self.allowed(g)
+        self.go(g, *SIB)
+
+    def grad_role(self, g, role):
+        if role == 0:
+            self.ready(g)
+        self.part(g, self.chip(*ROLES[role]))
+        if role == 0:
+            self.allowed(g)
+        self.go(g, SIB[role])
+
+    def accumulate(self, dst, lanes, src_ref, src, from_lanes):
+        self.gb[dst, lanes] = (
+            self.gb[dst, lanes].astype(F32) + src_ref[src, from_lanes].astype(F32)).astype(BF)
+
+    def rs1(self, g, role):
+        self.came(g, SIB[role])
+        rows = self.own(g, self.chip(*ROLES[role]))
+        self.accumulate(rows, slice(None), self.wf, rows, slice(None))
+        self.go(g, *(((9, 10), (3, 5), (6, 8), ()) if PAIR[g] else ((1, 2), (3,), (6,), ()))[role])
+
+    def rs2(self, g, half):
+        if PAIR[g]:
+            self.came(g, 9 + half)
+            self.accumulate(
+                self.own(g, self.chip(1, 1), half), self.lanes(g, True),
+                self.lb, self.land(g, half), self.lanes(g, False))
+            self.go(g, 1 + half)
+
+    def rs3(self, g, half):
+        kind, spot, late = ((1, (0, 1), 7), (2, (1, 0), 4))[half]
+        self.came(g, kind)
+        self.accumulate(
+            self.own(g, self.chip(*spot), half), self.lanes(g, True),
+            self.lb, self.land(g, kind - 1), self.lanes(g, True))
+        self.go(g, late)
+
+    def rs4(self, g):
+        self.came(g, *((3, 5, 6, 8, 4, 7) if PAIR[g] else (3, 6, 4, 7)))
         rows = self.own(g, self.chip())
         self.gb[rows, :] = (
             self.gb[rows, :].astype(F32) + self.lb[self.land(g, 2), :].astype(F32)
@@ -676,15 +775,14 @@
         def _():
             self.to_owner(g).start()
 
-    def rs4(self, g):
+    def rs5(self, g):
         t, zb = GROUPS[g]
         unit = UNIT[g]
 
         @pl.when(self.z == zb)
         def _():
             for slot in range(3):
-                self.from_plane(g, slot).wait_recv()
-            rows = self.own(g, self.chip())
+                self.to_owner(g, slot).wait_recv()
 
             def total(start, size, lanes):
                 at = pl.ds(al(OWN[g] + self.chip() * unit + start, 16), size)
@@ -694,7 +792,6 @@
                         pl.ds(ZBASE[t] + slot * unit + start, size), lanes].astype(F32)
                 return value
 
-            del rows
             if t < 2:
                 out = (self.gs, self.gc)[t]
                 for k in range(6):
@@ -734,8 +831,9 @@
                     tall(0, 192, 0)
 
     def group_sent(self, g):
-        for kind in range(1, 7):
-            self.scopy(g, kind).wait_send()
+        for kind in range(1, 11):
+            if PAIR[g] or kind not in (5, 8, 9, 10):
+                self.scopy(g, kind).wait_send()
 
         @pl.when(self.z != GROUPS[g][1])
         def _():
@@ -762,6 +860,80 @@
         self.redt[step + 1] = self.redt[step] + self.landt[step]
 
 
+    def finish(self):
+        for tensor in (0, 1):
+            self.z_sent(tensor)
+            for k in range(4):
+                self.plane_sent(tensor, k)
+        for g in range(12):
+            self.group_sent(g)
+        for g in (10, 11):
+            for role in range(4):
+                self.scopy(g, SIB[role]).wait_send()
+        self.ggain[...] = self.redga[5, 0:3, :]
+        self.gtable[...] = self.redta[5, 0:H, 0:NB]
+        for step in range(5):
+            for which in range(2):
+                self.small(step, which).wait_send()
+
+
+K = Layer
+SCHEDULE = (
+    (K.own_z, 0, 1), (K.own_xy, 0), (K.own_square, 1), (K.own_z, 1, 1), (K.own_xy, 1),
+    (K.p1, 0, 1), (K.own_z, 0, 3), (K.p2x, 0, 0), (K.own_z, 0, 2), (K.own_z, 1, 2),
+    (K.p1, 1, 1), (K.p2x, 1, 0), (K.p2y, 1, 0), (K.p2y, 0, 0), (K.p2x, 0, 1), (K.p2y, 0, 1),
+    (K.own_z, 1, 3), (K.p2y, 1, 1), (K.p1, 0, 3), (K.p3, 1, 0, 0), (K.p3, 0, 0, 0),
+    (K.p1, 0, 2), (K.p3, 0, 0, 1), (K.own_ff,), (K.own_z, 2, 3), (K.own_z, 2, 1), (K.p2y, 0, 3),
+    (K.p3, 0, 1, 0), (K.p2x, 0, 3), (K.p3, 0, 1, 1), (K.p2x, 1, 1), (K.p2y, 0, 2), (K.p4, 0, 0),
+    (K.p1, 1, 3), (K.p3, 1, 0, 1), (K.p3, 0, 3, 0), (K.p4, 1, 0), (K.p1, 1, 2), (K.p3, 0, 3, 1),
+    (K.p2y, 1, 3), (K.p3, 1, 1, 0), (K.bias,), (K.p2x, 1, 3), (K.p2x, 0, 2), (K.p2y, 1, 2),
+    (K.p3, 1, 1, 1), (K.p3, 1, 3, 0), (K.p3, 1, 3, 1), (K.p5, 1, 0), (K.p2x, 1, 2),
+    (K.own_z, 2, 2), (K.p4, 1, 1), (K.p3, 0, 2, 0), (K.p1, 2, 1), (K.p3, 0, 2, 1), (K.p4, 1, 3),
+    (K.p3, 1, 2, 0), (K.p3, 1, 2, 1), (K.p4, 1, 2), (K.p5, 1, 2), (K.p5, 1, 3), (K.p1, 2, 0),
+    (K.p2y, 2, 1), (K.p4, 0, 2), (K.p5, 1, 1), (K.cross_kv, 2), (K.p1, 2, 2), (K.p2x, 2, 0),
+    (K.cross_kv, 1), (K.p2x, 2, 1), (K.p5, 0, 2), (K.p4, 0, 1), (K.p2y, 2, 0), (K.p4, 0, 3),
+    (K.p5, 0, 3), (K.p5, 0, 0), (K.p5, 0, 1), (K.self_forward,), (K.cross_forward, 0),
+    (K.p3, 2, 0, 0), (K.p2y, 2, 2), (K.p2x, 2, 2), (K.p3, 2, 1, 0), (K.p3, 2, 0, 1),
+    (K.p1, 2, 3), (K.p3, 2, 1, 1), (K.cross_forward, 1), (K.p3, 2, 2, 0), (K.cross_forward, 2),
+    (K.p4, 2, 0), (K.p3, 2, 2, 1), (K.p4, 2, 1), (K.p5, 2, 0), (K.build_plane, 0),
+    (K.p2x, 2, 3), (K.p2y, 2, 3), (K.credit, 0), (K.p5, 2, 1), (K.build_plane, 1), (K.p4, 2, 2),
+    (K.ff_gate,), (K.p3, 2, 3, 0), (K.p5, 2, 2), (K.build_plane, 2), (K.p3, 2, 3, 1),
+    (K.ff_up,), (K.grad_role, 0, 0), (K.grad_role, 0, 1), (K.grad_role, 0, 2), (K.rs1, 0, 0),
+    (K.p4, 2, 3), (K.rs1, 0, 1), (K.grad_role, 0, 3), (K.rs1, 0, 2), (K.p5, 2, 3),
+    (K.build_plane, 3), (K.d_hidden, 0), (K.d_hidden, 1), (K.rs2, 0, 0), (K.rs2, 0, 1),
+    (K.grad, 1), (K.rs1, 1, 0), (K.credit, 1), (K.rs1, 1, 1), (K.rs3, 0, 1), (K.rs3, 0, 0),
+    (K.rs1, 1, 2), (K.grad, 2), (K.norm_three_back,), (K.rs1, 2, 0), (K.grad, 3), (K.rs2, 1, 0),
+    (K.rs1, 2, 2), (K.rs2, 2, 0), (K.rs1, 2, 1), (K.grad_role, 4, 0), (K.grad_role, 4, 1),
+    (K.grad_role, 4, 2), (K.rs1, 3, 0), (K.rs1, 0, 3), (K.rs2, 3, 1), (K.grad_role, 4, 3),
+    (K.rs1, 2, 3), (K.rs2, 2, 1), (K.rs1, 4, 0), (K.rs3, 2, 0), (K.rs2, 4, 1),
+    (K.cross_back, 0), (K.rs1, 3, 2), (K.rs2, 1, 1), (K.cross_back, 1), (K.rs3, 2, 1),
+    (K.cross_back, 2), (K.rs2, 3, 0), (K.rs1, 4, 1), (K.rs3, 4, 1), (K.rs4, 0), (K.rs1, 3, 1),
+    (K.rs3, 3, 0), (K.grad, 5), (K.grad, 6), (K.rs3, 1, 0), (K.rs3, 3, 1), (K.rs4, 2),
+    (K.grad, 7), (K.rs1, 5, 0), (K.rs2, 5, 0), (K.norm_two_back,), (K.self_back, 0),
+    (K.rs1, 1, 3), (K.rs1, 7, 2), (K.rs1, 3, 3), (K.rs1, 5, 2), (K.rs3, 1, 1), (K.rs1, 4, 2),
+    (K.self_back, 1), (K.rs1, 6, 0), (K.grad, 8), (K.rs1, 5, 1), (K.norm_one_back,), (K.rs4, 1),
+    (K.grad_role, 9, 0), (K.rs4, 3), (K.rs1, 7, 0), (K.rs2, 7, 1), (K.table_back,),
+    (K.rs2, 4, 0), (K.small_start, 0), (K.rs1, 8, 0), (K.rs1, 7, 1), (K.rs1, 5, 3),
+    (K.rs3, 5, 0), (K.grad_role, 9, 1), (K.small_add, 0), (K.grad_role, 9, 2), (K.rs1, 8, 3),
+    (K.grad_role, 9, 3), (K.grad_role, 10, 0), (K.rs2, 6, 1), (K.grad_role, 10, 1),
+    (K.grad_role, 10, 2), (K.small_start, 1), (K.rs1, 6, 2), (K.rs1, 9, 0), (K.rs2, 7, 0),
+    (K.rs5, 2), (K.grad_role, 10, 3), (K.rs3, 7, 1), (K.rs1, 6, 1), (K.grad_role, 11, 0),
+    (K.rs5, 0), (K.rs2, 6, 0), (K.out_rows,), (K.memory_rows, 3), (K.small_add, 1),
+    (K.rs2, 5, 1), (K.rs1, 6, 3), (K.rs3, 5, 1), (K.small_start, 2), (K.rs2, 8, 1),
+    (K.rs1, 9, 1), (K.rs3, 7, 0), (K.rs1, 10, 0), (K.grad_role, 11, 1), (K.rs3, 4, 0),
+    (K.rs2, 9, 0), (K.rs2, 10, 1), (K.rs3, 6, 0), (K.rs1, 7, 3), (K.rs1, 9, 2), (K.rs1, 10, 2),
+    (K.memory_rows, 1), (K.small_add, 2), (K.rs3, 6, 1), (K.rs1, 10, 1), (K.memory_rows, 0),
+    (K.small_start, 3), (K.rs1, 11, 0), (K.rs2, 11, 0), (K.rs2, 8, 0), (K.rs4, 7),
+    (K.rs2, 10, 0), (K.rs4, 5), (K.grad_role, 11, 2), (K.rs2, 9, 1), (K.rs1, 4, 3),
+    (K.grad_role, 11, 3), (K.rs3, 10, 1), (K.rs3, 9, 1), (K.rs1, 10, 3), (K.rs1, 9, 3),
+    (K.memory_rows, 2), (K.rs3, 9, 0), (K.rs1, 11, 3), (K.rs4, 4), (K.small_add, 3),
+    (K.rs1, 8, 2), (K.rs3, 10, 0), (K.rs3, 8, 0), (K.rs1, 8, 1), (K.rs3, 8, 1), (K.rs5, 7),
+    (K.small_start, 4), (K.rs1, 11, 2), (K.rs2, 11, 1), (K.rs1, 11, 1), (K.rs4, 6), (K.rs5, 4),
+    (K.rs5, 3), (K.rs3, 11, 1), (K.rs4, 10), (K.rs3, 11, 0), (K.rs4, 9), (K.rs4, 11),
+    (K.rs4, 8), (K.rs5, 8), (K.rs5, 5), (K.rs5, 10), (K.small_add, 4), (K.rs5, 6), (K.rs5, 11),
+    (K.rs5, 1), (K.rs5, 9),
+)
+
 NAMES = (
     "x_in", "mem", "g", "dl", "ml", "sh_s", "sh_c", "sh_f", "gains", "table",
     "block", "xgrad", "mgrad", "gs", "gc", "gf", "ggain", "gtable",
@@ -774,199 +946,39 @@
 
 
 def kernel(*args):
-    refs = dict(zip(NAMES, args))
-    st = Layer(refs)
-    st.redg, st.redt = st.redga.at[0], st.redta.at[0]
-
+    st = Layer(dict(zip(NAMES, args)))
+    st.redg, st.redt = st.redga, st.redta
     barrier = pltpu.get_barrier_semaphore()
     others = [st.dev(fc=1), st.dev(fx=1), st.dev(fy=1)] + [
         st.dev(z=(st.z + k) % 4) for k in (1, 2, 3)]
     for other in others:
         pl.semaphore_signal(barrier, inc=1, device_id=other, device_id_type=MESH)
-    st.own_rows()
+    st.own_square(0)
     st.masks()
     pl.semaphore_wait(barrier, 6)
-
-    st.z_sends(0)
-    plane = [(st.z + 4 - k) % 4 for k in range(4)]
-    st.p1(0, plane[0], 0)
-    st.bias()
-    st.p1(0, plane[1], 1)
-    st.p2(0, plane[0])
-    st.p1(0, plane[3], 3)
-    st.p2(0, plane[1])
-    st.p3(0, plane[0])
-    st.p1(0, plane[2], 2)
-    st.z_sends(1)
-    st.p2(0, plane[3])
-    st.p3(0, plane[1])
-    st.p1(1, plane[0], 0)
-    st.p2(0, plane[2])
-    st.p3(0, plane[3])
-    st.p1(1, plane[1], 1)
-    st.p2(1, plane[0])
-    st.p3(0, plane[2])
-    for zs in range(4):
-        st.p4(0, plane[zs])
-    st.self_forward()
-    st.p1(1, plane[3], 3)
-    st.p2(1, plane[1])
-    st.p3(1, plane[0])
-    st.p1(1, plane[2], 2)
-    st.z_sends(2)
-    st.p2(1, plane[3])
-    st.p3(1, plane[1])
-    st.p1(2, 0)
-    st.p2(1, plane[2])
-    st.p3(1, plane[3])
-    st.p1(2, 1)
-    st.p2(2, 0)
-    st.p3(1, plane[2])
-    for zs in range(4):
-        st.p4(1, plane[zs])
-    st.cross_kv(1, st.ck)
-    st.cross_kv(2, st.cv)
-    st.p1(2, 2)
-    st.p2(2, 1)
-    st.p3(2, 0)
-    st.cross_forward()
-    st.p1(2, 3)
-    st.p2(2, 2)
-    st.p3(2, 1)
-    st.p4(2, 0)
-    st.build_plane(0)
-    st.p4(2, 1)
-    st.build_plane(1)
-    st.p2(2, 3)
-    st.p3(2, 2)
-    st.p4(2, 2)
-    st.build_plane(2)
-    st.ff_forward()
-    st.hidt[...] = st.hid[...].T
-    st.p3(2, 3)
-    st.p4(2, 3)
-    st.build_plane(3)
-    for t in range(3):
-        st.sends_done(t)
-    pl.semaphore_signal(st.free, inc=1, device_id=st.dev(fc=1), device_id_type=MESH)
-    st.grad_ff(0)
-    pl.semaphore_wait(st.free, 1)
-    st.rs0(0)
-    st.d_hidden()
-    st.n3t[...] = st.n3[...].T
-    st.grad_ff(1)
-    st.rs0(1)
-    st.rs1(0)
-    st.out_rows()
-    st.stage_free(2)
-    st.grad_ff(2)
-    st.rs0(2)
-    st.rs1(1)
-    st.rs2(0)
-    st.stage_free(3)
-    st.grad_ff(3)
-    st.rs0(3)
-    st.rs1(2)
-    st.rs2(1)
-    st.rs3(0)
-    st.norm_three_back()
-    st.tt[...] = st.cmix[...].T
-    st.stage_free(4)
-    st.grad_square(4, st.tt, st.drb)
-    st.rs0(4)
-    st.rs1(3)
-    st.rs2(2)
-    st.rs3(1)
-    st.rs4(0)
-    st.cross_back()
-    st.memt[...] = st.mem[...].T
-    st.stage_free(5)
-    st.grad_square(5, st.memt, st.cv)
-    st.rs0(5)
-    st.rs1(4)
-    st.rs2(3)
-    st.rs3(2)
-    st.rs4(1)
-    st.stage_free(6)
-    st.grad_square(6, st.memt, st.ck)
-    st.rs0(6)
-    st.rs1(5)
-    st.rs2(4)
-    st.rs3(3)
-    st.rs4(2)
-    st.tt[...] = st.n2[...].T
-    st.stage_free(7)
-    st.grad_square(7, st.tt, st.cq)
-    st.rs0(7)
-    st.norm_two_back()
-    st.rs1(6)
-    st.rs2(5)
-    st.rs3(4)
-    st.rs4(3)
-    st.tt[...] = st.mix[...].T
-    st.stage_free(8)
-    st.grad_square(8, st.tt, st.drb)
-    st.rs0(8)
-    st.self_back()
-    st.rs1(7)
-    st.rs2(6)
-    st.rs3(5)
-    st.rs4(4)
-    st.tt[...] = st.n1[...].T
-    st.stage_free(9)
-    st.grad_square(9, st.tt, st.v)
-    st.rs0(9)
-    st.rs1(8)
-    st.rs2(7)
-    st.rs3(6)
-    st.rs4(5)
-    st.stage_free(10)
-    st.grad_square(10, st.tt, st.k)
-    st.rs0(10)
-    st.norm_one_back()
-    st.table_back()
-    st.redg, st.redt = st.redga, st.redta
-    st.small_start(0)
-    st.rs1(9)
-    st.rs2(8)
-    st.rs3(7)
-    st.rs4(6)
-    st.small_add(0)
-    st.small_start(1)
-    st.stage_free(11)
-    st.grad_square(11, st.tt, st.q)
-    st.rs0(11)
-    st.rs1(10)
-    st.rs2(9)
-    st.rs3(8)
-    st.rs4(7)
-    st.small_add(1)
-    st.small_start(2)
-    st.rs1(11)
-    st.rs2(10)
-    st.rs3(9)
-    st.rs4(8)
-    st.memory_rows()
-    st.small_add(2)
-    st.small_start(3)
-    st.rs2(11)
-    st.rs3(10)
-    st.rs4(9)
-    st.small_add(3)
-    st.small_start(4)
-    st.rs3(11)
-    st.rs4(10)
-    st.small_add(4)
-    st.ggain[...] = st.redga[5, 0:3, :]
-    st.gtable[...] = st.redta[5, :, 0:H]
-    st.rs4(11)
-    for g in range(12):
-        st.group_sent(g)
-    st.scopy(10, 0).wait_send()
-    st.scopy(11, 0).wait_send()
-    for step in range(5):
-        for which in range(2):
-            st.small(step, which).wait_send()
+    for step, *numbers in SCHEDULE:
+        step(st, *numbers)
+    st.finish()
+
+
+def settle_kernel(count, *refs):
+    out = [pltpu.make_async_copy(refs[i], refs[count + i], refs[-1].at[i]) for i in range(count)]
+    for one in out:
+        one.start()
+    for one in out:
+        one.wait()
+
+
+def settle(arrays):
+    count = len(arrays)
+    return pl.pallas_call(
+        functools.partial(settle_kernel, count),
+        out_shape=tuple(jax.ShapeDtypeStruct(v.shape, v.dtype) for v in arrays),
+        in_specs=[pl.BlockSpec(memory_space=pltpu.VMEM)] * count,
+        out_specs=tuple([pl.BlockSpec(memory_space=pl.ANY)] * count),
+        scratch_shapes=[pltpu.SemaphoreType.DMA((count,))],
+        compiler_params=pltpu.CompilerParams(vmem_limit_bytes=67000000),
+    )(*arrays)
 
 
 def fused(inputs, memory, out_cotangent, dec_lengths, mem_lengths, self_params, cross_params,
@@ -986,7 +998,7 @@
         out_shape=(
             s((length, D), BF), s((length, D), BF), s((mem_len, D), BF),
             s((rows_s, 128), F32), s((rows_s, 128), F32), s((rows_f, 128), F32),
-            s((3, D), F32), s((NB, H), F32),
+            s((3, D), F32), s((H, NB), F32),
         ),
         in_specs=[vm, vm, vm, sm, sm, vm, vm, vm, vm, sm],
         out_specs=[vm] * 8,
@@ -1004,10 +1016,10 @@
             rowf, rowf, row, pltpu.VMEM((D, length), BF), pltpu.VMEM((D, mem_len), BF),
             pltpu.VMEM((H * length, length), F32),
             pltpu.VMEM((16, 128), F32),
-            pltpu.VMEM((6, 8, D), F32), pltpu.VMEM((6, NB, 128), F32),
-            pltpu.VMEM((5, 8, D), F32), pltpu.VMEM((5, NB, 128), F32),
-            dma((96,)), dma((96,)), dma((9,)), dma((9,)), dma((96,)), dma((96,)), dma((9,)),
-            dma((10,)), dma((10,)), pltpu.SemaphoreType.REGULAR,
+            pltpu.VMEM((6, 8, D), F32), pltpu.VMEM((6, 16, 128), F32),
+            pltpu.VMEM((5, 8, D), F32), pltpu.VMEM((5, 16, 128), F32),
+            dma((120,)), dma((120,)), dma((9,)), dma((9,)), dma((180,)), dma((180,)), dma((9,)),
+            dma((10,)), dma((10,)), pltpu.SemaphoreType.REGULAR((2,)),
         ],
         compiler_params=pltpu.CompilerParams(
             collective_id=0, has_side_effects=True, vmem_limit_bytes=67000000),
@@ -1017,12 +1029,13 @@
         inputs.reshape(length, width), memory.reshape(mem_len, width),
         out_cotangent.reshape(length, width), dec_lengths, mem_lengths,
         self_params.reshape(rows_s, 128), cross_params.reshape(rows_s, 128),
-        ff_params.reshape(rows_f, 128), gains, table,
-    )
+        ff_params.reshape(rows_f, 128), gains, table.T,
+    )
+    outs = settle(outs)
     return (
         outs[0].reshape(inputs.shape), outs[1].reshape(inputs.shape),
         outs[2].reshape(memory.shape), outs[3].reshape(-1), outs[4].reshape(-1),
-        outs[5].reshape(-1), outs[6], outs[7],
+        outs[5].reshape(-1), outs[6], outs[7].T,
     )
 
 

time: 234 us -> 198 us (0.85)
  Pallas kernels: 223 us -> 195 us
  local copies, waits for them, and re-layouts: 9.45 us -> 0 us
    pallas_call x1, Pallas kernels: 223 us -> 192 us  [fused(): pl.pallas_call(kernel, out_shape=(s((length, D), BF), s((length, D), BF),...]
    unnamed x21 -> x0, local copies, waits for them, and re-layouts: 9.45 us -> none
    pallas_call x0 -> x1, Pallas kernels: none -> 3.11 us  [settle(): pl.pallas_call(functools.partial(settle_kernel, count), out_shape=tuple((...]
where the time goes in v2:
time: 198 us; the launch traced here: 197 us
  Pallas kernels  195 us (98%)
  between operations  2.11 us (1%)
    pallas_call x1, Pallas kernels, fused(): pl.pallas_call(kernel, out_shape=(s((length, D), BF), s((length, D), BF),...  192 us

profile of v2, /device:TPU:0, one launch (start us, length us, event | category | flops | bytes accessed | tf_op | source)
XLA Modules:
  0.0 197.1 jit_solution(1114767034390461960)
XLA Ops:
  1.9 191.8 %shard_map.161 = (bf16[128,768]{1,0:T(8,128)(2,1)}, bf16[128,768]{1,0:T(8,128)(2,1)}, bf16[512,768]{1,0:T(8,128)(2,1)}, f32[576,128]{1,0:T(8,128)}, f32[576,128]...) custom-call(bf16[128,768]{1,0:T(8,128)(2,1)} %bitcast.20, bf16[512,768]{1,0:T(8,128)(2,1)} %bitcast.14, ...), custom_call_target="tpu_custom_call" | custom-call | flops 10000000000 | bytes 8000000 | tf_op jit(solution)/shard_map/pallas_call | solution.py:996
  193.8 3.1 %shard_map.162 = (bf16[128,768]{1,0:T(8,128)(2,1)}, bf16[128,768]{1,0:T(8,128)(2,1)}, bf16[512,768]{1,0:T(8,128)(2,1)}, f32[576,128]{1,0:T(8,128)}, f32[576,128]...) custom-call(bf16[128,768]{1,0:T(8,128)(2,1)} %get-tuple-element.24.refs_0_, ...), custom_call_target="tpu_custom_call" | custom-call | tf_op jit(solution)/shard_map/pallas_call | solution.py:974

commit v3 on v2

--- a/solution.py
+++ b/solution.py
@@ -28,8 +28,8 @@
     (1, 3), (1, 2), (1, 1), (1, 0),
     (0, 3), (0, 0), (0, 2), (0, 1),
 )
-PAIR = (True,) * 2 + (False,) * 10
-SHARED = (False, False, True)
+PAIR = (True,) * 4 + (False,) * 8
+SHARED = (True, True, True)
 UNIT = tuple(FU if t == 2 else AU for t, _ in GROUPS)
 OWN = tuple(4 * sum(UNIT[:g]) for g in range(12))
 OWN_ROWS = 4 * sum(UNIT)
@@ -130,7 +130,10 @@
         return ref.at[start, pl.ds(al(par * width, 128), width)]
 
     def plane(self, tensor, k):
-        return k if tensor == 2 else (self.z + 4 - k) % 4
+        if tensor == 2:
+            return k
+        far = self.z // 2
+        return (self.z, self.z + 1 - 2 * (self.z % 2), 2 - far, 3 - 3 * far)[k]
 
     def gcopy(self, tensor, zs, kind, there=False):
         par = self.z % 2
@@ -164,38 +167,44 @@
         for kind in kinds:
             self.gcopy(tensor, zs, kind, True).wait_recv()
 
-    def zcopy(self, tensor, k):
-        part = self.piece(tensor, self.shard)
-        row = tensor * 3 + k - 1
+    def zcopy(self, tensor, zs, up):
+        part = self.piece(tensor, self.shard_at(zs))
+        row = tensor * 4 + zs
         return self.copy(
-            part, part, self.zsend.at[row], self.zrecv.at[row], self.dev(z=(self.z + k) % 4))
-
-    def z_arrive(self, tensor, k):
-        part = self.piece(tensor, self.shard_at((self.z + 4 - k) % 4))
-        row = tensor * 3 + k - 1
-        self.copy(
-            part, part, self.zsend.at[row], self.zrecv.at[row], self.dev(fc=1)).wait_recv()
-
-    def own_z(self, tensor, k):
-        self.zcopy(tensor, k).start()
+            part, part, self.zsend.at[2 * row + up], self.zrecv.at[row],
+            self.dev(z=(self.z + (1 if up else 3)) % 4))
+
+    def inner(self, up):
+        return self.z < 3 if up else self.z > 0
+
+    def own_z(self, tensor, up):
+        @pl.when(self.inner(up))
+        def _():
+            self.zcopy(tensor, self.z, up).start()
+
+    def z_arrive(self, tensor, zs):
+        self.zcopy(tensor, zs, 0).wait_recv()
+        for up in (0, 1):
+            @pl.when((zs < self.z if up else zs > self.z) & self.inner(up))
+            def _(up=up):
+                self.zcopy(tensor, zs, up).start()
+        self.start(tensor, zs, 0, 1, 4)
 
     def own_xy(self, tensor):
         self.start(tensor, self.z, 0, 1, 4)
 
     def p1(self, tensor, k):
         if tensor < 2:
-            self.z_arrive(tensor, k)
-            self.start(tensor, self.plane(tensor, k), 0, 1, 4)
+            self.z_arrive(tensor, self.plane(tensor, k))
             return
-        for up in (1, 2, 3):
-            @pl.when((self.z + 4 - up) % 4 == k)
-            def _(up=up):
-                self.z_arrive(tensor, up)
-                self.start(tensor, k, 0, 1, 4)
 
         @pl.when(self.z == k)
         def _():
             self.start(tensor, k, 0, 1, 4)
+
+        @pl.when(self.z != k)
+        def _():
+            self.z_arrive(tensor, k)
 
     def p2x(self, tensor, k):
         zs = self.plane(tensor, k)
@@ -228,15 +237,16 @@
         for kind in range(10 if SHARED[tensor] else 8):
             self.gcopy(tensor, self.plane(tensor, k), kind).wait_send()
 
-    def z_sent(self, tensor):
-        for k in (1, 2, 3):
-            self.zcopy(tensor, k).wait_send()
+    def z_sent(self, tensor, zs):
+        for up in (0, 1):
+            @pl.when((zs <= self.z if up else zs >= self.z) & self.inner(up))
+            def _(up=up):
+                self.zcopy(tensor, zs, up).wait_send()
 
     def credit(self, which):
-        if which == 0:
-            self.z_sent(2)
         for k in ((0,), (1, 2, 3))[which]:
             self.plane_sent(2, k)
+            self.z_sent(2, k)
         pl.semaphore_signal(
             self.free.at[which], inc=1, device_id=self.dev(fc=1), device_id_type=MESH)
 
@@ -862,9 +872,9 @@
 
     def finish(self):
         for tensor in (0, 1):
-            self.z_sent(tensor)
             for k in range(4):
                 self.plane_sent(tensor, k)
+                self.z_sent(tensor, k)
         for g in range(12):
             self.group_sent(g)
         for g in (10, 11):
@@ -879,59 +889,58 @@
 
 K = Layer
 SCHEDULE = (
-    (K.own_z, 0, 1), (K.own_xy, 0), (K.own_square, 1), (K.own_z, 1, 1), (K.own_xy, 1),
-    (K.p1, 0, 1), (K.own_z, 0, 3), (K.p2x, 0, 0), (K.own_z, 0, 2), (K.own_z, 1, 2),
-    (K.p1, 1, 1), (K.p2x, 1, 0), (K.p2y, 1, 0), (K.p2y, 0, 0), (K.p2x, 0, 1), (K.p2y, 0, 1),
-    (K.own_z, 1, 3), (K.p2y, 1, 1), (K.p1, 0, 3), (K.p3, 1, 0, 0), (K.p3, 0, 0, 0),
-    (K.p1, 0, 2), (K.p3, 0, 0, 1), (K.own_ff,), (K.own_z, 2, 3), (K.own_z, 2, 1), (K.p2y, 0, 3),
-    (K.p3, 0, 1, 0), (K.p2x, 0, 3), (K.p3, 0, 1, 1), (K.p2x, 1, 1), (K.p2y, 0, 2), (K.p4, 0, 0),
-    (K.p1, 1, 3), (K.p3, 1, 0, 1), (K.p3, 0, 3, 0), (K.p4, 1, 0), (K.p1, 1, 2), (K.p3, 0, 3, 1),
-    (K.p2y, 1, 3), (K.p3, 1, 1, 0), (K.bias,), (K.p2x, 1, 3), (K.p2x, 0, 2), (K.p2y, 1, 2),
-    (K.p3, 1, 1, 1), (K.p3, 1, 3, 0), (K.p3, 1, 3, 1), (K.p5, 1, 0), (K.p2x, 1, 2),
-    (K.own_z, 2, 2), (K.p4, 1, 1), (K.p3, 0, 2, 0), (K.p1, 2, 1), (K.p3, 0, 2, 1), (K.p4, 1, 3),
-    (K.p3, 1, 2, 0), (K.p3, 1, 2, 1), (K.p4, 1, 2), (K.p5, 1, 2), (K.p5, 1, 3), (K.p1, 2, 0),
-    (K.p2y, 2, 1), (K.p4, 0, 2), (K.p5, 1, 1), (K.cross_kv, 2), (K.p1, 2, 2), (K.p2x, 2, 0),
-    (K.cross_kv, 1), (K.p2x, 2, 1), (K.p5, 0, 2), (K.p4, 0, 1), (K.p2y, 2, 0), (K.p4, 0, 3),
-    (K.p5, 0, 3), (K.p5, 0, 0), (K.p5, 0, 1), (K.self_forward,), (K.cross_forward, 0),
-    (K.p3, 2, 0, 0), (K.p2y, 2, 2), (K.p2x, 2, 2), (K.p3, 2, 1, 0), (K.p3, 2, 0, 1),
-    (K.p1, 2, 3), (K.p3, 2, 1, 1), (K.cross_forward, 1), (K.p3, 2, 2, 0), (K.cross_forward, 2),
-    (K.p4, 2, 0), (K.p3, 2, 2, 1), (K.p4, 2, 1), (K.p5, 2, 0), (K.build_plane, 0),
-    (K.p2x, 2, 3), (K.p2y, 2, 3), (K.credit, 0), (K.p5, 2, 1), (K.build_plane, 1), (K.p4, 2, 2),
-    (K.ff_gate,), (K.p3, 2, 3, 0), (K.p5, 2, 2), (K.build_plane, 2), (K.p3, 2, 3, 1),
-    (K.ff_up,), (K.grad_role, 0, 0), (K.grad_role, 0, 1), (K.grad_role, 0, 2), (K.rs1, 0, 0),
-    (K.p4, 2, 3), (K.rs1, 0, 1), (K.grad_role, 0, 3), (K.rs1, 0, 2), (K.p5, 2, 3),
-    (K.build_plane, 3), (K.d_hidden, 0), (K.d_hidden, 1), (K.rs2, 0, 0), (K.rs2, 0, 1),
-    (K.grad, 1), (K.rs1, 1, 0), (K.credit, 1), (K.rs1, 1, 1), (K.rs3, 0, 1), (K.rs3, 0, 0),
-    (K.rs1, 1, 2), (K.grad, 2), (K.norm_three_back,), (K.rs1, 2, 0), (K.grad, 3), (K.rs2, 1, 0),
-    (K.rs1, 2, 2), (K.rs2, 2, 0), (K.rs1, 2, 1), (K.grad_role, 4, 0), (K.grad_role, 4, 1),
-    (K.grad_role, 4, 2), (K.rs1, 3, 0), (K.rs1, 0, 3), (K.rs2, 3, 1), (K.grad_role, 4, 3),
-    (K.rs1, 2, 3), (K.rs2, 2, 1), (K.rs1, 4, 0), (K.rs3, 2, 0), (K.rs2, 4, 1),
-    (K.cross_back, 0), (K.rs1, 3, 2), (K.rs2, 1, 1), (K.cross_back, 1), (K.rs3, 2, 1),
-    (K.cross_back, 2), (K.rs2, 3, 0), (K.rs1, 4, 1), (K.rs3, 4, 1), (K.rs4, 0), (K.rs1, 3, 1),
-    (K.rs3, 3, 0), (K.grad, 5), (K.grad, 6), (K.rs3, 1, 0), (K.rs3, 3, 1), (K.rs4, 2),
-    (K.grad, 7), (K.rs1, 5, 0), (K.rs2, 5, 0), (K.norm_two_back,), (K.self_back, 0),
-    (K.rs1, 1, 3), (K.rs1, 7, 2), (K.rs1, 3, 3), (K.rs1, 5, 2), (K.rs3, 1, 1), (K.rs1, 4, 2),
-    (K.self_back, 1), (K.rs1, 6, 0), (K.grad, 8), (K.rs1, 5, 1), (K.norm_one_back,), (K.rs4, 1),
-    (K.grad_role, 9, 0), (K.rs4, 3), (K.rs1, 7, 0), (K.rs2, 7, 1), (K.table_back,),
-    (K.rs2, 4, 0), (K.small_start, 0), (K.rs1, 8, 0), (K.rs1, 7, 1), (K.rs1, 5, 3),
-    (K.rs3, 5, 0), (K.grad_role, 9, 1), (K.small_add, 0), (K.grad_role, 9, 2), (K.rs1, 8, 3),
-    (K.grad_role, 9, 3), (K.grad_role, 10, 0), (K.rs2, 6, 1), (K.grad_role, 10, 1),
-    (K.grad_role, 10, 2), (K.small_start, 1), (K.rs1, 6, 2), (K.rs1, 9, 0), (K.rs2, 7, 0),
-    (K.rs5, 2), (K.grad_role, 10, 3), (K.rs3, 7, 1), (K.rs1, 6, 1), (K.grad_role, 11, 0),
-    (K.rs5, 0), (K.rs2, 6, 0), (K.out_rows,), (K.memory_rows, 3), (K.small_add, 1),
-    (K.rs2, 5, 1), (K.rs1, 6, 3), (K.rs3, 5, 1), (K.small_start, 2), (K.rs2, 8, 1),
-    (K.rs1, 9, 1), (K.rs3, 7, 0), (K.rs1, 10, 0), (K.grad_role, 11, 1), (K.rs3, 4, 0),
-    (K.rs2, 9, 0), (K.rs2, 10, 1), (K.rs3, 6, 0), (K.rs1, 7, 3), (K.rs1, 9, 2), (K.rs1, 10, 2),
-    (K.memory_rows, 1), (K.small_add, 2), (K.rs3, 6, 1), (K.rs1, 10, 1), (K.memory_rows, 0),
-    (K.small_start, 3), (K.rs1, 11, 0), (K.rs2, 11, 0), (K.rs2, 8, 0), (K.rs4, 7),
-    (K.rs2, 10, 0), (K.rs4, 5), (K.grad_role, 11, 2), (K.rs2, 9, 1), (K.rs1, 4, 3),
-    (K.grad_role, 11, 3), (K.rs3, 10, 1), (K.rs3, 9, 1), (K.rs1, 10, 3), (K.rs1, 9, 3),
-    (K.memory_rows, 2), (K.rs3, 9, 0), (K.rs1, 11, 3), (K.rs4, 4), (K.small_add, 3),
-    (K.rs1, 8, 2), (K.rs3, 10, 0), (K.rs3, 8, 0), (K.rs1, 8, 1), (K.rs3, 8, 1), (K.rs5, 7),
-    (K.small_start, 4), (K.rs1, 11, 2), (K.rs2, 11, 1), (K.rs1, 11, 1), (K.rs4, 6), (K.rs5, 4),
-    (K.rs5, 3), (K.rs3, 11, 1), (K.rs4, 10), (K.rs3, 11, 0), (K.rs4, 9), (K.rs4, 11),
-    (K.rs4, 8), (K.rs5, 8), (K.rs5, 5), (K.rs5, 10), (K.small_add, 4), (K.rs5, 6), (K.rs5, 11),
-    (K.rs5, 1), (K.rs5, 9),
+    (K.own_xy, 0), (K.own_z, 0, 0), (K.own_z, 0, 1), (K.own_square, 1), (K.own_z, 1, 0),
+    (K.own_ff,), (K.own_xy, 1), (K.own_z, 1, 1), (K.p2x, 0, 0), (K.p1, 0, 1), (K.p1, 0, 2),
+    (K.p1, 1, 2), (K.p2y, 0, 0), (K.own_z, 2, 1), (K.p1, 1, 1), (K.p2y, 1, 0), (K.own_z, 2, 0),
+    (K.p2x, 0, 2), (K.p2x, 0, 1), (K.p2x, 1, 0), (K.p2y, 0, 1), (K.p1, 0, 3), (K.p1, 1, 3),
+    (K.p1, 2, 2), (K.p3, 1, 0, 0), (K.p2y, 1, 1), (K.p2x, 1, 1), (K.p1, 2, 1), (K.p3, 1, 0, 1),
+    (K.p2y, 0, 2), (K.p3, 0, 0, 0), (K.p3, 0, 0, 1), (K.p2y, 1, 2), (K.p2x, 1, 2), (K.p1, 2, 0),
+    (K.p3, 0, 1, 0), (K.p3, 1, 1, 0), (K.p3, 1, 1, 1), (K.p2y, 0, 3), (K.p3, 0, 1, 1),
+    (K.p4, 0, 1), (K.p2y, 1, 3), (K.p2x, 0, 3), (K.p2y, 2, 2), (K.p2x, 2, 2), (K.p2x, 2, 1),
+    (K.p2x, 1, 3), (K.p5, 0, 1), (K.p2y, 2, 1), (K.p3, 0, 2, 0), (K.p3, 0, 2, 1),
+    (K.p3, 1, 2, 0), (K.p3, 1, 2, 1), (K.p1, 2, 3), (K.p3, 0, 3, 0), (K.p4, 0, 2),
+    (K.p3, 0, 3, 1), (K.p3, 2, 2, 0), (K.p4, 0, 0), (K.p2x, 2, 0), (K.p2y, 2, 0), (K.p4, 1, 0),
+    (K.p3, 1, 3, 0), (K.p5, 0, 2), (K.bias,), (K.p4, 0, 3), (K.p3, 1, 3, 1), (K.p4, 1, 2),
+    (K.p5, 0, 0), (K.p3, 2, 1, 0), (K.p3, 2, 1, 1), (K.p3, 2, 2, 1), (K.p4, 1, 1), (K.p5, 1, 0),
+    (K.p5, 0, 3), (K.p5, 1, 1), (K.self_forward,), (K.p4, 1, 3), (K.p3, 2, 0, 0), (K.p5, 1, 2),
+    (K.p2x, 2, 3), (K.p2y, 2, 3), (K.p3, 2, 0, 1), (K.p4, 2, 1), (K.p5, 1, 3), (K.cross_kv, 2),
+    (K.cross_kv, 1), (K.p4, 2, 2), (K.cross_forward, 0), (K.p5, 2, 1), (K.p3, 2, 3, 0),
+    (K.cross_forward, 1), (K.p5, 2, 2), (K.build_plane, 1), (K.p3, 2, 3, 1), (K.p4, 2, 0),
+    (K.cross_forward, 2), (K.build_plane, 2), (K.p5, 2, 0), (K.build_plane, 0), (K.ff_gate,),
+    (K.ff_up,), (K.credit, 0), (K.p4, 2, 3), (K.grad_role, 0, 0), (K.grad_role, 0, 1),
+    (K.grad_role, 0, 2), (K.grad_role, 0, 3), (K.p5, 2, 3), (K.rs1, 0, 0), (K.build_plane, 3),
+    (K.d_hidden, 0), (K.rs1, 0, 2), (K.rs1, 0, 1), (K.d_hidden, 1), (K.grad, 1), (K.credit, 1),
+    (K.rs2, 0, 1), (K.rs2, 0, 0), (K.grad, 2), (K.rs1, 1, 2), (K.rs1, 1, 1), (K.rs1, 1, 0),
+    (K.grad, 3), (K.rs1, 2, 2), (K.rs1, 2, 0), (K.rs1, 2, 1), (K.norm_three_back,),
+    (K.grad_role, 4, 0), (K.cross_back, 0), (K.rs2, 1, 1), (K.rs2, 1, 0), (K.rs2, 2, 0),
+    (K.rs2, 2, 1), (K.rs3, 0, 1), (K.rs1, 1, 3), (K.rs1, 4, 0), (K.rs3, 0, 0),
+    (K.grad_role, 4, 1), (K.cross_back, 1), (K.rs1, 3, 0), (K.cross_back, 2),
+    (K.grad_role, 4, 2), (K.rs3, 2, 0), (K.grad_role, 4, 3), (K.rs3, 2, 1), (K.rs1, 3, 2),
+    (K.rs1, 0, 3), (K.rs1, 2, 3), (K.rs1, 3, 1), (K.rs2, 3, 0), (K.rs3, 1, 1), (K.grad, 5),
+    (K.rs3, 1, 0), (K.rs2, 3, 1), (K.rs4, 0), (K.grad, 6), (K.rs4, 2), (K.grad, 7),
+    (K.rs1, 4, 2), (K.norm_two_back,), (K.rs1, 5, 0), (K.rs1, 4, 3), (K.grad, 8), (K.rs1, 6, 0),
+    (K.self_back, 0), (K.rs3, 3, 0), (K.rs1, 8, 0), (K.rs1, 4, 1), (K.self_back, 1),
+    (K.rs3, 3, 1), (K.grad_role, 9, 0), (K.grad_role, 9, 1), (K.rs2, 8, 0), (K.rs4, 1),
+    (K.grad_role, 9, 2), (K.rs2, 4, 0), (K.grad_role, 9, 3), (K.rs2, 6, 0), (K.rs1, 7, 0),
+    (K.table_back,), (K.rs2, 7, 0), (K.rs1, 8, 3), (K.rs3, 4, 0), (K.rs2, 7, 1), (K.rs2, 4, 1),
+    (K.grad_role, 10, 0), (K.grad_role, 10, 1), (K.grad_role, 10, 2), (K.grad_role, 10, 3),
+    (K.rs1, 8, 1), (K.rs1, 8, 2), (K.norm_one_back,), (K.rs1, 3, 3), (K.grad_role, 11, 0),
+    (K.rs1, 10, 0), (K.rs2, 8, 1), (K.small_start, 0), (K.rs2, 6, 1), (K.rs4, 3),
+    (K.small_add, 0), (K.small_start, 1), (K.rs3, 8, 1), (K.grad_role, 11, 1),
+    (K.grad_role, 11, 2), (K.memory_rows, 0), (K.rs1, 11, 0), (K.rs2, 11, 1), (K.rs2, 11, 0),
+    (K.rs3, 4, 1), (K.small_add, 1), (K.small_start, 2), (K.rs1, 9, 3), (K.rs3, 8, 0),
+    (K.memory_rows, 3), (K.rs2, 10, 0), (K.out_rows,), (K.grad_role, 11, 3), (K.rs1, 11, 2),
+    (K.rs1, 7, 1), (K.rs5, 2), (K.rs1, 7, 3), (K.rs3, 11, 0), (K.rs1, 6, 2), (K.rs1, 9, 2),
+    (K.rs1, 7, 2), (K.rs1, 10, 2), (K.small_add, 2), (K.rs2, 10, 1), (K.small_start, 3),
+    (K.rs1, 11, 1), (K.rs4, 8), (K.rs3, 7, 0), (K.rs3, 11, 1), (K.rs1, 11, 3),
+    (K.memory_rows, 2), (K.rs3, 7, 1), (K.rs4, 4), (K.rs3, 10, 0), (K.rs1, 9, 0), (K.rs1, 6, 3),
+    (K.rs3, 6, 0), (K.rs1, 10, 1), (K.rs4, 11), (K.rs1, 9, 1), (K.rs3, 10, 1), (K.rs1, 10, 3),
+    (K.rs2, 9, 0), (K.rs1, 6, 1), (K.memory_rows, 1), (K.rs3, 9, 0), (K.rs3, 6, 1),
+    (K.rs2, 9, 1), (K.rs5, 1), (K.small_add, 3), (K.rs4, 7), (K.rs1, 5, 3), (K.rs4, 10),
+    (K.rs3, 9, 1), (K.rs1, 5, 2), (K.rs5, 0), (K.rs1, 5, 1), (K.rs4, 6), (K.small_start, 4),
+    (K.rs5, 8), (K.rs5, 10), (K.rs2, 5, 1), (K.rs3, 5, 1), (K.rs4, 9), (K.rs2, 5, 0),
+    (K.rs3, 5, 0), (K.rs5, 7), (K.rs4, 5), (K.rs5, 9), (K.rs5, 6), (K.rs5, 3), (K.small_add, 4),
+    (K.rs5, 5), (K.rs5, 11), (K.rs5, 4),
 )
 
 NAMES = (
@@ -1018,7 +1027,7 @@
             pltpu.VMEM((16, 128), F32),
             pltpu.VMEM((6, 8, D), F32), pltpu.VMEM((6, 16, 128), F32),
             pltpu.VMEM((5, 8, D), F32), pltpu.VMEM((5, 16, 128), F32),
-            dma((120,)), dma((120,)), dma((9,)), dma((9,)), dma((180,)), dma((180,)), dma((9,)),
+            dma((120,)), dma((120,)), dma((24,)), dma((12,)), dma((180,)), dma((180,)), dma((9,)),
             dma((10,)), dma((10,)), pltpu.SemaphoreType.REGULAR((2,)),
         ],
         compiler_params=pltpu.CompilerParams(

time: 198 us -> 186 us (0.939)
  Pallas kernels: 195 us -> 184 us
    pallas_call x1, Pallas kernels: 192 us -> 181 us  [fused(): pl.pallas_call(kernel, out_shape=(s((length, D), BF), s((length, D), BF),...]
where the time goes in v3:
time: 186 us
  Pallas kernels  184 us (99%)
  between operations  2.11 us (1%)
    pallas_call x1, Pallas kernels, fused(): pl.pallas_call(kernel, out_shape=(s((length, D), BF), s((length, D), BF),...  181 us

profile of v3, /device:TPU:0, one launch (start us, length us, event | category | flops | bytes accessed | tf_op | source)
XLA Modules:
  0.0 185.9 jit_solution(17021580723832508457)
XLA Ops:
  1.9 180.7 %shard_map.161 = (bf16[128,768]{1,0:T(8,128)(2,1)}, bf16[128,768]{1,0:T(8,128)(2,1)}, bf16[512,768]{1,0:T(8,128)(2,1)}, f32[576,128]{1,0:T(8,128)}, f32[576,128]...) custom-call(bf16[128,768]{1,0:T(8,128)(2,1)} %bitcast.20, bf16[512,768]{1,0:T(8,128)(2,1)} %bitcast.14, ...), custom_call_target="tpu_custom_call" | custom-call | flops 10000000000 | bytes 8000000 | tf_op jit(solution)/shard_map/pallas_call | solution.py:1005
  182.6 3.1 %shard_map.162 = (bf16[128,768]{1,0:T(8,128)(2,1)}, bf16[128,768]{1,0:T(8,128)(2,1)}, bf16[512,768]{1,0:T(8,128)(2,1)}, f32[576,128]{1,0:T(8,128)}, f32[576,128]...) custom-call(bf16[128,768]{1,0:T(8,128)(2,1)} %get-tuple-element.24.refs_0_, ...), custom_call_target="tpu_custom_call" | custom-call | tf_op jit(solution)/shard_map/pallas_call | solution.py:983

commit v4 on v3

--- a/solution.py
+++ b/solution.py
@@ -250,8 +250,23 @@
         pl.semaphore_signal(
             self.free.at[which], inc=1, device_id=self.dev(fc=1), device_id_type=MESH)
 
+    def enter(self, i):
+        src = (self.sh_s_hbm, self.sh_c_hbm, self.sh_f_hbm, self.x_hbm, self.mem_hbm, self.g_hbm)
+        dst = (self.sh_s, self.sh_c, self.sh_f, self.x_in, self.mem, self.g)
+        return pltpu.make_async_copy(src[i], dst[i], self.isem.at[i])
+
+    def leave(self, i, part=None):
+        if part is not None:
+            rows = slice(128 * part, 128 * part + 128)
+            return pltpu.make_async_copy(
+                self.mgrad.at[rows, :], self.mgrad_hbm.at[rows, :], self.osem.at[i])
+        src = (self.block, self.xgrad, None, self.gs, self.gc, self.gf)[i]
+        dst = (self.block_hbm, self.xgrad_hbm, None, self.gs_hbm, self.gc_hbm, self.gf_hbm)[i]
+        return pltpu.make_async_copy(src, dst, self.osem.at[i])
+
     def own_square(self, tensor):
         src, dst = ((self.sh_s, self.ws), (self.sh_c, self.wc))[tensor]
+        self.enter(tensor).wait()
         self.flat[0:576, :] = src[...].astype(F32)
         row = al(self.shard * AR, 16)
         for t in range(6):
@@ -259,6 +274,7 @@
                 pl.ds(t, AR, stride=6), :].astype(BF)
 
     def own_ff(self):
+        self.enter(2).wait()
         self.flat[0:1152, :] = self.sh_f[...].astype(F32)
         base = self.shard * FU
         flat, wf = self.flat, self.wf
@@ -363,6 +379,8 @@
         return pl.ds(al(p * 256, 256), 256)
 
     def self_forward(self):
+        for i in (3, 4, 5):
+            self.enter(i).wait()
         x = self.x_in[...].astype(F32)
         self.n1[...] = rms(x, self.gains[0:1, :]).astype(BF)
         n1 = self.n1[...]
@@ -452,6 +470,7 @@
         for p in range(3):
             cols = slice(256 * p, 256 * p + 256)
             self.block[:, cols] = (self.r2[:, cols] + nn(hid, self.wd[:, cols])).astype(BF)
+        self.leave(0).start()
 
     def d_hidden(self, part):
         g = self.g[...]
@@ -583,6 +602,7 @@
                 nt(self.ck[rows, :], self.wc[D + wrow:D + wrow + 256, :])
                 + nt(self.cv[rows, :], self.wc[2 * D + wrow:2 * D + wrow + 256, :])
             ).astype(BF)
+        self.leave(6 + i, i).start()
 
     def norm_two_back(self):
         self.back_product(((self.cq, self.wc, 0, D),), self.dz)
@@ -619,6 +639,7 @@
         dv, dg = rms_back(self.x_in[...].astype(F32), self.gains[0:1, :], self.dz[...])
         self.redg[0, 0:1, :] = dg
         self.xgrad[...] = (self.dr[...] + dv).astype(BF)
+        self.leave(1).start()
 
     def table_back(self):
         row = lax.broadcasted_iota(jnp.int32, (128, 128), 0)
@@ -807,6 +828,7 @@
                 for k in range(6):
                     out[pl.ds(k, AR, stride=6), :] = total(
                         96 * (k // 2), 96, slice(128 * (k % 2), 128 * (k % 2) + 128))
+                self.leave(3 + t).start()
                 return
             out = self.gf
 
@@ -839,6 +861,8 @@
                 @pl.when(self.shard > 21)
                 def _():
                     tall(0, 192, 0)
+
+            self.leave(5).start()
 
     def group_sent(self, g):
         for kind in range(1, 11):
@@ -880,6 +904,10 @@
         for g in (10, 11):
             for role in range(4):
                 self.scopy(g, SIB[role]).wait_send()
+        for i in (0, 1, 3, 4, 5):
+            self.leave(i).wait()
+        for i in range(4):
+            self.leave(6 + i, i).wait()
         self.ggain[...] = self.redga[5, 0:3, :]
         self.gtable[...] = self.redta[5, 0:H, 0:NB]
         for step in range(5):
@@ -944,8 +972,10 @@
 )
 
 NAMES = (
-    "x_in", "mem", "g", "dl", "ml", "sh_s", "sh_c", "sh_f", "gains", "table",
-    "block", "xgrad", "mgrad", "gs", "gc", "gf", "ggain", "gtable",
+    "x_hbm", "mem_hbm", "g_hbm", "dl", "ml", "sh_s_hbm", "sh_c_hbm", "sh_f_hbm", "gains", "table",
+    "block_hbm", "xgrad_hbm", "mgrad_hbm", "gs_hbm", "gc_hbm", "gf_hbm", "ggain", "gtable",
+    "x_in", "mem", "g", "sh_s", "sh_c", "sh_f", "block", "xgrad", "mgrad", "gs", "gc", "gf",
+    "isem", "osem",
     "ws", "wc", "wf", "wgu", "wd", "gb", "lb", "zb",
     "n1", "q", "k", "v", "mix", "r1", "n2", "cq", "ck", "cv", "cmix", "r2", "n3",
     "ga", "ub", "hid", "hidt", "n3t", "dg", "du", "dz", "dr", "drb", "tt", "memt",
@@ -962,6 +992,8 @@
         st.dev(z=(st.z + k) % 4) for k in (1, 2, 3)]
     for other in others:
         pl.semaphore_signal(barrier, inc=1, device_id=other, device_id_type=MESH)
+    for i in range(6):
+        st.enter(i).start()
     st.own_square(0)
     st.masks()
     pl.semaphore_wait(barrier, 6)
@@ -971,21 +1003,29 @@
 
 
 def settle_kernel(count, *refs):
-    out = [pltpu.make_async_copy(refs[i], refs[count + i], refs[-1].at[i]) for i in range(count)]
-    for one in out:
+    src, dst, held = refs[:count], refs[count:2 * count], refs[2 * count:3 * count]
+    arrive, go = refs[3 * count:]
+    into = [pltpu.make_async_copy(src[i], held[i], arrive.at[i]) for i in range(count)]
+    out = [pltpu.make_async_copy(held[i], dst[i], go.at[i]) for i in range(count)]
+    for one in into:
         one.start()
+    for first, then in zip(into, out):
+        first.wait()
+        then.start()
     for one in out:
         one.wait()
 
 
 def settle(arrays):
+    anywhere = pl.BlockSpec(memory_space=pl.ANY)
     count = len(arrays)
     return pl.pallas_call(
         functools.partial(settle_kernel, count),
         out_shape=tuple(jax.ShapeDtypeStruct(v.shape, v.dtype) for v in arrays),
-        in_specs=[pl.BlockSpec(memory_space=pltpu.VMEM)] * count,
-        out_specs=tuple([pl.BlockSpec(memory_space=pl.ANY)] * count),
-        scratch_shapes=[pltpu.SemaphoreType.DMA((count,))],
+        in_specs=[anywhere] * count,
+        out_specs=tuple([anywhere] * count),
+        scratch_shapes=[pltpu.VMEM(v.shape, v.dtype) for v in arrays] + [
+            pltpu.SemaphoreType.DMA((count,)), pltpu.SemaphoreType.DMA((count,))],
         compiler_params=pltpu.CompilerParams(vmem_limit_bytes=67000000),
     )(*arrays)
 
@@ -994,6 +1034,7 @@
           ff_params, gains, table):
     slots, length, width = inputs.shape
     mem_len = memory.shape[1]
+    hbm = pl.BlockSpec(memory_space=pl.ANY)
     vm = pl.BlockSpec(memory_space=pltpu.VMEM)
     sm = pl.BlockSpec(memory_space=pltpu.SMEM)
     s = jax.ShapeDtypeStruct
@@ -1009,9 +1050,13 @@
             s((rows_s, 128), F32), s((rows_s, 128), F32), s((rows_f, 128), F32),
             s((3, D), F32), s((H, NB), F32),
         ),
-        in_specs=[vm, vm, vm, sm, sm, vm, vm, vm, vm, sm],
-        out_specs=[vm] * 8,
+        in_specs=[hbm, hbm, hbm, sm, sm, hbm, hbm, hbm, vm, sm],
+        out_specs=[hbm] * 6 + [vm] * 2,
         scratch_shapes=[
+            row, memory_row, row, pltpu.VMEM((rows_s, 128), BF), pltpu.VMEM((rows_s, 128), BF),
+            pltpu.VMEM((rows_f, 128), BF), row, row, memory_row,
+            pltpu.VMEM((rows_s, 128), F32), pltpu.VMEM((rows_s, 128), F32),
+            pltpu.VMEM((rows_f, 128), F32), dma((6,)), dma((10,)),
             pltpu.VMEM((4 * D, D), BF), pltpu.VMEM((4 * D, D), BF),
             pltpu.VMEM((32 * FU, 256), BF),
             pltpu.VMEM((2 * D, FF), BF), pltpu.VMEM((FF, D), BF),

time: 186 us -> 185 us (level)
  no operation moved by 1% of the time
where the time goes in v4:
time: 185 us
  Pallas kernels  183 us (99%)
  between operations  2.11 us (1%)
    pallas_call x1, Pallas kernels, fused(): pl.pallas_call(kernel, out_shape=(s((length, D), BF), s((length, D), BF),...  180 us

profile of v4, /device:TPU:0, one launch (start us, length us, event | category | flops | bytes accessed | tf_op | source)
XLA Modules:
  0.0 184.7 jit_solution(14275716533192320940)
XLA Ops:
  1.9 179.8 %shard_map.161 = (bf16[128,768]{1,0:T(8,128)(2,1)}, bf16[128,768]{1,0:T(8,128)(2,1)}, bf16[512,768]{1,0:T(8,128)(2,1)}, f32[576,128]{1,0:T(8,128)}, f32[576,128]...) custom-call(bf16[128,768]{1,0:T(8,128)(2,1)} %bitcast.20, bf16[512,768]{1,0:T(8,128)(2,1)} %bitcast.14, ...), custom_call_target="tpu_custom_call" | custom-call | flops 10000000000 | bytes 8000000 | tf_op jit(solution)/shard_map/pallas_call | solution.py:1046
  181.7 2.8 %shard_map.162 = (bf16[128,768]{1,0:T(8,128)(2,1)}, bf16[128,768]{1,0:T(8,128)(2,1)}, bf16[512,768]{1,0:T(8,128)(2,1)}, f32[576,128]{1,0:T(8,128)}, f32[576,128]...) custom-call(bf16[128,768]{1,0:T(8,128)(2,1)} %get-tuple-element.24.refs_0_, ...), custom_call_target="tpu_custom_call" | custom-call | tf_op jit(solution)/shard_map/pallas_call | solution.py:1022

commit v5 on v4

--- a/solution.py
+++ b/solution.py
@@ -28,15 +28,14 @@
     (1, 3), (1, 2), (1, 1), (1, 0),
     (0, 3), (0, 0), (0, 2), (0, 1),
 )
-PAIR = (True,) * 4 + (False,) * 8
+PAIR = (True,) * 10 + (False,) * 2
 SHARED = (True, True, True)
 UNIT = tuple(FU if t == 2 else AU for t, _ in GROUPS)
 OWN = tuple(4 * sum(UNIT[:g]) for g in range(12))
 OWN_ROWS = 4 * sum(UNIT)
 LAND = tuple(3 * sum(UNIT[:g]) for g in range(12))
 LAND_ROWS = 3 * sum(UNIT)
-ZBASE = (0, 3 * AU, 6 * AU)
-Z_ROWS = 6 * AU + 3 * FU
+Z_ROWS = 5 * FU
 STAGE = 4 * FU
 ROLES = ((1, 1), (1, 0), (0, 1), (0, 0))
 SIB = (0, 12, 13, 14)
@@ -573,6 +572,12 @@
         self.redg[0, 2:3, :] = dg
         self.dr[...] = self.g[...].astype(F32) + dv
         self.drb[...] = self.dr[...].astype(BF)
+        for up in (0, 1):
+            @pl.when(self.inner(up))
+            def _(up=up):
+                pl.semaphore_signal(
+                    self.free.at[3 - up], inc=1,
+                    device_id=self.dev(z=(self.z + (1 if up else 3)) % 4), device_id_type=MESH)
 
     def cross_back(self, part):
         for p in range(3) if part == 0 else ():
@@ -726,15 +731,44 @@
         for kind in kinds:
             self.scopy(g, kind).start()
 
-    def to_owner(self, g, slot=None):
-        t, zb = GROUPS[g]
-        unit = UNIT[g]
-        if slot is None:
-            slot = (self.z + 3 - zb) % 4
+    def z_land(self, g, second):
+        t = GROUPS[g][0]
+        if t == 2:
+            return self.zb.at[pl.ds((4 if second else g) * FU, FU), :]
+        if second:
+            return self.wgu.at[AU:2 * AU, 256 * t:256 * t + 256]
+        return self.wgu.at[0:AU, 256 * (g - 4):256 * (g - 4) + 256]
+
+    def to_owner(self, g, below, second):
         return self.copy(
-            self.gb.at[self.own(g, self.chip()), :],
-            self.zb.at[pl.ds(al(ZBASE[t] + slot * unit, 16), unit), :],
-            self.rsend.at[g * 15 + 11], self.orecv.at[t * 3 + slot], self.dev(z=zb))
+            self.gb.at[self.own(g, self.chip()), :], self.z_land(g, second),
+            self.rsend.at[g * 15 + 11], self.orecv.at[g * 2 + second],
+            self.dev(z=(self.z + (1 if below else 3)) % 4))
+
+    def hop(self, g, stage, act):
+        zb = GROUPS[g][1]
+        for below in (True, False):
+            z = stage if below else 3 - stage
+            last = zb - 1 if below else zb + 1
+            if not (z <= last if below else z >= last) or not 0 <= last < 4:
+                continue
+
+            @pl.when(self.z == z)
+            def _(below=below, z=z, last=last):
+                act(self.to_owner(g, below, 1 if z == last and not below and zb > 0 else 0))
+
+    def z_came(self, g, second):
+        part = self.z_land(g, second)
+        self.copy(
+            part, part, self.rsend.at[g * 15 + 11], self.orecv.at[g * 2 + second],
+            self.dev(fc=1)).wait_recv()
+        return part
+
+    def zfree(self):
+        for up in (0, 1):
+            @pl.when(self.inner(up))
+            def _(up=up):
+                pl.semaphore_wait(self.free.at[2 + up], 1)
 
     def ready(self, g):
         self.turn(g)
@@ -802,9 +836,16 @@
             self.gb[rows, :].astype(F32) + self.lb[self.land(g, 2), :].astype(F32)
             + self.lb[self.land(g, 3), :].astype(F32)).astype(BF)
 
-        @pl.when(self.z != GROUPS[g][1])
-        def _():
-            self.to_owner(g).start()
+    def rsz(self, g, stage):
+        def act(copy):
+            if stage:
+                part = self.z_came(g, 0)
+                everything = slice(None)
+                self.accumulate(
+                    self.own(g, self.chip()), everything, part, everything, everything)
+            copy.start()
+
+        self.hop(g, stage, act)
 
     def rs5(self, g):
         t, zb = GROUPS[g]
@@ -812,15 +853,14 @@
 
         @pl.when(self.z == zb)
         def _():
-            for slot in range(3):
-                self.to_owner(g, slot).wait_recv()
+            places = (0, 1) if 0 < zb < 3 else (0,)
+            parts = [self.z_came(g, second) for second in places]
 
             def total(start, size, lanes):
                 at = pl.ds(al(OWN[g] + self.chip() * unit + start, 16), size)
                 value = self.gb[at, lanes].astype(F32)
-                for slot in range(3):
-                    value = value + self.zb[
-                        pl.ds(ZBASE[t] + slot * unit + start, size), lanes].astype(F32)
+                for part in parts:
+                    value = value + part[pl.ds(start, size), lanes].astype(F32)
                 return value
 
             if t < 2:
@@ -869,9 +909,8 @@
             if PAIR[g] or kind not in (5, 8, 9, 10):
                 self.scopy(g, kind).wait_send()
 
-        @pl.when(self.z != GROUPS[g][1])
-        def _():
-            self.to_owner(g).wait_send()
+        for stage in range(3):
+            self.hop(g, stage, lambda copy: copy.wait_send())
 
     def small(self, step, which):
         dev = (
@@ -917,58 +956,64 @@
 
 K = Layer
 SCHEDULE = (
-    (K.own_xy, 0), (K.own_z, 0, 0), (K.own_z, 0, 1), (K.own_square, 1), (K.own_z, 1, 0),
-    (K.own_ff,), (K.own_xy, 1), (K.own_z, 1, 1), (K.p2x, 0, 0), (K.p1, 0, 1), (K.p1, 0, 2),
-    (K.p1, 1, 2), (K.p2y, 0, 0), (K.own_z, 2, 1), (K.p1, 1, 1), (K.p2y, 1, 0), (K.own_z, 2, 0),
-    (K.p2x, 0, 2), (K.p2x, 0, 1), (K.p2x, 1, 0), (K.p2y, 0, 1), (K.p1, 0, 3), (K.p1, 1, 3),
-    (K.p1, 2, 2), (K.p3, 1, 0, 0), (K.p2y, 1, 1), (K.p2x, 1, 1), (K.p1, 2, 1), (K.p3, 1, 0, 1),
-    (K.p2y, 0, 2), (K.p3, 0, 0, 0), (K.p3, 0, 0, 1), (K.p2y, 1, 2), (K.p2x, 1, 2), (K.p1, 2, 0),
-    (K.p3, 0, 1, 0), (K.p3, 1, 1, 0), (K.p3, 1, 1, 1), (K.p2y, 0, 3), (K.p3, 0, 1, 1),
-    (K.p4, 0, 1), (K.p2y, 1, 3), (K.p2x, 0, 3), (K.p2y, 2, 2), (K.p2x, 2, 2), (K.p2x, 2, 1),
-    (K.p2x, 1, 3), (K.p5, 0, 1), (K.p2y, 2, 1), (K.p3, 0, 2, 0), (K.p3, 0, 2, 1),
-    (K.p3, 1, 2, 0), (K.p3, 1, 2, 1), (K.p1, 2, 3), (K.p3, 0, 3, 0), (K.p4, 0, 2),
-    (K.p3, 0, 3, 1), (K.p3, 2, 2, 0), (K.p4, 0, 0), (K.p2x, 2, 0), (K.p2y, 2, 0), (K.p4, 1, 0),
-    (K.p3, 1, 3, 0), (K.p5, 0, 2), (K.bias,), (K.p4, 0, 3), (K.p3, 1, 3, 1), (K.p4, 1, 2),
-    (K.p5, 0, 0), (K.p3, 2, 1, 0), (K.p3, 2, 1, 1), (K.p3, 2, 2, 1), (K.p4, 1, 1), (K.p5, 1, 0),
-    (K.p5, 0, 3), (K.p5, 1, 1), (K.self_forward,), (K.p4, 1, 3), (K.p3, 2, 0, 0), (K.p5, 1, 2),
-    (K.p2x, 2, 3), (K.p2y, 2, 3), (K.p3, 2, 0, 1), (K.p4, 2, 1), (K.p5, 1, 3), (K.cross_kv, 2),
-    (K.cross_kv, 1), (K.p4, 2, 2), (K.cross_forward, 0), (K.p5, 2, 1), (K.p3, 2, 3, 0),
-    (K.cross_forward, 1), (K.p5, 2, 2), (K.build_plane, 1), (K.p3, 2, 3, 1), (K.p4, 2, 0),
-    (K.cross_forward, 2), (K.build_plane, 2), (K.p5, 2, 0), (K.build_plane, 0), (K.ff_gate,),
-    (K.ff_up,), (K.credit, 0), (K.p4, 2, 3), (K.grad_role, 0, 0), (K.grad_role, 0, 1),
-    (K.grad_role, 0, 2), (K.grad_role, 0, 3), (K.p5, 2, 3), (K.rs1, 0, 0), (K.build_plane, 3),
-    (K.d_hidden, 0), (K.rs1, 0, 2), (K.rs1, 0, 1), (K.d_hidden, 1), (K.grad, 1), (K.credit, 1),
-    (K.rs2, 0, 1), (K.rs2, 0, 0), (K.grad, 2), (K.rs1, 1, 2), (K.rs1, 1, 1), (K.rs1, 1, 0),
-    (K.grad, 3), (K.rs1, 2, 2), (K.rs1, 2, 0), (K.rs1, 2, 1), (K.norm_three_back,),
-    (K.grad_role, 4, 0), (K.cross_back, 0), (K.rs2, 1, 1), (K.rs2, 1, 0), (K.rs2, 2, 0),
-    (K.rs2, 2, 1), (K.rs3, 0, 1), (K.rs1, 1, 3), (K.rs1, 4, 0), (K.rs3, 0, 0),
-    (K.grad_role, 4, 1), (K.cross_back, 1), (K.rs1, 3, 0), (K.cross_back, 2),
-    (K.grad_role, 4, 2), (K.rs3, 2, 0), (K.grad_role, 4, 3), (K.rs3, 2, 1), (K.rs1, 3, 2),
-    (K.rs1, 0, 3), (K.rs1, 2, 3), (K.rs1, 3, 1), (K.rs2, 3, 0), (K.rs3, 1, 1), (K.grad, 5),
-    (K.rs3, 1, 0), (K.rs2, 3, 1), (K.rs4, 0), (K.grad, 6), (K.rs4, 2), (K.grad, 7),
-    (K.rs1, 4, 2), (K.norm_two_back,), (K.rs1, 5, 0), (K.rs1, 4, 3), (K.grad, 8), (K.rs1, 6, 0),
-    (K.self_back, 0), (K.rs3, 3, 0), (K.rs1, 8, 0), (K.rs1, 4, 1), (K.self_back, 1),
-    (K.rs3, 3, 1), (K.grad_role, 9, 0), (K.grad_role, 9, 1), (K.rs2, 8, 0), (K.rs4, 1),
-    (K.grad_role, 9, 2), (K.rs2, 4, 0), (K.grad_role, 9, 3), (K.rs2, 6, 0), (K.rs1, 7, 0),
-    (K.table_back,), (K.rs2, 7, 0), (K.rs1, 8, 3), (K.rs3, 4, 0), (K.rs2, 7, 1), (K.rs2, 4, 1),
-    (K.grad_role, 10, 0), (K.grad_role, 10, 1), (K.grad_role, 10, 2), (K.grad_role, 10, 3),
-    (K.rs1, 8, 1), (K.rs1, 8, 2), (K.norm_one_back,), (K.rs1, 3, 3), (K.grad_role, 11, 0),
-    (K.rs1, 10, 0), (K.rs2, 8, 1), (K.small_start, 0), (K.rs2, 6, 1), (K.rs4, 3),
-    (K.small_add, 0), (K.small_start, 1), (K.rs3, 8, 1), (K.grad_role, 11, 1),
-    (K.grad_role, 11, 2), (K.memory_rows, 0), (K.rs1, 11, 0), (K.rs2, 11, 1), (K.rs2, 11, 0),
-    (K.rs3, 4, 1), (K.small_add, 1), (K.small_start, 2), (K.rs1, 9, 3), (K.rs3, 8, 0),
-    (K.memory_rows, 3), (K.rs2, 10, 0), (K.out_rows,), (K.grad_role, 11, 3), (K.rs1, 11, 2),
-    (K.rs1, 7, 1), (K.rs5, 2), (K.rs1, 7, 3), (K.rs3, 11, 0), (K.rs1, 6, 2), (K.rs1, 9, 2),
-    (K.rs1, 7, 2), (K.rs1, 10, 2), (K.small_add, 2), (K.rs2, 10, 1), (K.small_start, 3),
-    (K.rs1, 11, 1), (K.rs4, 8), (K.rs3, 7, 0), (K.rs3, 11, 1), (K.rs1, 11, 3),
-    (K.memory_rows, 2), (K.rs3, 7, 1), (K.rs4, 4), (K.rs3, 10, 0), (K.rs1, 9, 0), (K.rs1, 6, 3),
-    (K.rs3, 6, 0), (K.rs1, 10, 1), (K.rs4, 11), (K.rs1, 9, 1), (K.rs3, 10, 1), (K.rs1, 10, 3),
-    (K.rs2, 9, 0), (K.rs1, 6, 1), (K.memory_rows, 1), (K.rs3, 9, 0), (K.rs3, 6, 1),
-    (K.rs2, 9, 1), (K.rs5, 1), (K.small_add, 3), (K.rs4, 7), (K.rs1, 5, 3), (K.rs4, 10),
-    (K.rs3, 9, 1), (K.rs1, 5, 2), (K.rs5, 0), (K.rs1, 5, 1), (K.rs4, 6), (K.small_start, 4),
-    (K.rs5, 8), (K.rs5, 10), (K.rs2, 5, 1), (K.rs3, 5, 1), (K.rs4, 9), (K.rs2, 5, 0),
-    (K.rs3, 5, 0), (K.rs5, 7), (K.rs4, 5), (K.rs5, 9), (K.rs5, 6), (K.rs5, 3), (K.small_add, 4),
-    (K.rs5, 5), (K.rs5, 11), (K.rs5, 4),
+    (K.own_z, 0, 0), (K.own_xy, 0), (K.own_z, 0, 1), (K.own_square, 1), (K.own_xy, 1),
+    (K.own_z, 1, 0), (K.own_z, 1, 1), (K.p1, 0, 1), (K.own_ff,), (K.own_z, 2, 0),
+    (K.own_z, 2, 1), (K.p2x, 1, 0), (K.p1, 1, 1), (K.p2y, 0, 1), (K.p2x, 0, 0), (K.p2x, 0, 1),
+    (K.p2y, 0, 0), (K.p1, 0, 3), (K.p1, 0, 2), (K.p1, 1, 2), (K.p2y, 1, 1), (K.p2x, 1, 1),
+    (K.p1, 1, 3), (K.p2x, 0, 3), (K.p2y, 1, 0), (K.p2y, 0, 3), (K.p2x, 0, 2), (K.p2y, 0, 2),
+    (K.p1, 2, 2), (K.p3, 0, 1, 0), (K.p3, 0, 0, 0), (K.p3, 1, 1, 0), (K.p3, 0, 1, 1),
+    (K.p3, 0, 0, 1), (K.p3, 1, 0, 0), (K.p2x, 1, 2), (K.p2y, 1, 2), (K.p3, 1, 1, 1),
+    (K.p1, 2, 1), (K.p1, 2, 0), (K.p3, 1, 0, 1), (K.p3, 0, 3, 0), (K.p3, 0, 2, 0),
+    (K.p2y, 1, 3), (K.p3, 0, 2, 1), (K.p3, 0, 3, 1), (K.p2x, 1, 3), (K.p4, 0, 0), (K.p4, 0, 1),
+    (K.p2y, 2, 2), (K.p3, 1, 2, 0), (K.p2x, 2, 2), (K.p1, 2, 3), (K.p4, 0, 3), (K.p3, 1, 2, 1),
+    (K.p5, 0, 0), (K.p3, 1, 3, 0), (K.p4, 1, 0), (K.p4, 1, 1), (K.p3, 1, 3, 1), (K.p5, 0, 1),
+    (K.p2x, 2, 1), (K.p4, 0, 2), (K.p5, 0, 3), (K.p3, 2, 2, 0), (K.p2y, 2, 1), (K.p2x, 2, 0),
+    (K.p5, 0, 2), (K.p3, 2, 2, 1), (K.bias,), (K.self_forward,), (K.p4, 1, 2), (K.p2y, 2, 0),
+    (K.p4, 1, 3), (K.p2x, 2, 3), (K.p2y, 2, 3), (K.p3, 2, 1, 0), (K.p5, 1, 1), (K.p4, 2, 2),
+    (K.p3, 2, 1, 1), (K.p5, 1, 2), (K.p5, 1, 3), (K.p5, 1, 0), (K.cross_kv, 1), (K.cross_kv, 2),
+    (K.p3, 2, 0, 0), (K.cross_forward, 0), (K.p3, 2, 0, 1), (K.p3, 2, 3, 0), (K.p3, 2, 3, 1),
+    (K.p5, 2, 2), (K.p4, 2, 1), (K.cross_forward, 1), (K.p4, 2, 0), (K.build_plane, 2),
+    (K.cross_forward, 2), (K.p5, 2, 1), (K.build_plane, 1), (K.p5, 2, 0), (K.build_plane, 0),
+    (K.ff_gate,), (K.ff_up,), (K.credit, 0), (K.p4, 2, 3), (K.grad_role, 0, 0),
+    (K.grad_role, 0, 1), (K.grad_role, 0, 2), (K.grad_role, 0, 3), (K.p5, 2, 3),
+    (K.build_plane, 3), (K.rs1, 0, 0), (K.d_hidden, 0), (K.rs1, 0, 1), (K.d_hidden, 1),
+    (K.credit, 1), (K.rs1, 0, 2), (K.grad, 1), (K.grad, 2), (K.rs2, 0, 0), (K.rs1, 1, 0),
+    (K.rs2, 0, 1), (K.rs1, 1, 1), (K.rs1, 1, 2), (K.grad, 3), (K.rs1, 2, 0),
+    (K.norm_three_back,), (K.rs1, 2, 3), (K.rs3, 0, 1), (K.rs1, 3, 1), (K.rs3, 0, 0),
+    (K.rs1, 3, 2), (K.cross_back, 0), (K.rs2, 1, 1), (K.grad_role, 4, 0), (K.grad_role, 4, 1),
+    (K.cross_back, 1), (K.grad_role, 4, 2), (K.rs2, 2, 0), (K.rs1, 3, 0), (K.rs2, 1, 0),
+    (K.cross_back, 2), (K.rs2, 2, 1), (K.rs1, 2, 1), (K.rs1, 0, 3), (K.grad_role, 4, 3),
+    (K.rs1, 4, 0), (K.rs4, 0), (K.rs1, 2, 2), (K.grad, 5), (K.rsz, 0, 0), (K.rs3, 2, 0),
+    (K.grad, 6), (K.rs3, 2, 1), (K.rs1, 5, 0), (K.rs3, 1, 1), (K.rs2, 3, 0), (K.grad, 7),
+    (K.rs1, 6, 0), (K.rs2, 3, 1), (K.rs2, 4, 0), (K.rs3, 1, 0), (K.rs1, 5, 1),
+    (K.norm_two_back,), (K.rs1, 7, 0), (K.rsz, 0, 1), (K.rs1, 4, 2), (K.rs4, 2), (K.rsz, 2, 0),
+    (K.grad, 8), (K.self_back, 0), (K.rs3, 3, 0), (K.rs3, 3, 1), (K.rs2, 5, 0),
+    (K.self_back, 1), (K.grad_role, 9, 0), (K.rs2, 4, 1), (K.rs1, 6, 3), (K.rs2, 7, 0),
+    (K.rs3, 4, 0), (K.zfree,), (K.rs1, 8, 0), (K.rs1, 7, 1), (K.rs1, 1, 3), (K.rs1, 3, 3),
+    (K.rs2, 5, 1), (K.rs1, 4, 3), (K.rs1, 9, 0), (K.rs1, 7, 2), (K.rs1, 5, 2), (K.rs1, 4, 1),
+    (K.rs4, 3), (K.rsz, 3, 0), (K.rs1, 8, 3), (K.rs4, 1), (K.rs1, 8, 1), (K.rs2, 7, 1),
+    (K.rsz, 0, 2), (K.rsz, 2, 1), (K.rs1, 8, 2), (K.rsz, 1, 0), (K.table_back,),
+    (K.memory_rows, 1), (K.rs3, 5, 0), (K.rs3, 5, 1), (K.norm_one_back,), (K.rs3, 4, 1),
+    (K.rs2, 6, 1), (K.rs2, 8, 0), (K.small_start, 0), (K.memory_rows, 0), (K.rs2, 9, 0),
+    (K.small_add, 0), (K.rs2, 8, 1), (K.rs2, 6, 0), (K.rs3, 7, 0), (K.grad_role, 9, 1),
+    (K.grad_role, 9, 2), (K.grad_role, 9, 3), (K.grad_role, 10, 0), (K.grad_role, 10, 1),
+    (K.grad_role, 10, 2), (K.grad_role, 10, 3), (K.grad_role, 11, 0), (K.small_start, 1),
+    (K.rs4, 4), (K.grad_role, 11, 1), (K.rs3, 7, 1), (K.grad_role, 11, 2), (K.rs1, 7, 3),
+    (K.rs2, 9, 1), (K.rs1, 10, 0), (K.rs2, 10, 1), (K.rs1, 5, 3), (K.grad_role, 11, 3),
+    (K.rsz, 2, 2), (K.rsz, 3, 1), (K.small_add, 1), (K.small_start, 2), (K.rs3, 8, 1),
+    (K.rsz, 1, 1), (K.rsz, 4, 0), (K.rs2, 10, 0), (K.rs1, 9, 1), (K.rs1, 11, 3), (K.rs4, 5),
+    (K.rs1, 9, 3), (K.rs3, 8, 0), (K.rs1, 11, 0), (K.rs1, 9, 2), (K.memory_rows, 2),
+    (K.rs2, 11, 0), (K.rs3, 9, 0), (K.rs1, 6, 2), (K.rs1, 10, 3), (K.rs4, 7), (K.rsz, 7, 0),
+    (K.rsz, 4, 1), (K.small_add, 2), (K.rs3, 9, 1), (K.rsz, 5, 0), (K.rs2, 11, 1),
+    (K.rs1, 6, 1), (K.rs3, 6, 1), (K.rs1, 11, 1), (K.rs4, 8), (K.small_start, 3), (K.rsz, 7, 1),
+    (K.rs3, 6, 0), (K.rsz, 8, 0), (K.rs1, 11, 2), (K.rsz, 7, 2), (K.rs3, 11, 0), (K.rsz, 8, 1),
+    (K.rs1, 10, 2), (K.rs5, 1), (K.rs4, 9), (K.rsz, 9, 0), (K.rsz, 9, 1), (K.rsz, 5, 1),
+    (K.memory_rows, 3), (K.rs5, 2), (K.rs3, 11, 1), (K.small_add, 3), (K.rs5, 0),
+    (K.small_start, 4), (K.out_rows,), (K.rs4, 6), (K.rs1, 10, 1), (K.rs3, 10, 0),
+    (K.rsz, 6, 0), (K.rs3, 10, 1), (K.rsz, 4, 2), (K.rs5, 3), (K.rsz, 6, 1), (K.rs4, 11),
+    (K.rsz, 11, 0), (K.rsz, 8, 2), (K.rsz, 11, 1), (K.rs4, 10), (K.rs5, 5), (K.rsz, 9, 2),
+    (K.rsz, 10, 0), (K.rsz, 10, 1), (K.rs5, 9), (K.rs5, 4), (K.rs5, 8), (K.small_add, 4),
+    (K.rs5, 6), (K.rs5, 7), (K.rs5, 10), (K.rs5, 11),
 )
 
 NAMES = (
@@ -1072,8 +1117,8 @@
             pltpu.VMEM((16, 128), F32),
             pltpu.VMEM((6, 8, D), F32), pltpu.VMEM((6, 16, 128), F32),
             pltpu.VMEM((5, 8, D), F32), pltpu.VMEM((5, 16, 128), F32),
-            dma((120,)), dma((120,)), dma((24,)), dma((12,)), dma((180,)), dma((180,)), dma((9,)),
-            dma((10,)), dma((10,)), pltpu.SemaphoreType.REGULAR((2,)),
+            dma((120,)), dma((120,)), dma((24,)), dma((12,)), dma((180,)), dma((180,)), dma((24,)),
+            dma((10,)), dma((10,)), pltpu.SemaphoreType.REGULAR((4,)),
         ],
         compiler_params=pltpu.CompilerParams(
             collective_id=0, has_side_effects=True, vmem_limit_bytes=67000000),

time: 185 us -> 178 us (0.962)
  Pallas kernels: 183 us -> 174 us
    pallas_call x1, Pallas kernels: 180 us -> 172 us  [fused(): pl.pallas_call(kernel, out_shape=(s((length, D), BF), s((length, D), BF),...]
where the time goes in v5:
time: 178 us; the launch traced here: 177 us
  Pallas kernels  174 us (98%)
  between operations  2.11 us (1%)
    pallas_call x1, Pallas kernels, fused(): pl.pallas_call(kernel, out_shape=(s((length, D), BF), s((length, D), BF),...  172 us

profile of v5, /device:TPU:0, one launch (start us, length us, event | category | flops | bytes accessed | tf_op | source)
XLA Modules:
  0.0 176.6 jit_solution(99069111449729613)
XLA Ops:
  1.9 171.7 %shard_map.161 = (bf16[128,768]{1,0:T(8,128)(2,1)}, bf16[128,768]{1,0:T(8,128)(2,1)}, bf16[512,768]{1,0:T(8,128)(2,1)}, f32[576,128]{1,0:T(8,128)}, f32[576,128]...) custom-call(bf16[128,768]{1,0:T(8,128)(2,1)} %bitcast.20, bf16[512,768]{1,0:T(8,128)(2,1)} %bitcast.14, ...), custom_call_target="tpu_custom_call" | custom-call | flops 10000000000 | bytes 8000000 | tf_op jit(solution)/shard_map/pallas_call | solution.py:1091
  173.6 2.8 %shard_map.162 = (bf16[128,768]{1,0:T(8,128)(2,1)}, bf16[128,768]{1,0:T(8,128)(2,1)}, bf16[512,768]{1,0:T(8,128)(2,1)}, f32[576,128]{1,0:T(8,128)}, f32[576,128]...) custom-call(bf16[128,768]{1,0:T(8,128)(2,1)} %get-tuple-element.24.refs_0_, ...), custom_call_target="tpu_custom_call" | custom-call | tf_op jit(solution)/shard_map/pallas_call | solution.py:1067

commit v6 on v5

--- a/solution.py
+++ b/solution.py
@@ -956,64 +956,63 @@
 
 K = Layer
 SCHEDULE = (
-    (K.own_z, 0, 0), (K.own_xy, 0), (K.own_z, 0, 1), (K.own_square, 1), (K.own_xy, 1),
-    (K.own_z, 1, 0), (K.own_z, 1, 1), (K.p1, 0, 1), (K.own_ff,), (K.own_z, 2, 0),
-    (K.own_z, 2, 1), (K.p2x, 1, 0), (K.p1, 1, 1), (K.p2y, 0, 1), (K.p2x, 0, 0), (K.p2x, 0, 1),
-    (K.p2y, 0, 0), (K.p1, 0, 3), (K.p1, 0, 2), (K.p1, 1, 2), (K.p2y, 1, 1), (K.p2x, 1, 1),
-    (K.p1, 1, 3), (K.p2x, 0, 3), (K.p2y, 1, 0), (K.p2y, 0, 3), (K.p2x, 0, 2), (K.p2y, 0, 2),
-    (K.p1, 2, 2), (K.p3, 0, 1, 0), (K.p3, 0, 0, 0), (K.p3, 1, 1, 0), (K.p3, 0, 1, 1),
-    (K.p3, 0, 0, 1), (K.p3, 1, 0, 0), (K.p2x, 1, 2), (K.p2y, 1, 2), (K.p3, 1, 1, 1),
-    (K.p1, 2, 1), (K.p1, 2, 0), (K.p3, 1, 0, 1), (K.p3, 0, 3, 0), (K.p3, 0, 2, 0),
-    (K.p2y, 1, 3), (K.p3, 0, 2, 1), (K.p3, 0, 3, 1), (K.p2x, 1, 3), (K.p4, 0, 0), (K.p4, 0, 1),
-    (K.p2y, 2, 2), (K.p3, 1, 2, 0), (K.p2x, 2, 2), (K.p1, 2, 3), (K.p4, 0, 3), (K.p3, 1, 2, 1),
-    (K.p5, 0, 0), (K.p3, 1, 3, 0), (K.p4, 1, 0), (K.p4, 1, 1), (K.p3, 1, 3, 1), (K.p5, 0, 1),
-    (K.p2x, 2, 1), (K.p4, 0, 2), (K.p5, 0, 3), (K.p3, 2, 2, 0), (K.p2y, 2, 1), (K.p2x, 2, 0),
-    (K.p5, 0, 2), (K.p3, 2, 2, 1), (K.bias,), (K.self_forward,), (K.p4, 1, 2), (K.p2y, 2, 0),
-    (K.p4, 1, 3), (K.p2x, 2, 3), (K.p2y, 2, 3), (K.p3, 2, 1, 0), (K.p5, 1, 1), (K.p4, 2, 2),
-    (K.p3, 2, 1, 1), (K.p5, 1, 2), (K.p5, 1, 3), (K.p5, 1, 0), (K.cross_kv, 1), (K.cross_kv, 2),
-    (K.p3, 2, 0, 0), (K.cross_forward, 0), (K.p3, 2, 0, 1), (K.p3, 2, 3, 0), (K.p3, 2, 3, 1),
-    (K.p5, 2, 2), (K.p4, 2, 1), (K.cross_forward, 1), (K.p4, 2, 0), (K.build_plane, 2),
-    (K.cross_forward, 2), (K.p5, 2, 1), (K.build_plane, 1), (K.p5, 2, 0), (K.build_plane, 0),
-    (K.ff_gate,), (K.ff_up,), (K.credit, 0), (K.p4, 2, 3), (K.grad_role, 0, 0),
-    (K.grad_role, 0, 1), (K.grad_role, 0, 2), (K.grad_role, 0, 3), (K.p5, 2, 3),
-    (K.build_plane, 3), (K.rs1, 0, 0), (K.d_hidden, 0), (K.rs1, 0, 1), (K.d_hidden, 1),
-    (K.credit, 1), (K.rs1, 0, 2), (K.grad, 1), (K.grad, 2), (K.rs2, 0, 0), (K.rs1, 1, 0),
-    (K.rs2, 0, 1), (K.rs1, 1, 1), (K.rs1, 1, 2), (K.grad, 3), (K.rs1, 2, 0),
-    (K.norm_three_back,), (K.rs1, 2, 3), (K.rs3, 0, 1), (K.rs1, 3, 1), (K.rs3, 0, 0),
-    (K.rs1, 3, 2), (K.cross_back, 0), (K.rs2, 1, 1), (K.grad_role, 4, 0), (K.grad_role, 4, 1),
-    (K.cross_back, 1), (K.grad_role, 4, 2), (K.rs2, 2, 0), (K.rs1, 3, 0), (K.rs2, 1, 0),
-    (K.cross_back, 2), (K.rs2, 2, 1), (K.rs1, 2, 1), (K.rs1, 0, 3), (K.grad_role, 4, 3),
-    (K.rs1, 4, 0), (K.rs4, 0), (K.rs1, 2, 2), (K.grad, 5), (K.rsz, 0, 0), (K.rs3, 2, 0),
-    (K.grad, 6), (K.rs3, 2, 1), (K.rs1, 5, 0), (K.rs3, 1, 1), (K.rs2, 3, 0), (K.grad, 7),
-    (K.rs1, 6, 0), (K.rs2, 3, 1), (K.rs2, 4, 0), (K.rs3, 1, 0), (K.rs1, 5, 1),
-    (K.norm_two_back,), (K.rs1, 7, 0), (K.rsz, 0, 1), (K.rs1, 4, 2), (K.rs4, 2), (K.rsz, 2, 0),
-    (K.grad, 8), (K.self_back, 0), (K.rs3, 3, 0), (K.rs3, 3, 1), (K.rs2, 5, 0),
-    (K.self_back, 1), (K.grad_role, 9, 0), (K.rs2, 4, 1), (K.rs1, 6, 3), (K.rs2, 7, 0),
-    (K.rs3, 4, 0), (K.zfree,), (K.rs1, 8, 0), (K.rs1, 7, 1), (K.rs1, 1, 3), (K.rs1, 3, 3),
-    (K.rs2, 5, 1), (K.rs1, 4, 3), (K.rs1, 9, 0), (K.rs1, 7, 2), (K.rs1, 5, 2), (K.rs1, 4, 1),
-    (K.rs4, 3), (K.rsz, 3, 0), (K.rs1, 8, 3), (K.rs4, 1), (K.rs1, 8, 1), (K.rs2, 7, 1),
-    (K.rsz, 0, 2), (K.rsz, 2, 1), (K.rs1, 8, 2), (K.rsz, 1, 0), (K.table_back,),
-    (K.memory_rows, 1), (K.rs3, 5, 0), (K.rs3, 5, 1), (K.norm_one_back,), (K.rs3, 4, 1),
-    (K.rs2, 6, 1), (K.rs2, 8, 0), (K.small_start, 0), (K.memory_rows, 0), (K.rs2, 9, 0),
-    (K.small_add, 0), (K.rs2, 8, 1), (K.rs2, 6, 0), (K.rs3, 7, 0), (K.grad_role, 9, 1),
-    (K.grad_role, 9, 2), (K.grad_role, 9, 3), (K.grad_role, 10, 0), (K.grad_role, 10, 1),
-    (K.grad_role, 10, 2), (K.grad_role, 10, 3), (K.grad_role, 11, 0), (K.small_start, 1),
-    (K.rs4, 4), (K.grad_role, 11, 1), (K.rs3, 7, 1), (K.grad_role, 11, 2), (K.rs1, 7, 3),
-    (K.rs2, 9, 1), (K.rs1, 10, 0), (K.rs2, 10, 1), (K.rs1, 5, 3), (K.grad_role, 11, 3),
-    (K.rsz, 2, 2), (K.rsz, 3, 1), (K.small_add, 1), (K.small_start, 2), (K.rs3, 8, 1),
-    (K.rsz, 1, 1), (K.rsz, 4, 0), (K.rs2, 10, 0), (K.rs1, 9, 1), (K.rs1, 11, 3), (K.rs4, 5),
-    (K.rs1, 9, 3), (K.rs3, 8, 0), (K.rs1, 11, 0), (K.rs1, 9, 2), (K.memory_rows, 2),
-    (K.rs2, 11, 0), (K.rs3, 9, 0), (K.rs1, 6, 2), (K.rs1, 10, 3), (K.rs4, 7), (K.rsz, 7, 0),
-    (K.rsz, 4, 1), (K.small_add, 2), (K.rs3, 9, 1), (K.rsz, 5, 0), (K.rs2, 11, 1),
-    (K.rs1, 6, 1), (K.rs3, 6, 1), (K.rs1, 11, 1), (K.rs4, 8), (K.small_start, 3), (K.rsz, 7, 1),
-    (K.rs3, 6, 0), (K.rsz, 8, 0), (K.rs1, 11, 2), (K.rsz, 7, 2), (K.rs3, 11, 0), (K.rsz, 8, 1),
-    (K.rs1, 10, 2), (K.rs5, 1), (K.rs4, 9), (K.rsz, 9, 0), (K.rsz, 9, 1), (K.rsz, 5, 1),
-    (K.memory_rows, 3), (K.rs5, 2), (K.rs3, 11, 1), (K.small_add, 3), (K.rs5, 0),
-    (K.small_start, 4), (K.out_rows,), (K.rs4, 6), (K.rs1, 10, 1), (K.rs3, 10, 0),
-    (K.rsz, 6, 0), (K.rs3, 10, 1), (K.rsz, 4, 2), (K.rs5, 3), (K.rsz, 6, 1), (K.rs4, 11),
-    (K.rsz, 11, 0), (K.rsz, 8, 2), (K.rsz, 11, 1), (K.rs4, 10), (K.rs5, 5), (K.rsz, 9, 2),
-    (K.rsz, 10, 0), (K.rsz, 10, 1), (K.rs5, 9), (K.rs5, 4), (K.rs5, 8), (K.small_add, 4),
-    (K.rs5, 6), (K.rs5, 7), (K.rs5, 10), (K.rs5, 11),
+    (K.own_z, 0, 1), (K.own_xy, 0), (K.own_z, 0, 0), (K.own_square, 1), (K.own_ff,),
+    (K.own_xy, 1), (K.bias,), (K.own_z, 1, 1), (K.own_z, 1, 0), (K.p1, 0, 1), (K.p1, 0, 2),
+    (K.p1, 1, 2), (K.p1, 1, 1), (K.p1, 0, 3), (K.own_z, 2, 1), (K.p2x, 1, 0), (K.own_z, 2, 0),
+    (K.p2x, 0, 1), (K.p2y, 0, 2), (K.p2x, 1, 2), (K.p2y, 1, 2), (K.p2x, 1, 1), (K.p2y, 1, 1),
+    (K.p2y, 1, 0), (K.p1, 1, 3), (K.p2x, 0, 2), (K.p2x, 0, 3), (K.p2y, 0, 1), (K.p2x, 0, 0),
+    (K.p2y, 0, 0), (K.p1, 2, 1), (K.p3, 1, 1, 0), (K.p2y, 0, 3), (K.p3, 1, 2, 0),
+    (K.p3, 1, 2, 1), (K.p1, 2, 2), (K.p1, 2, 0), (K.p4, 1, 2), (K.p3, 1, 0, 0), (K.p3, 0, 2, 0),
+    (K.p3, 0, 3, 0), (K.p3, 1, 0, 1), (K.p3, 0, 1, 0), (K.p2x, 1, 3), (K.p3, 0, 0, 0),
+    (K.p3, 0, 0, 1), (K.p3, 0, 1, 1), (K.p3, 0, 2, 1), (K.p2y, 1, 3), (K.p3, 1, 1, 1),
+    (K.p3, 0, 3, 1), (K.p2x, 2, 1), (K.p2y, 2, 1), (K.p1, 2, 3), (K.p2x, 2, 0), (K.p4, 0, 0),
+    (K.p3, 1, 3, 0), (K.p4, 1, 0), (K.p4, 0, 2), (K.p3, 1, 3, 1), (K.p4, 1, 1), (K.p2x, 2, 2),
+    (K.p4, 0, 1), (K.p5, 0, 2), (K.p4, 0, 3), (K.p2y, 2, 0), (K.p3, 2, 1, 0), (K.p2y, 2, 2),
+    (K.p5, 0, 0), (K.p5, 0, 3), (K.p3, 2, 1, 1), (K.p5, 0, 1), (K.p4, 1, 3), (K.p5, 1, 2),
+    (K.self_forward,), (K.p5, 1, 1), (K.p5, 1, 0), (K.p5, 1, 3), (K.p2x, 2, 3), (K.cross_kv, 1),
+    (K.p3, 2, 0, 0), (K.p2y, 2, 3), (K.cross_kv, 2), (K.p3, 2, 0, 1), (K.cross_forward, 0),
+    (K.p3, 2, 2, 0), (K.p3, 2, 2, 1), (K.p4, 2, 1), (K.p3, 2, 3, 0), (K.cross_forward, 1),
+    (K.p4, 2, 0), (K.p5, 2, 1), (K.build_plane, 1), (K.p3, 2, 3, 1), (K.cross_forward, 2),
+    (K.p5, 2, 0), (K.build_plane, 0), (K.credit, 0), (K.p4, 2, 2), (K.ff_gate,), (K.p5, 2, 2),
+    (K.build_plane, 2), (K.ff_up,), (K.p4, 2, 3), (K.grad_role, 0, 0), (K.grad_role, 0, 1),
+    (K.grad_role, 0, 2), (K.grad_role, 0, 3), (K.p5, 2, 3), (K.build_plane, 3), (K.d_hidden, 0),
+    (K.rs1, 0, 2), (K.credit, 1), (K.rs1, 0, 1), (K.rs1, 0, 0), (K.d_hidden, 1), (K.grad, 1),
+    (K.grad, 2), (K.rs2, 0, 0), (K.rs1, 1, 1), (K.rs1, 1, 2), (K.rs1, 1, 0), (K.grad, 3),
+    (K.rs1, 2, 2), (K.rs1, 2, 1), (K.rs1, 2, 0), (K.norm_three_back,), (K.rs2, 1, 0),
+    (K.grad_role, 4, 0), (K.grad_role, 4, 1), (K.rs2, 0, 1), (K.grad_role, 4, 2),
+    (K.cross_back, 0), (K.rs1, 3, 0), (K.rs2, 2, 0), (K.rs2, 1, 1), (K.cross_back, 1),
+    (K.rs1, 4, 0), (K.rs1, 3, 2), (K.rs1, 3, 1), (K.grad_role, 4, 3), (K.cross_back, 2),
+    (K.rs3, 1, 0), (K.grad, 5), (K.rs3, 1, 1), (K.rs2, 2, 1), (K.grad, 6), (K.rs1, 5, 0),
+    (K.rs2, 3, 1), (K.rs3, 0, 1), (K.rs1, 4, 2), (K.rs1, 1, 3), (K.rs2, 4, 0), (K.rs2, 3, 0),
+    (K.rs1, 6, 0), (K.grad, 7), (K.rs1, 2, 3), (K.rs3, 0, 0), (K.rs4, 1), (K.rsz, 1, 0),
+    (K.rs3, 2, 1), (K.rs3, 2, 0), (K.norm_two_back,), (K.rs1, 4, 1), (K.rs1, 0, 3), (K.grad, 8),
+    (K.rs2, 6, 0), (K.rs3, 3, 1), (K.rs1, 7, 0), (K.rs1, 5, 1), (K.rs2, 5, 1), (K.rs3, 3, 0),
+    (K.rs2, 6, 1), (K.self_back, 0), (K.self_back, 1), (K.rs1, 8, 0), (K.rs1, 6, 2), (K.rs4, 0),
+    (K.rs4, 2), (K.grad_role, 9, 0), (K.rsz, 1, 1), (K.rs1, 6, 1), (K.rs3, 4, 0), (K.rsz, 0, 0),
+    (K.rs3, 6, 1), (K.rs1, 4, 3), (K.zfree,), (K.rsz, 2, 0), (K.grad_role, 9, 1), (K.rs1, 7, 2),
+    (K.grad_role, 9, 2), (K.rs2, 7, 1), (K.rs1, 9, 0), (K.grad_role, 9, 3), (K.rs2, 5, 0),
+    (K.rs2, 7, 0), (K.rs3, 5, 1), (K.rs1, 7, 3), (K.rs1, 3, 3), (K.rs4, 3), (K.rsz, 3, 0),
+    (K.grad_role, 10, 0), (K.grad_role, 10, 1), (K.rs1, 6, 3), (K.rs1, 5, 2), (K.rs2, 8, 0),
+    (K.rs1, 7, 1), (K.grad_role, 10, 2), (K.grad_role, 10, 3), (K.grad_role, 11, 0),
+    (K.grad_role, 11, 1), (K.grad_role, 11, 2), (K.rs3, 6, 0), (K.rsz, 0, 1), (K.rs1, 8, 3),
+    (K.norm_one_back,), (K.rs1, 9, 3), (K.rs2, 8, 1), (K.rs3, 5, 0), (K.rs3, 7, 1),
+    (K.memory_rows, 2), (K.rs2, 4, 1), (K.rs3, 7, 0), (K.rsz, 2, 1), (K.rs1, 10, 0),
+    (K.rs1, 11, 0), (K.rs2, 9, 1), (K.table_back,), (K.rs1, 10, 3), (K.rs1, 9, 2),
+    (K.rs2, 11, 0), (K.grad_role, 11, 3), (K.small_start, 0), (K.rs2, 9, 0), (K.rs1, 8, 1),
+    (K.rs1, 8, 2), (K.memory_rows, 1), (K.rs4, 6), (K.rs1, 5, 3), (K.rs3, 8, 1), (K.rsz, 6, 0),
+    (K.rs3, 4, 1), (K.rs2, 10, 1), (K.rs1, 9, 1), (K.rs4, 7), (K.rs4, 5), (K.rs5, 1),
+    (K.rsz, 7, 0), (K.rs2, 11, 1), (K.rsz, 3, 1), (K.rsz, 0, 2), (K.rs2, 10, 0), (K.rs3, 9, 0),
+    (K.small_add, 0), (K.small_start, 1), (K.rsz, 5, 0), (K.rsz, 2, 2), (K.memory_rows, 0),
+    (K.rsz, 7, 1), (K.rs3, 9, 1), (K.rs3, 8, 0), (K.rs1, 10, 2), (K.memory_rows, 3),
+    (K.rs3, 10, 0), (K.rsz, 5, 1), (K.rs1, 10, 1), (K.out_rows,), (K.rsz, 6, 1), (K.rs1, 11, 2),
+    (K.rs3, 11, 0), (K.rs3, 10, 1), (K.rs4, 4), (K.rs1, 11, 1), (K.rsz, 4, 0), (K.rsz, 4, 1),
+    (K.rs4, 8), (K.rsz, 8, 0), (K.rs5, 3), (K.rs4, 9), (K.rsz, 9, 0), (K.rsz, 9, 1),
+    (K.rs3, 11, 1), (K.small_add, 1), (K.small_start, 2), (K.rsz, 7, 2), (K.rsz, 8, 1),
+    (K.rs4, 10), (K.rs5, 6), (K.rsz, 4, 2), (K.rs1, 11, 3), (K.rsz, 10, 0), (K.rs4, 11),
+    (K.rsz, 10, 1), (K.rsz, 11, 0), (K.small_add, 2), (K.small_start, 3), (K.rs5, 5),
+    (K.rs5, 0), (K.rs5, 2), (K.rs5, 4), (K.rs5, 7), (K.rsz, 11, 1), (K.rsz, 9, 2),
+    (K.rsz, 8, 2), (K.small_add, 3), (K.small_start, 4), (K.rs5, 10), (K.rs5, 11), (K.rs5, 9),
+    (K.small_add, 4), (K.rs5, 8),
 )
 
 NAMES = (

time: 178 us -> 180 us (1.011)
  Pallas kernels: 174 us -> 177 us
    pallas_call x1, Pallas kernels: 172 us -> 175 us  [fused(): pl.pallas_call(kernel, out_shape=(s((length, D), BF), s((length, D), BF),...]
where the time goes in v6:
time: 180 us; the launch traced here: 179 us
  Pallas kernels  177 us (98%)
  between operations  2.11 us (1%)
    pallas_call x1, Pallas kernels, fused(): pl.pallas_call(kernel, out_shape=(s((length, D), BF), s((length, D), BF),...  175 us

profile of v6, /device:TPU:0, one launch (start us, length us, event | category | flops | bytes accessed | tf_op | source)
XLA Modules:
  0.0 179.5 jit_solution(4024790577316637907)
XLA Ops:
  1.9 174.6 %shard_map.161 = (bf16[128,768]{1,0:T(8,128)(2,1)}, bf16[128,768]{1,0:T(8,128)(2,1)}, bf16[512,768]{1,0:T(8,128)(2,1)}, f32[576,128]{1,0:T(8,128)}, f32[576,128]...) custom-call(bf16[128,768]{1,0:T(8,128)(2,1)} %bitcast.20, bf16[512,768]{1,0:T(8,128)(2,1)} %bitcast.14, ...), custom_call_target="tpu_custom_call" | custom-call | flops 10000000000 | bytes 8000000 | tf_op jit(solution)/shard_map/pallas_call | solution.py:1090
  176.6 2.8 %shard_map.162 = (bf16[128,768]{1,0:T(8,128)(2,1)}, bf16[128,768]{1,0:T(8,128)(2,1)}, bf16[512,768]{1,0:T(8,128)(2,1)}, f32[576,128]{1,0:T(8,128)}, f32[576,128]...) custom-call(bf16[128,768]{1,0:T(8,128)(2,1)} %get-tuple-element.24.refs_0_, ...), custom_call_target="tpu_custom_call" | custom-call | tf_op jit(solution)/shard_map/pallas_call | solution.py:1066
